TPU v7x, 32 devices: a whole 2x2x4 slice. The times are simulated.
32 devices in a mesh: fsdp: 8 (over y, x, core), dp: 4 (over z).
Axes of the slice: x: 2, y: 2, z: 4, core: 2. Of those that a mesh axis runs over, the one named last changes fastest.
Arguments:
- inputs: bfloat16 [8, 1024, 2048], P(None, 'fsdp'), may hold values from -6 to 6
- cotangent: bfloat16 [8, 1024, 2048], P(None, 'fsdp'), may hold values from -6 to 6
- piece_start: int32 [8, 2], replicated, may hold values from 0 to 768, as said below
- piece_image: int32 [8, 2], replicated, may hold values from 0 to 1
- valid_mask: int32 [8, 1024], replicated, may hold values from 0 to 1, as said below
- query_weight: bfloat16 [2048, 2048], P('fsdp', 'dp'), may hold values from -0.125 to 0.125
- key_weight: bfloat16 [2048, 2048], P('fsdp', 'dp'), may hold values from -0.125 to 0.125
- value_weight: bfloat16 [2048, 2048], P('fsdp', 'dp'), may hold values from -0.125 to 0.125
- output_weight: bfloat16 [2048, 2048], P('dp', 'fsdp'), may hold values from -1.5 to 1.5
- attn_gain: bfloat16 [2048], P('fsdp'), may hold values from 0.5 to 1.5
- gate_weight: bfloat16 [2048, 8192], P('fsdp', 'dp'), may hold values from -0.125 to 0.125
- up_weight: bfloat16 [2048, 8192], P('fsdp', 'dp'), may hold values from -0.125 to 0.125
- down_weight: bfloat16 [8192, 2048], P('dp', 'fsdp'), may hold values from -0.0625 to 0.0625
- mlp_gain: bfloat16 [2048], P('fsdp'), may hold values from 0.5 to 1.5
Outputs:
- output: bfloat16 [8, 1024, 2048], P(None, 'fsdp')
- input_grad: bfloat16 [8, 1024, 2048], P(None, 'fsdp')
- query_grad: float32 [2048, 2048], P('fsdp', 'dp')
- key_grad: float32 [2048, 2048], P('fsdp', 'dp')
- value_grad: float32 [2048, 2048], P('fsdp', 'dp')
- output_weight_grad: float32 [2048, 2048], P('dp', 'fsdp')
- attn_gain_grad: float32 [2048], P('fsdp')
- gate_grad: float32 [2048, 8192], P('fsdp', 'dp')
- up_grad: float32 [2048, 8192], P('fsdp', 'dp')
- down_grad: float32 [8192, 2048], P('dp', 'fsdp')
- mlp_gain_grad: float32 [2048], P('fsdp')
- rms_residual: float32 [], replicated
- rms_attention: float32 [], replicated
- rms_mlp: float32 [], replicated
Inputs may be any that keep to these rules, and one draw needn't show every extreme that they name: `piece_start`: the starts of a sequence are distinct multiples of 256, so its 2 pieces do not intersect. `piece_image`: pieces of one sequence with the same number belong to one image. `valid_mask`: in each sequence the valid slots form a prefix of 512 tokens or more.
All inputs are finite; a program needn't handle non-finite values.
Results may differ from a plain program's by a relative error of at most 0.024.
Values may be sent and summed in bfloat16 or wider, within the bound.
A program may use at most 384 MiB of HBM per device.

v0:
```python
import jax
import jax.numpy as jnp
from jax import lax
from jax.sharding import PartitionSpec as P

HD = 64
PIECE = 256


EPS = 1e-05
THETA = 130000.0
NEG = -1e30


def rope_tables(positions, head_size):
    half = head_size // 2
    rates = THETA ** (-(jnp.arange(half, dtype=jnp.float32) * 2.0 / head_size))
    angle = positions.astype(jnp.float32)[:, None] * rates[None, :]
    cosine = jnp.concatenate([jnp.cos(angle), jnp.cos(angle)], axis=-1)
    sine = jnp.concatenate([jnp.sin(angle), jnp.sin(angle)], axis=-1)
    return (cosine, sine)


def rotate(values, cosine, sine):
    half = values.shape[-1] // 2
    turned = jnp.concatenate([-values[..., half:], values[..., :half]], axis=-1)
    return values * cosine[:, None, :] + turned * sine[:, None, :]


def unrotate(grads, cosine, sine):
    half = grads.shape[-1] // 2
    scaled = grads * sine[:, None, :]
    turned = jnp.concatenate([scaled[..., half:], -scaled[..., :half]], axis=-1)
    return grads * cosine[:, None, :] + turned


def image_of(positions, starts, images):
    inside = (positions[:, None] >= starts[None, :]) & (
        positions[:, None] < starts[None, :] + PIECE
    )
    return jnp.sum(jnp.where(inside, images[None, :] + 1, 0), axis=1) - 1


def allowed_mask(query_pos, key_pos, query_image, key_image, key_valid):
    causal = key_pos[None, :] <= query_pos[:, None]
    same = (query_image[:, None] >= 0) & (query_image[:, None] == key_image[None, :])
    return (causal | same) & (key_valid[None, :] > 0)


def project(values, weight):
    return jnp.einsum("std,de->ste", values, weight, preferred_element_type=jnp.float32)


def project_back(grads, weight):
    return jnp.einsum("ste,de->std", grads, weight, preferred_element_type=jnp.float32)


def weight_term(values, grads):
    return jnp.einsum("std,ste->de", values, grads, preferred_element_type=jnp.float32)


def masked_scores(queries, key_heads, allowed):
    raw = jnp.einsum(
        "qhd,khd->hqk", queries, key_heads, preferred_element_type=jnp.float32
    ) * HD ** (-0.5)
    return jnp.where(allowed[None, :, :], raw, NEG)


def norm_back(grad, source, scale, gain):
    scaled = grad * gain.astype(jnp.float32)
    inner = jnp.mean(scaled * source, axis=2, keepdims=True)
    return scale * (scaled - source * scale * scale * inner)


def blocked(step, items):
    total = items[0].shape[0]
    block_size = max((candidate for candidate in range(1, 9) if total % candidate == 0))
    groups = total // block_size
    shaped = tuple((item.reshape((groups, block_size) + item.shape[1:]) for item in items))
    results = lax.map(lambda group: jax.vmap(step)(*group), shaped)
    return jax.tree.map(
        lambda result: result.reshape((groups * block_size,) + result.shape[2:]), results
    )


def per_device(
    inputs,
    cotangent,
    piece_start,
    piece_image,
    valid_mask,
    query_weight,
    key_weight,
    value_weight,
    output_weight,
    attn_gain,
    gate_weight,
    up_weight,
    down_weight,
    mlp_gain,
):
    seqs, local, width = inputs.shape
    length = valid_mask.shape[1]
    band = query_weight.shape[1]
    heads_here = band // HD
    offset = lax.axis_index("fsdp") * local
    positions = offset + jnp.arange(local, dtype=jnp.int32)
    key_places = jnp.arange(length, dtype=jnp.int32)
    cosine, sine = rope_tables(positions, HD)
    local_valid = lax.dynamic_slice_in_dim(valid_mask, offset, local, 1).astype(jnp.float32)

    def sequence_mask(starts, images, valid_row):
        query_image = image_of(positions, starts, images)
        key_image = image_of(key_places, starts, images)
        return allowed_mask(positions, key_places, query_image, key_image, valid_row)

    attn_set = (
        lax.all_gather(query_weight, "fsdp", axis=0, tiled=True),
        lax.all_gather(key_weight, "fsdp", axis=0, tiled=True),
        lax.all_gather(value_weight, "fsdp", axis=0, tiled=True),
        lax.all_gather(output_weight, "fsdp", axis=1, tiled=True),
        lax.all_gather(attn_gain, "fsdp", axis=0, tiled=True),
    )
    residual = inputs.astype(jnp.float32)
    scale_one = lax.rsqrt(jnp.mean(residual * residual, axis=2, keepdims=True) + EPS)
    normed_one = (residual * scale_one * attn_set[4].astype(jnp.float32)).astype(jnp.bfloat16)
    queries = rotate(
        project(normed_one, attn_set[0]).reshape(seqs, local, heads_here, HD), cosine, sine
    ).astype(jnp.bfloat16)
    keys_here = (
        rotate(project(normed_one, attn_set[1]).reshape(seqs, local, heads_here, HD), cosine, sine)
        .astype(jnp.bfloat16)
        .reshape(seqs, local, band)
    )
    values_here = project(normed_one, attn_set[2]).astype(jnp.bfloat16)
    keys_all, values_all = (
        lax.all_gather(keys_here, "fsdp", axis=1, tiled=True),
        lax.all_gather(values_here, "fsdp", axis=1, tiled=True),
    )

    def attend(query_one, key_one, value_one, starts, images, valid_row):
        allowed = sequence_mask(starts, images, valid_row)
        scores = masked_scores(query_one, key_one.reshape(length, heads_here, HD), allowed)
        highest = jnp.max(scores, axis=2, keepdims=True)
        log_total = highest + jnp.log(jnp.sum(jnp.exp(scores - highest), axis=2, keepdims=True))
        probs = jnp.exp(scores - log_total).astype(jnp.bfloat16)
        mixed_one = jnp.einsum(
            "hqk,khd->qhd",
            probs,
            value_one.reshape(length, heads_here, HD),
            preferred_element_type=jnp.float32,
        )
        return (mixed_one.reshape(local, band).astype(jnp.bfloat16), log_total)

    mixed, log_totals = blocked(
        attend, (queries, keys_all, values_all, piece_start, piece_image, valid_mask)
    )
    attn_out = lax.psum(project(mixed, attn_set[3]).astype(jnp.bfloat16), "dp").astype(jnp.float32)
    middle = residual + attn_out
    scale_two = lax.rsqrt(jnp.mean(middle * middle, axis=2, keepdims=True) + EPS)
    mlp_set = (
        lax.all_gather(gate_weight, "fsdp", axis=0, tiled=True),
        lax.all_gather(up_weight, "fsdp", axis=0, tiled=True),
        lax.all_gather(down_weight, "fsdp", axis=1, tiled=True),
        lax.all_gather(mlp_gain, "fsdp", axis=0, tiled=True),
    )
    normed_two = (middle * scale_two * mlp_set[3].astype(jnp.float32)).astype(jnp.bfloat16)
    gate = project(normed_two, mlp_set[0])
    up = project(normed_two, mlp_set[1])
    sigmoid_gate = jax.nn.sigmoid(gate)
    activated = (gate * sigmoid_gate * up).astype(jnp.bfloat16)
    mlp_out = lax.psum(project(activated, mlp_set[2]).astype(jnp.bfloat16), "dp").astype(
        jnp.float32
    )
    output = (middle + mlp_out).astype(jnp.bfloat16)
    row_weight = local_valid[:, :, None]
    totals = lax.psum(
        (
            jnp.sum(middle * middle * row_weight),
            jnp.sum(attn_out * attn_out * row_weight),
            jnp.sum(mlp_out * mlp_out * row_weight),
        ),
        "fsdp",
    )
    count = jnp.sum(valid_mask).astype(jnp.float32) * width
    mlp_back = (
        lax.all_gather(gate_weight, "fsdp", axis=0, tiled=True),
        lax.all_gather(up_weight, "fsdp", axis=0, tiled=True),
        lax.all_gather(down_weight, "fsdp", axis=1, tiled=True),
        lax.all_gather(mlp_gain, "fsdp", axis=0, tiled=True),
    )
    upstream = cotangent.astype(jnp.float32)
    act_grad = project_back(cotangent, mlp_back[2])
    gate_back = (
        act_grad * up * (sigmoid_gate + gate * sigmoid_gate * (1.0 - sigmoid_gate))
    ).astype(jnp.bfloat16)
    up_back = (act_grad * gate * sigmoid_gate).astype(jnp.bfloat16)
    normed_two_back = lax.psum(
        (project_back(gate_back, mlp_back[0]) + project_back(up_back, mlp_back[1])).astype(
            jnp.bfloat16
        ),
        "dp",
    ).astype(jnp.float32)
    middle_back = upstream + norm_back(normed_two_back, middle, scale_two, mlp_back[3])
    mlp_gain_term = jnp.sum(normed_two_back * middle * scale_two, axis=(0, 1))
    mlp_parts = lax.psum_scatter(
        jnp.concatenate(
            [
                weight_term(normed_two, gate_back),
                weight_term(normed_two, up_back),
                weight_term(cotangent, activated),
            ],
            axis=1,
        ).astype(jnp.bfloat16),
        "fsdp",
        scatter_dimension=0,
        tiled=True,
    ).astype(jnp.float32)
    feed = gate_weight.shape[1]
    gate_part = mlp_parts[:, :feed]
    up_part = mlp_parts[:, feed : 2 * feed]
    down_part = mlp_parts[:, 2 * feed :].T
    attn_back = (
        lax.all_gather(query_weight, "fsdp", axis=0, tiled=True),
        lax.all_gather(key_weight, "fsdp", axis=0, tiled=True),
        lax.all_gather(value_weight, "fsdp", axis=0, tiled=True),
        lax.all_gather(output_weight, "fsdp", axis=1, tiled=True),
        lax.all_gather(attn_gain, "fsdp", axis=0, tiled=True),
    )
    middle_low = middle_back.astype(jnp.bfloat16)
    mixed_back = project_back(middle_low, attn_back[3]).astype(jnp.bfloat16)

    def query_grads(query_one, key_heads, value_heads, grad_heads, log_total, allowed):
        scores = masked_scores(query_one, key_heads, allowed)
        weights = jnp.exp(scores - log_total)
        prob_back = jnp.einsum(
            "qhd,khd->hqk", grad_heads, value_heads, preferred_element_type=jnp.float32
        )
        inner = jnp.sum(weights * prob_back, axis=2, keepdims=True)
        score_back = (weights * (prob_back - inner)).astype(jnp.bfloat16)
        query_back = jnp.einsum(
            "hqk,khd->qhd", score_back, key_heads, preferred_element_type=jnp.float32
        ) * HD ** (-0.5)
        return (query_back, weights, score_back, inner)

    def attend_back(query_one, key_one, value_one, grad_one, log_total, starts, images, valid_row):
        allowed = sequence_mask(starts, images, valid_row)
        grad_heads = grad_one.reshape(local, heads_here, HD)
        query_back, weights, score_back, inner = query_grads(
            query_one,
            key_one.reshape(length, heads_here, HD),
            value_one.reshape(length, heads_here, HD),
            grad_heads,
            log_total,
            allowed,
        )
        key_back = jnp.einsum(
            "hqk,qhd->khd", score_back, query_one, preferred_element_type=jnp.float32
        ) * HD ** (-0.5)
        value_back = jnp.einsum(
            "hqk,qhd->khd",
            weights.astype(jnp.bfloat16),
            grad_heads,
            preferred_element_type=jnp.float32,
        )
        return (query_back, key_back.reshape(length, band), value_back.reshape(length, band))

    query_backs, key_parts, value_parts = blocked(
        attend_back,
        (
            queries,
            keys_all,
            values_all,
            mixed_back,
            log_totals,
            piece_start,
            piece_image,
            valid_mask,
        ),
    )
    key_backs, value_backs = (
        lax.psum_scatter(
            key_parts.astype(jnp.bfloat16), "fsdp", scatter_dimension=1, tiled=True
        ).astype(jnp.float32),
        lax.psum_scatter(
            value_parts.astype(jnp.bfloat16), "fsdp", scatter_dimension=1, tiled=True
        ).astype(jnp.float32),
    )
    query_low = unrotate(query_backs, cosine, sine).reshape(seqs, local, band).astype(jnp.bfloat16)
    key_low = (
        unrotate(key_backs.reshape(seqs, local, heads_here, HD), cosine, sine)
        .reshape(seqs, local, band)
        .astype(jnp.bfloat16)
    )
    value_low = value_backs.astype(jnp.bfloat16)
    partial_back = (
        project_back(query_low, attn_back[0])
        + project_back(key_low, attn_back[1])
        + project_back(value_low, attn_back[2])
    )
    normed_one_back = lax.psum(partial_back.astype(jnp.bfloat16), "dp").astype(jnp.float32)
    input_grad = (
        middle_back + norm_back(normed_one_back, residual, scale_one, attn_back[4])
    ).astype(jnp.bfloat16)
    query_part, key_part, value_part, output_term, attn_gain_part, mlp_gain_part = (
        lax.psum_scatter(
            weight_term(normed_one, query_low).astype(jnp.bfloat16),
            "fsdp",
            scatter_dimension=0,
            tiled=True,
        ).astype(jnp.float32),
        lax.psum_scatter(
            weight_term(normed_one, key_low).astype(jnp.bfloat16),
            "fsdp",
            scatter_dimension=0,
            tiled=True,
        ).astype(jnp.float32),
        lax.psum_scatter(
            weight_term(normed_one, value_low).astype(jnp.bfloat16),
            "fsdp",
            scatter_dimension=0,
            tiled=True,
        ).astype(jnp.float32),
        lax.psum_scatter(
            weight_term(middle_low, mixed).astype(jnp.bfloat16),
            "fsdp",
            scatter_dimension=0,
            tiled=True,
        ).astype(jnp.float32),
        lax.psum_scatter(
            jnp.sum(normed_one_back * residual * scale_one, axis=(0, 1)).astype(jnp.bfloat16),
            "fsdp",
            scatter_dimension=0,
            tiled=True,
        ).astype(jnp.float32),
        lax.psum_scatter(
            mlp_gain_term.astype(jnp.bfloat16), "fsdp", scatter_dimension=0, tiled=True
        ).astype(jnp.float32),
    )
    output_part = output_term.T
    return (
        output,
        input_grad,
        query_part,
        key_part,
        value_part,
        output_part,
        attn_gain_part,
        gate_part,
        up_part,
        down_part,
        mlp_gain_part,
        jnp.sqrt(totals[0] / count),
        jnp.sqrt(totals[1] / count),
        jnp.sqrt(totals[2] / count),
    )


def solution(mesh):
    placed = (
        P(None, "fsdp", None),
        P(None, "fsdp", None),
        P(),
        P(),
        P(),
        P("fsdp", "dp"),
        P("fsdp", "dp"),
        P("fsdp", "dp"),
        P("dp", "fsdp"),
        P("fsdp"),
        P("fsdp", "dp"),
        P("fsdp", "dp"),
        P("dp", "fsdp"),
        P("fsdp"),
    )
    return jax.shard_map(
        per_device,
        mesh=mesh,
        in_specs=placed,
        out_specs=(
            P(None, "fsdp", None),
            P(None, "fsdp", None),
            P("fsdp", "dp"),
            P("fsdp", "dp"),
            P("fsdp", "dp"),
            P("dp", "fsdp"),
            P("fsdp"),
            P("fsdp", "dp"),
            P("fsdp", "dp"),
            P("dp", "fsdp"),
            P("fsdp"),
            P(),
            P(),
            P(),
        ),
        check_vma=False,
    )
```

profile of v0, /device:TPU:0, one launch (start us, length us, event | category | flops | bytes accessed | tf_op | source)
XLA Modules:
  0.0 1631.9 jit_solution(17268431177148580186)
XLA Ops:
  25.5 14.9 all-gather.18.cloned.1.call-done
  55.0 15.1 all-gather.12.cloned.1.call-done
  78.9 20.9 %all-gather.16.cloned.1.call-done = bf16[2048,512]{1,0:T(8,128)(2,1)} async-done(((bf16[256,512]{1,0:T(8,128)(2,1)}), bf16[2048,512]{1,0:T(8,128)(2,1)}) %all-gather.16.cloned.1.call-update) | async-done | bytes 2097168 | tf_op jit(solution)/shard_map/all_gather | solution.py:118
  105.6 50.9 %all-gather.20.cloned.1.call-done = bf16[8,1024,512]{2,1,0:T(8,128)(2,1)} async-done(((bf16[8,128,512]{2,1,0:T(8,128)(2,1)}), bf16[8,1024,512]{2,1,0:T(8,128)(2,1)}) %all-gather.20.cloned.1.call-update) | async-done | bytes 8388624 | tf_op jit(solution)/shard_map/all_gather | solution.py:137
  168.0 16.0 fusion
  184.1 15.7 exponential_reduce_fusion
  199.8 13.3 all-gather.14.cloned.1.call-done
  224.6 16.3 convolution_convert_fusion.2
  260.0 144.1 %all-reduce.9.cloned.1.call-done = bf16[8,128,2048]{2,1,0:T(8,128)(2,1)} async-done(((bf16[8,128,2048]{2,1,0:T(8,128)(2,1)}), bf16[8,128,2048]{2,1,0:T(8,128)(2,1)}) %all-reduce.9.cloned.1.call-update) | async-done | bytes 4194320 | tf_op jit(solution)/shard_map/psum | solution.py:158
  413.5 45.7 %all-gather.26.cloned.1.call-done = bf16[2048,2048]{1,0:T(8,128)(2,1)} async-done(((bf16[256,2048]{1,0:T(8,128)(2,1)}), bf16[2048,2048]{1,0:T(8,128)(2,1)}) %all-gather.26.cloned.1.call-update) | async-done | bytes 8388624 | tf_op jit(solution)/shard_map/all_gather | solution.py:163
  459.2 14.5 fusion.32
  473.7 41.7 %all-gather.24.cloned.1.call-done = bf16[2048,2048]{1,0:T(8,128)(2,1)} async-done(((bf16[256,2048]{1,0:T(8,128)(2,1)}), bf16[2048,2048]{1,0:T(8,128)(2,1)}) %all-gather.24.cloned.1.call-update) | async-done | bytes 8388624 | tf_op jit(solution)/shard_map/all_gather | solution.py:162
  515.4 14.5 fusion.36
  529.8 43.2 %all-gather.28.cloned.1.call-done = bf16[2048,2048]{1,0:T(8,128)(2,1)} async-done(((bf16[2048,256]{1,0:T(8,128)(2,1)}), bf16[2048,2048]{1,0:T(8,128)(2,1)}) %all-gather.28.cloned.1.call-update) | async-done | bytes 8388624 | tf_op jit(solution)/shard_map/all_gather | solution.py:164
  573.0 22.0 %multiply_convert_fusion.3 = (bf16[8,128,2048]{2,1,0:T(8,128)(2,1)}, bf16[8,128,2048]{2,1,0:T(8,128)(2,1)}, bf16[8,128,2048]{2,1,0:T(8,128)(2,1)}) fusion(f32[8,128,2048]{2,1,0:T(8,128)} %fusion.32, f32[8,128,2048]{2,1,0:T(8,128)} %fusion.36, bf16[8,128,2048]{2,1,0:T(8,128)(2,1)} %param.15, bf16[2048,2048]{1,0:T(8,128)(2,1)} %all-gather.28.cloned.1.call-done), kind=kOutput, calls=%fused_computation.63 | convolution fusion | flops 8621391872 | bytes 41943040 | tf_op jit(solution)/shard_map/ste,de->std/dot_general | solution.py:55
  595.0 14.7 fusion.30
  622.0 155.1 %all-reduce.11.cloned.1.call-done = bf16[8,128,2048]{2,1,0:T(8,128)(2,1)} async-done(((bf16[8,128,2048]{2,1,0:T(8,128)(2,1)}), bf16[8,128,2048]{2,1,0:T(8,128)(2,1)}) %all-reduce.11.cloned.1.call-update) | async-done | bytes 4194320 | tf_op jit(solution)/shard_map/psum | solution.py:198
  799.3 17.1 %convolution_convert_fusion = bf16[8,8,64,1024]{3,2,1,0:T(8,128)(2,1)} fusion(bf16[8,128,8,64]{1,3,2,0:T(8,128)(2,1)S(1)} %bitcast.139, f32[8,8,128,1024]{3,2,1,0:T(8,128)} %get-tuple-element.181, f32[8,8,128]{2,1,0:T(8,128)S(1)} %log_add_fusion, pred[8,128,1024]{2,1,0:T(8,128)(4,1)S(1)} %or_and_fusion), kind=kOutput, calls=%fused_computation.68 | convolution fusion | flops 1111490560 | bytes 44072960 | tf_op jit(solution)/shard_map/while/body/eval_jaxpr/vmap(hqk,qhd->khd)/dot_general | solution.py:260
  827.9 28.1 %multiply_reduce_fusion = (f32[8,8,128]{2,1,0:T(8,128)S(1)}, f32[8,8,128,1024]{3,2,1,0:T(8,128)}) fusion(f32[8,8,128,1024]{3,2,1,0:T(8,128)} %get-tuple-element.181, f32[8,8,128]{2,1,0:T(8,128)S(1)} %log_add_fusion, pred[8,128,1024]{2,1,0:T(8,128)(4,1)S(1)} %or_and_fusion, bf16[8,128,8,64]{1,3,2,0:T(8,128)(2,1)S(1)} %bitcast.140, ...), kind=kOutput, calls=%fused_computation.1 | convolution fusion | flops 1115676672 | bytes 77660160 | tf_op jit(solution)/shard_map/while/body/eval_jaxpr/vmap(qhd,khd->hqk)/dot_general | solution.py:236
  855.9 29.0 %multiply_convert_fusion = bf16[8,8,128,1024]{3,2,1,0:T(8,128)(2,1)} fusion(f32[8,8,128,1024]{3,2,1,0:T(8,128)} %get-tuple-element.183, f32[8,8,128,1024]{3,2,1,0:T(8,128)} %get-tuple-element.181, f32[8,8,128]{2,1,0:T(8,128)S(1)} %get-tuple-element.182, f32[8,8,128]{2,1,0:T(8,128)S(1)} %log_add_fusion, pred[8,128,1024]{2,1,0:T(8,128)(4,1)S(1)} %or_and_fusion), kind=kLoop, calls=%fused_computation | loop fusion | flops 50331648 | bytes 85000192 | tf_op jit(solution)/shard_map/while/body/eval_jaxpr/vmap()/convert_element_type | solution.py:240
  915.1 14.7 bitcast_multiply_fusion
  943.2 35.7 %reduce-scatter.8.cloned.1.call-done = bf16[8,128,512]{2,1,0:T(8,128)(2,1)} async-done(((bf16[8,1024,512]{2,1,0:T(8,128)(2,1)}), bf16[8,128,512]{2,1,0:T(8,128)(2,1)}) %reduce-scatter.8.cloned.1.call-update) | async-done | bytes 1048592 | tf_op jit(solution)/shard_map/reduce_scatter | solution.py:282
  992.2 14.4 fusion.42
  1017.2 14.5 bitcast_convert_fusion.2
  1054.4 18.7 %pad_maximum_fusion = bf16[2048,6144]{0,1:T(8,128)(2,1)} fusion(bf16[2048,2048]{0,1:T(8,128)(2,1)} %fusion.38, bf16[2048,2048]{0,1:T(8,128)(2,1)} %bitcast_convert_fusion.1, bf16[2048,2048]{0,1:T(8,128)(2,1)} %bitcast_convert_fusion.2), kind=kLoop, calls=%fused_computation.6 | loop fusion | flops 75497472 | bytes 50331648 | tf_op jit(solution)/shard_map/concatenate | solution.py:207
  1080.3 32.6 %reduce-scatter.16.cloned.1.call-done = bf16[256,512]{1,0:T(8,128)(2,1)} async-done(((bf16[2048,512]{1,0:T(8,128)(2,1)}), bf16[256,512]{1,0:T(8,128)(2,1)}) %reduce-scatter.16.cloned.1.call-update) | async-done | bytes 262160 | tf_op jit(solution)/shard_map/reduce_scatter | solution.py:318
  1114.7 43.1 %reduce-scatter.14.cloned.1.call-done = bf16[256,512]{1,0:T(8,128)(2,1)} async-done(((bf16[2048,512]{1,0:T(8,128)(2,1)}), bf16[256,512]{1,0:T(8,128)(2,1)}) %reduce-scatter.14.cloned.1.call-update) | async-done | bytes 262160 | tf_op jit(solution)/shard_map/reduce_scatter | solution.py:312
  1159.6 291.5 %all-reduce.13.cloned.1.call-done = (bf16[8,128,2048]{2,1,0:T(8,128)(2,1)}, bf16[8,128,2048]{2,1,0:T(8,128)(2,1)}) async-done(((bf16[8,128,2048]{2,1,0:T(8,128)(2,1)}, bf16[8,128,2048]{2,1,0:T(8,128)(2,1)}), (bf16[8,128,2048]{2,1,0:T(8,128)(2,1)}, bf16[8,128,2048]{2,1,0:T(8,128)(2,1)})) %all-reduce.13.cloned.1.call-update) | async-done | bytes 8388624 | tf_op jit(solution)/shard_map/psum | solution.py:172
  1457.0 16.4 %fusion.11 = (bf16[8,128,2048]{2,1,0:T(8,128)(2,1)}, bf16[8,128,2048]{2,1,0:T(8,128)(2,1)}, f32[]{:T(128)}) fusion(bf16[8,128,2048]{2,1,0:T(8,128)(2,1)S(1)} %copy-done.3, bf16[8,128,2048]{2,1,0:T(8,128)(2,1)} %get-tuple-element.157, f32[8,128]{1,0:T(8,128)S(1)} %broadcast_multiply_fusion.3, f32[2048]{0:T(1024)S(1)} %bitcast.156, ...), kind=kLoop, calls=%fused_computation.32 | loop fusion | flops 56623104 | bytes 33591300 | tf_op jit(solution)/shard_map/convert_element_type | solution.py:304
  1473.4 13.8 all-reduce.2
  1489.3 12.8 all-reduce.3
  1503.4 106.4 %reduce-scatter.20.cloned.1.call-done = bf16[256,6144]{0,1:T(8,128)(2,1)} async-done(((bf16[2048,6144]{0,1:T(8,128)(2,1)}), bf16[256,6144]{0,1:T(8,128)(2,1)}) %reduce-scatter.20.cloned.1.call-update) | async-done | bytes 3145744 | tf_op jit(solution)/shard_map/reduce_scatter | solution.py:206
  (236 shorter events, 262.7 us)
Async XLA Ops:
  7.2 33.2 %all-gather.18.cloned.1.call-start = ((), (), s32[]{:S(2)}) async-start(), calls=%async_computation.10 | async-start | bytes 2359296 | tf_op jit(solution)/shard_map/all_gather | solution.py:119
  7.9 62.2 %all-gather.12.cloned.1.call-start = ((), (), s32[]{:S(2)}) async-start(), calls=%async_computation.7 | async-start | bytes 2359296 | tf_op jit(solution)/shard_map/all_gather | solution.py:120
  8.7 91.1 %all-gather.16.cloned.1.call-start = ((), (), s32[]{:S(2)}) async-start(), calls=%async_computation.9 | async-start | bytes 2359296 | tf_op jit(solution)/shard_map/all_gather | solution.py:118
  9.4 147.0 %all-gather.20.cloned.1.call-start = ((), (), s32[]{:S(2)}) async-start(), calls=%async_computation.11 | async-start | bytes 9437184 | tf_op jit(solution)/shard_map/all_gather | solution.py:137
  20.5 79.3 %copy-start.32 = (f32[8,1,256]{2,1,0:T(1,128)}, f32[8,1,256]{2,1,0:T(1,128)S(1)}, u32[]{:S(2)}) copy-start(f32[8,1,256]{2,1,0:T(1,128)S(1)} %convert_element_type.232) | copy-start | bytes 24580
  21.3 83.7 %copy-start.22 = (f32[128,64]{0,1:T(8,128)}, f32[128,64]{0,1:T(8,128)S(1)}, u32[]{:S(2)}) copy-start(f32[128,64]{0,1:T(8,128)S(1)} %get-tuple-element.177) | copy-start | bytes 98308
  25.5 74.4 %copy-start.34 = (f32[8,128]{1,0:T(8,128)}, f32[8,128]{1,0:T(8,128)S(1)}, u32[]{:S(2)}) copy-start(f32[8,128]{1,0:T(8,128)S(1)} %add_rsqrt_fusion.1) | copy-start | bytes 12292
  54.9 158.1 %all-gather.14.cloned.1.call-start = ((), (), s32[]{:S(2)}) async-start(), calls=%async_computation.8 | async-start | bytes 9437184 | tf_op jit(solution)/shard_map/all_gather | solution.py:138
  76.3 166.6 %all-gather.22.cloned.1.call-start = ((), (), s32[]{:S(2)}) async-start(), calls=%async_computation.12 | async-start | bytes 2359296 | tf_op jit(solution)/shard_map/all_gather | solution.py:121
  76.9 327.1 %all-reduce.9.cloned.1.call-start = ((), (), s32[]{:S(2)}) async-start(), calls=%async_computation.13 | async-start | bytes 8388608 | tf_op jit(solution)/shard_map/psum | solution.py:158
  105.6 62.5 %copy-start.10 = (bf16[8,128,8,64]{1,3,2,0:T(8,128)(2,1)}, bf16[8,128,8,64]{1,3,2,0:T(8,128)(2,1)S(1)}, u32[]{:S(2)}) copy-start(bf16[8,128,8,64]{1,3,2,0:T(8,128)(2,1)S(1)} %fusion.47) | copy-start | bytes 3145732
  248.9 210.3 %all-gather.26.cloned.1.call-start = ((), (), s32[]{:S(2)}) async-start(), calls=%async_computation.15 | async-start | bytes 9437184 | tf_op jit(solution)/shard_map/all_gather | solution.py:163
  249.7 265.7 %all-gather.24.cloned.1.call-start = ((), (), s32[]{:S(2)}) async-start(), calls=%async_computation.14 | async-start | bytes 9437184 | tf_op jit(solution)/shard_map/all_gather | solution.py:162
  250.4 322.6 %all-gather.28.cloned.1.call-start = ((), (), s32[]{:S(2)}) async-start(), calls=%async_computation.16 | async-start | bytes 9437184 | tf_op jit(solution)/shard_map/all_gather | solution.py:164
  251.0 526.0 %all-reduce.11.cloned.1.call-start = ((), (), s32[]{:S(2)}) async-start(), calls=%async_computation.17 | async-start | bytes 8388608 | tf_op jit(solution)/shard_map/psum | solution.py:198
  260.0 527.1 %copy-start.25 = (f32[8,1,256]{2,1,0:T(1,128)}, f32[8,1,256]{2,1,0:T(1,128)S(1)}, u32[]{:S(2)}) copy-start(f32[8,1,256]{2,1,0:T(1,128)S(1)} %convert_element_type.233) | copy-start | bytes 24580
  409.1 378.0 %copy-start.30 = (f32[8,128]{1,0:T(8,128)}, f32[8,128]{1,0:T(8,128)S(1)}, u32[]{:S(2)}) copy-start(f32[8,128]{1,0:T(8,128)S(1)} %add_rsqrt_fusion) | copy-start | bytes 12292
  621.9 314.8 %reduce-scatter.10.cloned.1.call-start = ((), (), s32[]{:S(2)}) async-start(), calls=%async_computation.19 | async-start | bytes 9437184 | tf_op jit(solution)/shard_map/reduce_scatter | solution.py:285
  621.9 165.1 %copy-start.36 = (f32[8,128]{1,0:T(8,128)}, f32[8,128]{1,0:T(8,128)S(1)}, u32[]{:S(2)}) copy-start(f32[8,128]{1,0:T(8,128)S(1)} %dynamic-slice_convert_fusion) | copy-start | bytes 12292
  827.8 151.1 %reduce-scatter.8.cloned.1.call-start = ((), (), s32[]{:S(2)}) async-start(), calls=%async_computation.18 | async-start | bytes 9437184 | tf_op jit(solution)/shard_map/reduce_scatter | solution.py:282
  907.9 168.5 %reduce-scatter.18.cloned.1.call-start = ((), (), s32[]{:S(2)}) async-start(), calls=%async_computation.23 | async-start | bytes 2359296 | tf_op jit(solution)/shard_map/reduce_scatter | solution.py:324
  915.0 163.5 %reduce-scatter.12.cloned.1.call-start = ((), (), s32[]{:S(2)}) async-start(), calls=%async_computation.20 | async-start | bytes 2359296 | tf_op jit(solution)/shard_map/reduce_scatter | solution.py:306
  936.6 43.8 %copy-start.23 = (f32[128,64]{0,1:T(8,128)S(1)}, f32[128,64]{0,1:T(8,128)}, u32[]{:S(2)}) copy-start(f32[128,64]{0,1:T(8,128)} %copy-done.22) | copy-start | bytes 98308
  936.6 176.3 %reduce-scatter.16.cloned.1.call-start = ((), (), s32[]{:S(2)}) async-start(), calls=%async_computation.22 | async-start | bytes 2359296 | tf_op jit(solution)/shard_map/reduce_scatter | solution.py:318
  943.1 214.6 %reduce-scatter.14.cloned.1.call-start = ((), (), s32[]{:S(2)}) async-start(), calls=%async_computation.21 | async-start | bytes 2359296 | tf_op jit(solution)/shard_map/reduce_scatter | solution.py:312
  992.2 458.9 %all-reduce.13.cloned.1.call-start = ((), (), s32[]{:S(2)}) async-start(), calls=%async_computation.25 | async-start | bytes 16777216 | tf_op jit(solution)/shard_map/psum | solution.py:172
  1017.2 592.6 %reduce-scatter.20.cloned.1.call-start = ((), (), s32[]{:S(2)}) async-start(), calls=%async_computation.24 | async-start | bytes 28311552 | tf_op jit(solution)/shard_map/reduce_scatter | solution.py:206
  1073.1 383.5 %copy-start.26 = (f32[8,1,256]{2,1,0:T(1,128)S(1)}, f32[8,1,256]{2,1,0:T(1,128)}, u32[]{:S(2)}) copy-start(f32[8,1,256]{2,1,0:T(1,128)} %copy-done.25) | copy-start | bytes 24580
  1073.1 383.5 %copy-start.31 = (f32[8,128]{1,0:T(8,128)S(1)}, f32[8,128]{1,0:T(8,128)}, u32[]{:S(2)}) copy-start(f32[8,128]{1,0:T(8,128)} %copy-done.30) | copy-start | bytes 12292
  1073.1 383.5 %copy-start.37 = (f32[8,128]{1,0:T(8,128)S(1)}, f32[8,128]{1,0:T(8,128)}, u32[]{:S(2)}) copy-start(f32[8,128]{1,0:T(8,128)} %copy-done.36) | copy-start | bytes 12292
  1073.1 383.5 %copy-start.39 = (f32[8,128]{1,0:T(8,128)S(1)}, f32[8,128]{1,0:T(8,128)}, u32[]{:S(2)}) copy-start(f32[8,128]{1,0:T(8,128)} %copy-done.38) | copy-start | bytes 12292
  1457.0 32.3 %copy-start.40 = (bf16[2048]{0:T(1024)(128)(2,1)S(1)}, bf16[2048]{0:T(1024)(128)(2,1)}, u32[]{:S(2)}) copy-start(bf16[2048]{0:T(1024)(128)(2,1)} %get-tuple-element.145) | copy-start | bytes 12292
  (41 other events, 380.6 us)
Sparse Core Ops, SparseCore 0:
  9.9 30.4 all-gather.17
  42.3 27.7 all-gather.11
  72.0 27.7 all-gather.15
  102.1 54.2 all-gather.19
  158.8 54.2 all-gather.13
  214.8 28.0 all-gather.21
  249.0 154.9 all-reduce.8
  405.9 53.2 all-gather.25
  461.1 54.2 all-gather.23
  517.1 55.8 all-gather.27
  622.0 154.9 all-reduce.10
  827.9 70.3 reduce-scatter.9
  908.0 70.8 reduce-scatter.7
  982.1 41.0 reduce-scatter.17
  1026.9 41.1 reduce-scatter.11
  1071.8 41.0 reduce-scatter.15
  1116.6 41.1 reduce-scatter.13
  1160.2 290.8 all-reduce.12
  1454.7 155.0 reduce-scatter.19
where the time goes:
time: 1640 us; the launch traced here: 1630 us
  waiting for transfers between devices  1060 us (65%)
  matrix products  292 us (18%)
  other arithmetic  134 us (8%)
  local copies, waits for them, and re-layouts  76.2 us (5%)
  blocking collectives  45.9 us (3%)
  between operations  22.1 us (1%)
    psum x1, waiting for transfers between devices, per_device(): lax.psum(project(activated, mlp_set[2]).astype(jnp.bfloat16), 'dp')  292 us
    psum x1, waiting for transfers between devices, per_device(): lax.psum((project_back(gate_back, mlp_back[0]) + project_back(up_back, ml...  155 us
    psum x1, waiting for transfers between devices, per_device(): lax.psum(project(mixed, attn_set[3]).astype(jnp.bfloat16), 'dp')  144 us
    reduce_scatter x1, waiting for transfers between devices, per_device(): lax.psum_scatter(jnp.concatenate([weight_term(normed_two, gate_back), wei...  106 us
    dot_general x7, matrix products, project(): jnp.einsum('std,de->ste', values, weight, preferred_element_type=jnp.floa...  67.1 us
    dot_general x7, matrix products, project_back(): jnp.einsum('ste,de->std', grads, weight, preferred_element_type=jnp.float32)  61.6 us
    dot_general x7, matrix products, weight_term(): jnp.einsum('std,ste->de', values, grads, preferred_element_type=jnp.float32)  60 us
    all_gather x1, waiting for transfers between devices, per_device(): lax.all_gather(keys_here, 'fsdp', axis=1, tiled=True)  50.9 us
  transfers between devices with their start and end apart: 19, of which 16 were waited for; matrix products, arithmetic and copies ran while one was open for 23% of the time, Pallas kernels for 0%

commit v1 on v0

--- a/solution.py
+++ b/solution.py
@@ -1,7 +1,12 @@
+import functools
+
 import jax
 import jax.numpy as jnp
 from jax import lax
+from jax.experimental import pallas as pl
+from jax.experimental.pallas import tpu as pltpu
 from jax.sharding import PartitionSpec as P
+
 
 HD = 64
 PIECE = 256
@@ -83,7 +88,7 @@
     )
 
 
-def per_device(
+def per_device_gather(
     inputs,
     cotangent,
     piece_start,
@@ -356,6 +361,729 @@
     )
 
 
+VMEM_MOST = 66_000_000
+MESH = pl.DeviceIdType.MESH
+BF16 = jnp.bfloat16
+F32 = jnp.float32
+PAIR = 2 * HD
+TILE = 256
+STRIP = 64
+HOP = 2
+
+NT = (((1,), (1,)), ((), ()))
+TN = (((0,), (0,)), ((), ()))
+
+
+def mm(a, b):
+    return jnp.dot(a, b, preferred_element_type=F32)
+
+
+def mm_nt(a, b):
+    return lax.dot_general(a, b, NT, preferred_element_type=F32)
+
+
+def mm_tn(a, b):
+    return lax.dot_general(a, b, TN, preferred_element_type=F32)
+
+
+def half_swap(values):
+    lane = lax.broadcasted_iota(jnp.int32, values.shape, 1) % HD
+    ahead = pltpu.roll(values, PAIR - HD // 2, 1)
+    behind = pltpu.roll(values, HD // 2, 1)
+    return jnp.where(lane < HD // 2, ahead, behind)
+
+
+def head_lanes(values, head):
+    lane = lax.broadcasted_iota(jnp.int32, values.shape, 1) // HD
+    return jnp.where(lane == head, values, jnp.zeros_like(values))
+
+
+def diagonal_bias(is_piece):
+    key = lax.broadcasted_iota(jnp.int32, (TILE, TILE), 0)
+    query = lax.broadcasted_iota(jnp.int32, (TILE, TILE), 1)
+    return jnp.where((key <= query) | is_piece, 0.0, NEG).astype(F32)
+
+
+def attend_kernel(
+    image_ref,
+    q_in,
+    k_in,
+    v_in,
+    cos_ref,
+    sin_ref,
+    bias_ref,
+    q_ref,
+    k_ref,
+    v_ref,
+    mixed_ref,
+    lse_ref,
+    top,
+    total,
+    acc,
+    outs,
+):
+    length = q_in.shape[0]
+    tiles = length // TILE
+    cosine, sine = cos_ref[...], sin_ref[...]
+    raw = q_in[...]
+    q_ref[...] = ((raw * cosine + half_swap(raw) * sine) * HD ** (-0.5)).astype(BF16)
+    raw = k_in[...]
+    k_ref[...] = (raw * cosine + half_swap(raw) * sine).astype(BF16)
+    v_ref[...] = v_in[...].astype(BF16)
+    lse_ref[...] = jnp.zeros_like(lse_ref)
+    for tile in range(tiles):
+        here = slice(tile * TILE, (tile + 1) * TILE)
+        upto = (tile + 1) * TILE
+        corner = diagonal_bias(image_ref[tile] >= 0)
+        for head in range(2):
+            query = head_lanes(q_ref[here, :], head)
+            scores = mm_nt(k_ref[:upto, :], query) + bias_ref[:upto, :]
+            diag = scores[upto - TILE :, :] + corner
+            highest = jnp.max(diag, axis=0, keepdims=True)
+            if tile:
+                before = scores[: upto - TILE, :]
+                highest = jnp.maximum(highest, jnp.max(before, axis=0, keepdims=True))
+                weight_low = jnp.exp(before - highest)
+                weight_diag = jnp.exp(diag - highest)
+                summed = jnp.sum(weight_low, axis=0, keepdims=True) + jnp.sum(
+                    weight_diag, axis=0, keepdims=True
+                )
+                mixed = mm_tn(v_ref[: upto - TILE, :], weight_low.astype(BF16)) + mm_tn(
+                    v_ref[upto - TILE : upto, :], weight_diag.astype(BF16)
+                )
+            else:
+                weight_diag = jnp.exp(diag - highest)
+                summed = jnp.sum(weight_diag, axis=0, keepdims=True)
+                mixed = mm_tn(v_ref[:upto, :], weight_diag.astype(BF16))
+            top[...] = highest
+            total[...] = summed
+            acc[...] = mixed
+            for other in range(tile + 1, tiles):
+
+                @pl.when((image_ref[tile] >= 0) & (image_ref[tile] == image_ref[other]))
+                def _(other=other, query=query):
+                    there = slice(other * TILE, (other + 1) * TILE)
+                    extra = mm_nt(k_ref[there, :], query) + bias_ref[there, :]
+                    newest = jnp.maximum(top[...], jnp.max(extra, axis=0, keepdims=True))
+                    shrink = jnp.exp(top[...] - newest)
+                    weight = jnp.exp(extra - newest)
+                    total[...] = total[...] * shrink + jnp.sum(weight, axis=0, keepdims=True)
+                    acc[...] = acc[...] * shrink + mm_tn(v_ref[there, :], weight.astype(BF16))
+                    top[...] = newest
+
+            rows = slice(head * HD, (head + 1) * HD)
+            outs[rows, :] = acc[rows, :] / total[...]
+            lse_ref[0, head : head + 1, here] = top[...] + jnp.log(total[...])
+        mixed_ref[here, :] = outs[...].T.astype(BF16)
+
+
+def attend(qkv, cosine, sine, bias, image):
+    length, wide = qkv.shape
+    band = wide // 3
+    pairs = band // PAIR
+    column = lambda shift: pl.BlockSpec((length, PAIR), lambda g, img: (0, g + shift))
+    fixed = lambda cols: pl.BlockSpec((length, cols), lambda g, img: (0, 0))
+    low = jax.ShapeDtypeStruct((length, band), BF16)
+    return pl.pallas_call(
+        attend_kernel,
+        grid_spec=pltpu.PrefetchScalarGridSpec(
+            num_scalar_prefetch=1,
+            grid=(pairs,),
+            in_specs=[
+                column(0),
+                column(pairs),
+                column(2 * pairs),
+                fixed(PAIR),
+                fixed(PAIR),
+                fixed(1),
+            ],
+            out_specs=[column(0)] * 4 + [pl.BlockSpec((1, 8, length), lambda g, img: (g, 0, 0))],
+            scratch_shapes=[
+                pltpu.VMEM((1, TILE), F32),
+                pltpu.VMEM((1, TILE), F32),
+                pltpu.VMEM((PAIR, TILE), F32),
+                pltpu.VMEM((PAIR, TILE), F32),
+            ],
+        ),
+        out_shape=[low] * 4 + [jax.ShapeDtypeStruct((pairs, 8, length), F32)],
+        compiler_params=pltpu.CompilerParams(vmem_limit_bytes=VMEM_MOST),
+        cost_estimate=pl.CostEstimate(
+            flops=12_000_000_000, bytes_accessed=12_000_000, transcendentals=6_000_000
+        ),
+        name="attend",
+    )(image, qkv, qkv, qkv, cosine, sine, bias)
+
+
+def attend_back_kernel(
+    image_ref,
+    q_ref,
+    k_ref,
+    v_ref,
+    g_ref,
+    mixed_ref,
+    lse_ref,
+    cos_ref,
+    sin_ref,
+    bias_ref,
+    dq_ref,
+    dk_ref,
+    dv_ref,
+    dk_acc,
+    dv_acc,
+    dq_acc,
+):
+    length = q_ref.shape[0]
+    tiles = length // TILE
+    dk_acc[...] = jnp.zeros_like(dk_acc)
+    dv_acc[...] = jnp.zeros_like(dv_acc)
+    pick_row = lax.broadcasted_iota(jnp.int32, (8, PAIR), 0)
+    pick_lane = lax.broadcasted_iota(jnp.int32, (8, PAIR), 1) // HD
+    picker = (pick_row == pick_lane).astype(F32)
+    for tile in range(tiles):
+        here = slice(tile * TILE, (tile + 1) * TILE)
+        corner = diagonal_bias(image_ref[tile] >= 0)
+        product = mixed_ref[here, :].astype(F32) * g_ref[here, :].astype(F32)
+        inners = lax.dot_general(
+            picker, product, NT, precision=lax.Precision.HIGHEST, preferred_element_type=F32
+        )
+        for head in range(2):
+            query = head_lanes(q_ref[here, :], head)
+            grad = head_lanes(g_ref[here, :], head)
+            inner = inners[head : head + 1, :]
+            lse = lse_ref[0, head : head + 1, here]
+            rows = slice(head * HD, (head + 1) * HD)
+
+            def block(there, extra, first):
+                scores = mm_nt(k_ref[there, :], query) + bias_ref[there, :]
+                if extra is not None:
+                    scores = scores + extra
+                weight = jnp.exp(scores - lse)
+                back = mm_nt(v_ref[there, :], grad)
+                score_back = (weight * (back - inner)).astype(BF16)
+                dv_acc[there, :] += mm(weight.astype(BF16), grad)
+                dk_acc[there, :] += mm(score_back, query)
+                part = mm_tn(k_ref[there, :], score_back)
+                if first:
+                    dq_acc[rows, :] = part[rows, :]
+                else:
+                    dq_acc[rows, :] += part[rows, :]
+
+            block(here, corner, True)
+            for other in range(tile):
+                block(slice(other * TILE, (other + 1) * TILE), None, False)
+            for other in range(tile + 1, tiles):
+
+                @pl.when((image_ref[tile] >= 0) & (image_ref[tile] == image_ref[other]))
+                def _(other=other):
+                    block(slice(other * TILE, (other + 1) * TILE), None, False)
+
+        turned = dq_acc[...].T * HD ** (-0.5)
+        dq_ref[here, :] = (
+            turned * cos_ref[here, :] - half_swap(turned) * sin_ref[here, :]
+        ).astype(BF16)
+    turned = dk_acc[...]
+    dk_ref[...] = (turned * cos_ref[...] - half_swap(turned) * sin_ref[...]).astype(BF16)
+    dv_ref[...] = dv_acc[...].astype(BF16)
+
+
+def attend_back(queries, keys, values, grads, mixed, lse, cosine, sine, bias, image):
+    length, band = queries.shape
+    pairs = band // PAIR
+    column = pl.BlockSpec((length, PAIR), lambda g, img: (0, g))
+    fixed = lambda cols: pl.BlockSpec((length, cols), lambda g, img: (0, 0))
+    low = jax.ShapeDtypeStruct((length, band), BF16)
+    return pl.pallas_call(
+        attend_back_kernel,
+        grid_spec=pltpu.PrefetchScalarGridSpec(
+            num_scalar_prefetch=1,
+            grid=(pairs,),
+            in_specs=[column] * 5
+            + [
+                pl.BlockSpec((1, 8, length), lambda g, img: (g, 0, 0)),
+                fixed(PAIR),
+                fixed(PAIR),
+                fixed(1),
+            ],
+            out_specs=[column] * 3,
+            scratch_shapes=[
+                pltpu.VMEM((length, PAIR), F32),
+                pltpu.VMEM((length, PAIR), F32),
+                pltpu.VMEM((PAIR, TILE), F32),
+            ],
+        ),
+        out_shape=[low] * 3,
+        compiler_params=pltpu.CompilerParams(vmem_limit_bytes=VMEM_MOST),
+        cost_estimate=pl.CostEstimate(
+            flops=30_000_000_000, bytes_accessed=12_000_000, transcendentals=6_000_000
+        ),
+        name="attend_back",
+    )(image, queries, keys, values, grads, mixed, lse, cosine, sine, bias)
+
+
+def line_sum(n, own, flows, make, finish):
+    from_low, from_high, to_high, to_low, sems = flows
+    send_high, send_low, got_low, got_high = (sems.at[k] for k in range(4))
+    rank = lax.axis_index("dp")
+    strips = own.shape[0] // STRIP
+    has_low, has_high = rank > 0, rank < n - 1
+    higher, lower = lax.rem(rank + 1, n), lax.rem(rank + n - 1, n)
+
+    barrier = pltpu.get_barrier_semaphore()
+
+    @pl.when(has_low)
+    def _():
+        pl.semaphore_signal(barrier, inc=1, device_id={"dp": lower}, device_id_type=MESH)
+
+    @pl.when(has_high)
+    def _():
+        pl.semaphore_signal(barrier, inc=1, device_id={"dp": higher}, device_id_type=MESH)
+
+    pl.semaphore_wait(barrier, has_low.astype(jnp.int32) + has_high.astype(jnp.int32))
+
+    def rows_of(strip):
+        return pl.ds(pl.multiple_of(strip * STRIP, STRIP), STRIP)
+
+    def up(strip):
+        rows = rows_of(strip)
+        return pltpu.make_async_remote_copy(
+            src_ref=to_high.at[rows],
+            dst_ref=from_low.at[rows],
+            send_sem=send_high.at[strip],
+            recv_sem=got_low.at[strip],
+            device_id={"dp": higher},
+            device_id_type=MESH,
+        )
+
+    def down(strip):
+        rows = rows_of(strip)
+        return pltpu.make_async_remote_copy(
+            src_ref=to_low.at[rows],
+            dst_ref=from_high.at[rows],
+            send_sem=send_low.at[strip],
+            recv_sem=got_high.at[strip],
+            device_id={"dp": lower},
+            device_id_type=MESH,
+        )
+
+    @pl.when(jnp.logical_not(has_low))
+    def _():
+        from_low[...] = jnp.zeros_like(from_low)
+
+    @pl.when(jnp.logical_not(has_high))
+    def _():
+        from_high[...] = jnp.zeros_like(from_high)
+
+    late = jnp.maximum(rank, n - 1 - rank)
+
+    def step(s, carry):
+        @pl.when(s < strips)
+        def _():
+            make(s, rows_of(s))
+
+        a = s - rank * HOP
+
+        @pl.when((a >= 0) & (a < strips))
+        def _():
+            @pl.when(has_low)
+            def _():
+                up(a).wait_recv()
+
+            @pl.when(has_high)
+            def _():
+                rows = rows_of(a)
+                to_high[rows, :] = (
+                    own[rows, :].astype(F32) + from_low[rows, :].astype(F32)
+                ).astype(BF16)
+                up(a).start()
+
+        b = s - (n - 1 - rank) * HOP
+
+        @pl.when((b >= 0) & (b < strips))
+        def _():
+            @pl.when(has_high)
+            def _():
+                down(b).wait_recv()
+
+            @pl.when(has_low)
+            def _():
+                rows = rows_of(b)
+                to_low[rows, :] = (
+                    own[rows, :].astype(F32) + from_high[rows, :].astype(F32)
+                ).astype(BF16)
+                down(b).start()
+
+        c = s - late * HOP
+
+        @pl.when((c >= 0) & (c < strips))
+        def _():
+            rows = rows_of(c)
+            finish(
+                c,
+                rows,
+                own[rows, :].astype(F32)
+                + from_low[rows, :].astype(F32)
+                + from_high[rows, :].astype(F32),
+            )
+
+        return carry
+
+    lax.fori_loop(0, strips + (n - 1) * HOP, step, 0)
+
+    def drain(s, carry):
+        @pl.when(has_high)
+        def _():
+            up(s).wait_send()
+
+        @pl.when(has_low)
+        def _():
+            down(s).wait_send()
+
+        return carry
+
+    lax.fori_loop(0, strips, drain, 0)
+
+
+def flow_scratch(length, width):
+    whole = pltpu.VMEM((length, width), BF16)
+    return [whole] * 4 + [pltpu.SemaphoreType.DMA((4, length // STRIP))]
+
+
+VM = pl.BlockSpec(memory_space=pltpu.VMEM)
+ANY = pl.BlockSpec(memory_space=pl.ANY)
+
+
+def row_mean(values):
+    return jnp.mean(values, axis=1, keepdims=True)
+
+
+def col_sum(values):
+    return jnp.sum(values, axis=0, keepdims=True)
+
+
+def line_call(kernel, n, name, collective_id, args, out_shape, scratch, specs, flops=10**9):
+    return pl.pallas_call(
+        functools.partial(kernel, n),
+        in_specs=specs,
+        out_specs=[VM] * len(out_shape),
+        out_shape=out_shape,
+        scratch_shapes=scratch,
+        compiler_params=pltpu.CompilerParams(
+            collective_id=collective_id, has_side_effects=True, vmem_limit_bytes=VMEM_MOST
+        ),
+        cost_estimate=pl.CostEstimate(
+            flops=flops, bytes_accessed=200_000_000, transcendentals=0
+        ),
+        name=name,
+    )(*args)
+
+
+def middle_kernel(
+    n,
+    mixed_ref,
+    out_weight,
+    source,
+    gain,
+    valid,
+    middle_ref,
+    normed_ref,
+    stats_ref,
+    own,
+    weight,
+    weight_sem,
+    *flows,
+):
+    band = weight.shape[1]
+    load = pltpu.make_async_copy(
+        out_weight.at[:, pl.ds(out_weight.shape[1] - band, band)], weight, weight_sem
+    )
+    load.start()
+    stats_ref[...] = jnp.zeros_like(stats_ref)
+    load.wait()
+
+    def make(strip, rows):
+        own[rows, :] = mm_nt(mixed_ref[rows, :], weight[...]).astype(BF16)
+
+    def finish(strip, rows, total):
+        middle = source[rows, :].astype(F32) + total
+        middle_ref[rows, :] = middle
+        square = middle * middle
+        scale = lax.rsqrt(row_mean(square) + EPS)
+        normed_ref[rows, :] = (middle * scale * gain[...]).astype(BF16)
+        stats_ref[0:1, :] += col_sum(square * valid[rows, :])
+        stats_ref[1:2, :] += col_sum(total * total * valid[rows, :])
+
+    line_sum(n, own, flows, make, finish)
+
+
+def middle_sum(n, mixed, gathered, source, gain, valid):
+    length, width = source.shape
+    band = mixed.shape[1]
+    return line_call(
+        middle_kernel,
+        n,
+        "middle_sum",
+        1,
+        (mixed, gathered, source, gain, valid),
+        [
+            jax.ShapeDtypeStruct((length, width), F32),
+            jax.ShapeDtypeStruct((length, width), BF16),
+            jax.ShapeDtypeStruct((8, width), F32),
+        ],
+        [
+            pltpu.VMEM((length, width), BF16),
+            pltpu.VMEM((width, band), BF16),
+            pltpu.SemaphoreType.DMA,
+        ]
+        + flow_scratch(length, width),
+        [VM, ANY, VM, VM, VM],
+    )
+
+
+def middle_back_kernel(n, own, cotangent, middle_ref, gain, back_ref, low_ref, gain_ref, *flows):
+    gain_ref[...] = jnp.zeros_like(gain_ref)
+
+    def make(strip, rows):
+        pass
+
+    def finish(strip, rows, total):
+        middle = middle_ref[rows, :]
+        scale = lax.rsqrt(row_mean(middle * middle) + EPS)
+        scaled = total * gain[...]
+        inner = row_mean(scaled * middle)
+        back = cotangent[rows, :].astype(F32) + scale * (scaled - middle * (scale * scale * inner))
+        back_ref[rows, :] = back
+        low_ref[rows, :] = back.astype(BF16)
+        gain_ref[0:1, :] += col_sum(total * middle * scale)
+
+    line_sum(n, own, flows, make, finish)
+
+
+def middle_back_sum(n, part, cotangent, middle, gain):
+    length, width = part.shape
+    return line_call(
+        middle_back_kernel,
+        n,
+        "middle_back_sum",
+        2,
+        (part, cotangent, middle, gain),
+        [
+            jax.ShapeDtypeStruct((length, width), F32),
+            jax.ShapeDtypeStruct((length, width), BF16),
+            jax.ShapeDtypeStruct((8, width), F32),
+        ],
+        flow_scratch(length, width),
+        [VM] * 4,
+    )
+
+
+def output_kernel(n, own, middle_ref, valid, out_ref, stats_ref, *flows):
+    stats_ref[...] = jnp.zeros_like(stats_ref)
+
+    def make(strip, rows):
+        pass
+
+    def finish(strip, rows, total):
+        out_ref[rows, :] = (middle_ref[rows, :] + total).astype(BF16)
+        stats_ref[0:1, :] += col_sum(total * total * valid[rows, :])
+
+    line_sum(n, own, flows, make, finish)
+
+
+def output_sum(n, part, middle, valid):
+    length, width = part.shape
+    return line_call(
+        output_kernel,
+        n,
+        "output_sum",
+        3,
+        (part, middle, valid),
+        [
+            jax.ShapeDtypeStruct((length, width), BF16),
+            jax.ShapeDtypeStruct((8, width), F32),
+        ],
+        flow_scratch(length, width),
+        [VM] * 3,
+    )
+
+
+def input_kernel(n, own, source_ref, back_ref, gain, grad_ref, gain_ref, *flows):
+    gain_ref[...] = jnp.zeros_like(gain_ref)
+
+    def make(strip, rows):
+        pass
+
+    def finish(strip, rows, total):
+        source = source_ref[rows, :].astype(F32)
+        scale = lax.rsqrt(row_mean(source * source) + EPS)
+        scaled = total * gain[...]
+        inner = row_mean(scaled * source)
+        grad_ref[rows, :] = (
+            back_ref[rows, :] + scale * (scaled - source * (scale * scale * inner))
+        ).astype(BF16)
+        gain_ref[0:1, :] += col_sum(total * source * scale)
+
+    line_sum(n, own, flows, make, finish)
+
+
+def input_sum(n, part, source, back, gain):
+    length, width = part.shape
+    return line_call(
+        input_kernel,
+        n,
+        "input_sum",
+        4,
+        (part, source, back, gain),
+        [
+            jax.ShapeDtypeStruct((length, width), BF16),
+            jax.ShapeDtypeStruct((8, width), F32),
+        ],
+        flow_scratch(length, width),
+        [VM] * 4,
+    )
+
+
+def per_device(
+    mesh_sizes,
+    inputs,
+    cotangent,
+    piece_start,
+    piece_image,
+    valid_mask,
+    query_weight,
+    key_weight,
+    value_weight,
+    output_weight,
+    attn_gain,
+    gate_weight,
+    up_weight,
+    down_weight,
+    mlp_gain,
+):
+    spread, line = mesh_sizes
+    seqs, local, width = inputs.shape
+    length = valid_mask.shape[1]
+    band = query_weight.shape[1]
+    feed = gate_weight.shape[1]
+    mine = lax.axis_index("fsdp")
+
+    def swap(values):
+        return lax.all_to_all(values, "fsdp", split_axis=0, concat_axis=0, tiled=True)
+
+    attn_w = lax.all_gather(
+        jnp.concatenate([query_weight, key_weight, value_weight, output_weight.T], axis=1),
+        "fsdp",
+        axis=0,
+        tiled=True,
+    )
+    gains = lax.all_gather(jnp.stack([attn_gain, mlp_gain]), "fsdp", axis=1, tiled=True).astype(F32)
+    attn_g, mlp_g = gains[0:1], gains[1:2]
+    mlp_w = lax.all_gather(
+        jnp.concatenate([gate_weight, up_weight, down_weight.T], axis=1),
+        "fsdp",
+        axis=0,
+        tiled=True,
+    )
+    source = swap(inputs).reshape(length, width)
+    upstream = swap(cotangent).reshape(length, width)
+
+    places = jnp.arange(length, dtype=jnp.int32)
+    cosine, sine = rope_tables(places, HD)
+    signs = jnp.where(jnp.arange(HD) < HD // 2, -1.0, 1.0).astype(F32)
+    cosine = jnp.concatenate([cosine, cosine], axis=1)
+    sine = jnp.concatenate([sine * signs, sine * signs], axis=1)
+    valid_row = lax.dynamic_index_in_dim(valid_mask, mine, 0, keepdims=False)
+    valid = valid_row.astype(F32)[:, None]
+    bias = jnp.where(valid_row > 0, 0.0, NEG).astype(F32)[:, None]
+    starts = lax.dynamic_index_in_dim(piece_start, mine, 0, keepdims=False)
+    images = lax.dynamic_index_in_dim(piece_image, mine, 0, keepdims=False)
+    image = image_of(jnp.arange(length // TILE, dtype=jnp.int32) * TILE, starts, images).astype(
+        jnp.int32
+    )
+
+    residual = source.astype(F32)
+    scale_one = lax.rsqrt(jnp.mean(residual * residual, axis=1, keepdims=True) + EPS)
+    normed_one = (residual * scale_one * attn_g).astype(BF16)
+    qkv = mm(normed_one, attn_w[:, : 3 * band])
+    queries, keys, values, mixed, lse = attend(qkv, cosine, sine, bias, image)
+    middle, normed_two, stats = middle_sum(line, mixed, attn_w, source, mlp_g, valid)
+
+    gate = mm(normed_two, mlp_w[:, :feed])
+    up = mm(normed_two, mlp_w[:, feed : 2 * feed])
+    sig = jax.nn.sigmoid(gate)
+    activated = (gate * sig * up).astype(BF16)
+    act_grad = mm(upstream, mlp_w[:, 2 * feed :])
+    gate_back = (act_grad * up * (sig + gate * sig * (1.0 - sig))).astype(BF16)
+    up_back = (act_grad * gate * sig).astype(BF16)
+    back_part = (
+        mm_nt(gate_back, mlp_w[:, :feed]) + mm_nt(up_back, mlp_w[:, feed : 2 * feed])
+    ).astype(BF16)
+    middle_back, middle_low, mlp_gain_sum = middle_back_sum(
+        line, back_part, upstream, middle, mlp_g
+    )
+    mlp_grads = lax.psum_scatter(
+        jnp.concatenate(
+            [
+                mm_tn(normed_two, gate_back).astype(BF16),
+                mm_tn(normed_two, up_back).astype(BF16),
+                mm_tn(upstream, activated).astype(BF16),
+            ],
+            axis=1,
+        ),
+        "fsdp",
+        scatter_dimension=0,
+        tiled=True,
+    ).astype(F32)
+    mixed_back = mm(middle_low, attn_w[:, 3 * band :]).astype(BF16)
+    dq, dk, dv = attend_back(
+        queries, keys, values, mixed_back, mixed, lse, cosine, sine, bias, image
+    )
+    mlp_part = mm_nt(activated, mlp_w[:, 2 * feed :]).astype(BF16)
+    result, mlp_stats = output_sum(line, mlp_part, middle, valid)
+    output = swap(result.reshape(seqs, local, width))
+    front_part = mm_nt(jnp.concatenate([dq, dk, dv], axis=1), attn_w[:, : 3 * band]).astype(BF16)
+    source_grad, attn_gain_sum = input_sum(line, front_part, source, middle_back, attn_g)
+    input_grad = swap(source_grad.reshape(seqs, local, width))
+    attn_grads = lax.psum_scatter(
+        jnp.concatenate(
+            [
+                mm_tn(normed_one, dq).astype(BF16),
+                mm_tn(normed_one, dk).astype(BF16),
+                mm_tn(normed_one, dv).astype(BF16),
+                mm_tn(middle_low, mixed).astype(BF16),
+            ],
+            axis=1,
+        ),
+        "fsdp",
+        scatter_dimension=0,
+        tiled=True,
+    ).astype(F32)
+    sums = jnp.stack([jnp.sum(stats[0]), jnp.sum(stats[1]), jnp.sum(mlp_stats[0])])
+    small = lax.psum(
+        jnp.concatenate([attn_gain_sum[0], mlp_gain_sum[0], sums]), "fsdp"
+    )
+    share = width // spread
+    attn_gain_part = lax.dynamic_slice_in_dim(small, mine * share, share)
+    mlp_gain_part = lax.dynamic_slice_in_dim(small, width + mine * share, share)
+    count = jnp.sum(valid_mask).astype(F32) * width
+    roots = jnp.sqrt(small[2 * width :] / count)
+    return (
+        output,
+        input_grad,
+        attn_grads[:, :band],
+        attn_grads[:, band : 2 * band],
+        attn_grads[:, 2 * band : 3 * band],
+        attn_grads[:, 3 * band :].T,
+        attn_gain_part,
+        mlp_grads[:, :feed],
+        mlp_grads[:, feed : 2 * feed],
+        mlp_grads[:, 2 * feed :].T,
+        mlp_gain_part,
+        roots[0],
+        roots[1],
+        roots[2],
+    )
+
+
 def solution(mesh):
     placed = (
         P(None, "fsdp", None),
@@ -373,25 +1101,33 @@
         P("dp", "fsdp"),
         P("fsdp"),
     )
-    return jax.shard_map(
-        per_device,
-        mesh=mesh,
-        in_specs=placed,
-        out_specs=(
-            P(None, "fsdp", None),
-            P(None, "fsdp", None),
-            P("fsdp", "dp"),
-            P("fsdp", "dp"),
-            P("fsdp", "dp"),
-            P("dp", "fsdp"),
-            P("fsdp"),
-            P("fsdp", "dp"),
-            P("fsdp", "dp"),
-            P("dp", "fsdp"),
-            P("fsdp"),
-            P(),
-            P(),
-            P(),
-        ),
-        check_vma=False,
-    )
+    spread, line = mesh.shape["fsdp"], mesh.shape["dp"]
+
+    def whole(*arrays):
+        seqs, length, _ = arrays[0].shape
+        own_sequence = seqs == spread and length % (2 * TILE) == 0 and line > 1
+        each = functools.partial(per_device, (spread, line)) if own_sequence else per_device_gather
+        return jax.shard_map(
+            each,
+            mesh=mesh,
+            in_specs=placed,
+            out_specs=(
+                P(None, "fsdp", None),
+                P(None, "fsdp", None),
+                P("fsdp", "dp"),
+                P("fsdp", "dp"),
+                P("fsdp", "dp"),
+                P("dp", "fsdp"),
+                P("fsdp"),
+                P("fsdp", "dp"),
+                P("fsdp", "dp"),
+                P("dp", "fsdp"),
+                P("fsdp"),
+                P(),
+                P(),
+                P(),
+            ),
+            check_vma=False,
+        )(*arrays)
+
+    return whole

time: 1640 us -> 969 us (0.59)
  waiting for transfers between devices: 1060 us -> 4.13 us
  Pallas kernels: 0 us -> 539 us
  matrix products: 292 us -> 173 us
  other arithmetic: 134 us -> 46.3 us
  blocking collectives: 45.9 us -> 120 us
  local copies, waits for them, and re-layouts: 76.2 us -> 36 us
  starting transfers between devices: 0.98 us -> 33.9 us
    psum x3 -> x0, waiting for transfers between devices: 591 us -> none  [the longest x1 292 us: per_device(): lax.psum(project(activated, mlp_set[2]).astype(jnp.bfloat16), 'dp')]
    pallas_call x0 -> x6, Pallas kernels: none -> 539 us  [the longest x4 476 us: line_call(): pl.pallas_call(functools.partial(kernel, n), in_specs=specs, out_specs=[V...]
    all_gather x9 -> x2, waiting for transfers between devices: 248 us -> 4.05 us  [the longest x1 4.03 us: per_device(): lax.all_gather(jnp.concatenate([query_weight, key_weight, value_weight, o...]
    reduce_scatter x7 -> x2, waiting for transfers between devices: 218 us -> 0.01 us  [the longest x1 0.01 us: per_device(): lax.psum_scatter(jnp.concatenate([mm_tn(normed_one, dq).astype(BF16), mm_...]
    dot_general x27 -> x16, matrix products: 292 us -> 173 us  [the longest x5 66.2 us: mm(): return jnp.dot(a, b, preferred_element_type=F32)]
    convert_element_type x17 -> x5, other arithmetic: 68 us -> 6.63 us  [the longest x1 5.22 us: per_device(): normed_one = (residual * scale_one * attn_g).astype(BF16)]
    psum x1, blocking collectives: 13.8 us -> 57.9 us  [per_device(): lax.psum(jnp.concatenate([attn_gain_sum[0], mlp_gain_sum[0], sums]), 'fsdp')]
    all_gather x2 -> x1, blocking collectives: 19.3 us -> 62.2 us  [per_device(): lax.all_gather(jnp.stack([attn_gain, mlp_gain]), 'fsdp', axis=1, tiled=True)]
  transfers between devices with their start and end apart: 19 -> 8, of which waited for: 16 -> 1; matrix products, arithmetic and copies ran while one was open for 23% -> 13% of each run, Pallas kernels for 0% -> 40%
where the time goes in v1:
time: 969 us; the launch traced here: 967 us
  Pallas kernels  539 us (56%)
  matrix products  173 us (18%)
  blocking collectives  120 us (12%)
  other arithmetic  46.3 us (5%)
  local copies, waits for them, and re-layouts  36 us (4%)
  starting transfers between devices  33.9 us (3%)
  between operations  15.4 us (2%)
    pallas_call x4, Pallas kernels, line_call(): pl.pallas_call(functools.partial(kernel, n), in_specs=specs, out_specs=[V...  476 us
    dot_general x5, matrix products, mm(): return jnp.dot(a, b, preferred_element_type=F32)  66.2 us
    all_gather x1, blocking collectives, per_device(): lax.all_gather(jnp.stack([attn_gain, mlp_gain]), 'fsdp', axis=1, tiled=True)  62.2 us
    psum x1, blocking collectives, per_device(): lax.psum(jnp.concatenate([attn_gain_sum[0], mlp_gain_sum[0], sums]), 'fsdp')  57.9 us
    dot_general x7, matrix products, mm_tn(): return lax.dot_general(a, b, TN, preferred_element_type=F32)  56.1 us
    dot_general x4, matrix products, mm_nt(): return lax.dot_general(a, b, NT, preferred_element_type=F32)  50.2 us
    pallas_call x1, Pallas kernels, attend_back(): pl.pallas_call(attend_back_kernel, grid_spec=pltpu.PrefetchScalarGridSpec...  34.6 us
    all_to_all x4, starting transfers between devices, swap(): lax.all_to_all(values, 'fsdp', split_axis=0, concat_axis=0, tiled=True)  33.3 us
  transfers between devices with their start and end apart: 8, of which 1 were waited for; matrix products, arithmetic and copies ran while one was open for 13% of the time, Pallas kernels for 40%

profile of v1, /device:TPU:0, one launch (start us, length us, event | category | flops | bytes accessed | tf_op | source)
XLA Modules:
  0.0 967.1 jit_solution(9462428345553991655)
XLA Ops:
  14.7 5.3 all-to-all-start
  24.0 62.2 %all_gather.9 = bf16[2,2048]{1,0:T(2,128)(2,1)S(1)} all-gather(bf16[2,256]{1,0:T(2,128)(2,1)S(1)} %pad_maximum_fusion.6), channel_id=1, replica_groups=mesh['fsdp'=8,'dp'=4] {'fsdp'}, dimensions={1}, use_global_device_ids=true | all-gather | bytes 9216 | tf_op jit(solution)/shard_map/all_gather | solution.py:978
  91.1 4.5 all-to-all-start.2
  99.3 5.2 multiply_convert_fusion.1
  104.6 4.0 all-gather.3.cloned.1.call-done.out_weight
  108.6 11.7 %fusion.18.q_in.k_in.v_in = f32[1024,1536]{1,0:T(8,128)} fusion(bf16[1024,2048]{1,0:T(8,128)(2,1)} %multiply_convert_fusion.1, bf16[2048,2048]{1,0:T(8,128)(2,1)} %all-gather.3.cloned.1.call-done.out_weight), kind=kOutput, calls=%fused_computation.30 | convolution fusion | flops 6442450944 | bytes 16777216 | tf_op jit(solution)/shard_map/dot_general | solution.py:378
  120.3 28.2 %attend.1 = (bf16[1024,512]{1,0:T(8,128)(2,1)}, bf16[1024,512]{1,0:T(8,128)(2,1)}, bf16[1024,512]{1,0:T(8,128)(2,1)}, bf16[1024,512]{1,0:T(8,128)(2,1)}, f32[4,8,1024]{2,1,0:T(8,128)}) custom-call(s32[4]{0:T(128)} %broadcast_add_fusion.image_ref, f32[1024,1536]{1,0:T(8,128)} %fusion.18.q_in.k_in.v_in, f32[1024,1536]{1,0:T(8,128)} %fusion.18.q_in.k_in.v_in, ...), custom_call_target="tpu_custom_call" | custom-call | flops 12000000000 | bytes 12000000 | tf_op jit(solution)/shard_map/attend/pallas_call | solution.py:487
  148.5 118.7 %middle_sum.1 = (f32[1024,2048]{1,0:T(8,128)}, bf16[1024,2048]{1,0:T(8,128)(2,1)}, f32[8,2048]{1,0:T(8,128)}) custom-call(bf16[1024,512]{1,0:T(8,128)(2,1)} %get-tuple-element.32.mixed_ref, bf16[2048,2048]{1,0:T(8,128)(2,1)} %all-gather.3.cloned.1.call-done.out_weight, bf16[1024,2048]{1,0:T(8,128)(2,1)} %bitcast.source.source_ref, ...), custom_call_target="tpu_custom_call" | custom-call | flops 1000000000 | bytes 200000000 | tf_op jit(solution)/shard_map/middle_sum/pallas_call | solution.py:764
  267.2 14.7 %fusion.4 = f32[2048,1024]{0,1:T(8,128)} fusion(bf16[1024,2048]{1,0:T(8,128)(2,1)} %bitcast.8.cotangent, bf16[2048,6144]{0,1:T(8,128)(2,1)} %all-gather.5.cloned.1.call-done), kind=kOutput, calls=%fused_computation.16 | convolution fusion | flops 8589934592 | bytes 20971520 | tf_op jit(solution)/shard_map/dot_general | solution.py:378
  281.9 13.2 %fusion.14 = f32[1024,2048]{1,0:T(8,128)} fusion(bf16[1024,2048]{1,0:T(8,128)(2,1)S(1)} %copy-done.10, bf16[2048,6144]{0,1:T(8,128)(2,1)} %all-gather.5.cloned.1.call-done), kind=kOutput, calls=%fused_computation.26 | convolution fusion | flops 8589934592 | bytes 20971520 | tf_op jit(solution)/shard_map/dot_general | solution.py:378
  295.1 21.7 %fusion.1 = (bf16[1024,2048]{1,0:T(8,128)(2,1)}, bf16[1024,2048]{1,0:T(8,128)(2,1)}, bf16[1024,2048]{1,0:T(8,128)(2,1)}) fusion(f32[2048,1024]{0,1:T(8,128)} %fusion.4, f32[1024,2048]{1,0:T(8,128)} %fusion.14, bf16[1024,2048]{1,0:T(8,128)(2,1)} %get-tuple-element.33, bf16[2048,6144]{0,1:T(8,128)(2,1)} %all-gather.5.cloned.1.call-done), kind=kOutput, calls=%fused_computation.5 | convolution fusion | flops 8621391872 | bytes 41943040 | tf_op jit(solution)/shard_map/dot_general | solution.py:378
  316.9 12.6 %fusion.8 = f32[1024,2048]{1,0:T(8,128)S(1)} fusion(bf16[1024,2048]{1,0:T(8,128)(2,1)} %get-tuple-element.97, bf16[2048,6144]{0,1:T(8,128)(2,1)} %all-gather.5.cloned.1.call-done), kind=kOutput, calls=%fused_computation.20 | convolution fusion | flops 8589934592 | bytes 20971520 | tf_op jit(solution)/shard_map/dot_general | solution.py:382
  329.5 12.7 %add_convert_fusion.own = bf16[1024,2048]{1,0:T(8,128)(2,1)} fusion(f32[1024,2048]{1,0:T(8,128)S(1)} %fusion.8, bf16[1024,2048]{1,0:T(8,128)(2,1)S(1)} %copy-done.20, bf16[2048,6144]{0,1:T(8,128)(2,1)} %all-gather.5.cloned.1.call-done), kind=kOutput, calls=%fused_computation.9 | convolution fusion | flops 8594128896 | bytes 25165824 | tf_op jit(solution)/shard_map/dot_general | solution.py:382
  342.2 121.4 %middle_back_sum.1 = (f32[1024,2048]{1,0:T(8,128)}, bf16[1024,2048]{1,0:T(8,128)(2,1)}, f32[8,2048]{1,0:T(8,128)}) custom-call(bf16[1024,2048]{1,0:T(8,128)(2,1)} %add_convert_fusion.own, bf16[1024,2048]{1,0:T(8,128)(2,1)} %bitcast.8.cotangent, f32[1024,2048]{1,0:T(8,128)} %get-tuple-element.34.middle_ref, f32[1,2048]{1,0:T(1,128)} %get-tuple-element.106.gain), custom_call_target="tpu_custom_call" | custom-call | flops 1000000000 | bytes 200000000 | tf_op jit(solution)/shard_map/middle_back_sum/pallas_call | solution.py:764
  463.6 6.3 convolution_convert_fusion.2
  469.9 4.9 fusion.36.g_ref
  474.8 34.6 %attend_back.1 = (bf16[1024,512]{1,0:T(8,128)(2,1)}, bf16[1024,512]{1,0:T(8,128)(2,1)}, bf16[1024,512]{1,0:T(8,128)(2,1)}) custom-call(s32[4]{0:T(128)} %broadcast_add_fusion.image_ref, bf16[1024,512]{1,0:T(8,128)(2,1)} %get-tuple-element.36.q_ref, bf16[1024,512]{1,0:T(8,128)(2,1)} %get-tuple-element.37.k_ref, bf16[1024,512]{1,0:T(8,128)(2,1)} %get-tuple-element.38.v_ref, ...), custom_call_target="tpu_custom_call" | custom-call | flops 30000001024 | bytes 12000000 | tf_op jit(solution)/shard_map/attend_back/pallas_call | solution.py:595
  509.4 5.0 convolution_convert_fusion.3
  519.5 3.9 pad_maximum_fusion.1
  523.6 14.5 %convolution_convert_fusion = bf16[2048,2048]{0,1:T(8,128)(2,1)} fusion(bf16[1024,2048]{1,0:T(8,128)(2,1)} %get-tuple-element.33, bf16[1024,2048]{1,0:T(8,128)(2,1)} %get-tuple-element.97), kind=kOutput, calls=%fused_computation.14 | convolution fusion | flops 8594128896 | bytes 16777216 | tf_op jit(solution)/shard_map/dot_general | solution.py:386
  538.1 11.4 %convolution_convert_fusion.1 = bf16[2048,2048]{0,1:T(8,128)(2,1)} fusion(bf16[1024,2048]{1,0:T(8,128)(2,1)S(1)} %copy-done.11, bf16[1024,2048]{1,0:T(8,128)(2,1)S(1)} %copy-done.21), kind=kOutput, calls=%fused_computation.15 | convolution fusion | flops 8594128896 | bytes 16777216 | tf_op jit(solution)/shard_map/dot_general | solution.py:386
  549.5 13.8 %convert_bitcast_fusion = bf16[2048,2048]{0,1:T(8,128)(2,1)} fusion(bf16[1024,2048]{1,0:T(8,128)(2,1)S(1)} %copy-done.22, bf16[1024,2048]{1,0:T(8,128)(2,1)} %bitcast.8.cotangent), kind=kOutput, calls=%fused_computation.8 | convolution fusion | flops 8594128896 | bytes 16777216 | tf_op jit(solution)/shard_map/dot_general | solution.py:386
  563.3 18.7 %pad_maximum_fusion = bf16[2048,6144]{0,1:T(8,128)(2,1)} fusion(bf16[2048,2048]{0,1:T(8,128)(2,1)} %convert_bitcast_fusion, bf16[2048,2048]{0,1:T(8,128)(2,1)} %convolution_convert_fusion, bf16[2048,2048]{0,1:T(8,128)(2,1)} %convolution_convert_fusion.1), kind=kLoop, calls=%fused_computation | loop fusion | flops 75497472 | bytes 50331648 | tf_op jit(solution)/shard_map/concatenate | solution.py:1024
  582.1 13.9 %fusion.26.own = bf16[1024,2048]{1,0:T(8,128)(2,1)} fusion(bf16[1024,2048]{1,0:T(8,128)(2,1)} %get-tuple-element.98, bf16[2048,6144]{0,1:T(8,128)(2,1)} %all-gather.5.cloned.1.call-done), kind=kOutput, calls=%fused_computation.34 | convolution fusion | flops 8592031744 | bytes 16777216 | tf_op jit(solution)/shard_map/dot_general | solution.py:382
  596.0 114.9 %output_sum.1 = (bf16[1024,2048]{1,0:T(8,128)(2,1)}, f32[8,2048]{1,0:T(8,128)}) custom-call(bf16[1024,2048]{1,0:T(8,128)(2,1)} %fusion.26.own, f32[1024,2048]{1,0:T(8,128)} %get-tuple-element.34.middle_ref, f32[1024,1]{1,0:T(8,128)} %copy.52.valid), custom_call_target="tpu_custom_call" | custom-call | flops 1000000000 | bytes 200000000 | tf_op jit(solution)/shard_map/output_sum/pallas_call | solution.py:764
  710.9 18.8 %all-to-all-start.1 = ((bf16[8,128,2048]{2,1,0:T(8,128)(2,1)}), bf16[8,128,2048]{2,1,0:T(8,128)(2,1)}, u32[]{:S(2)}, u32[]{:S(2)}) async-start(bf16[8,128,2048]{2,1,0:T(8,128)(2,1)} %bitcast.62), calls=%async_computation.1 | async-start | bytes 8388608 | tf_op jit(solution)/shard_map/all_to_all | solution.py:970
  729.7 11.0 %fusion.23.own = bf16[1024,2048]{1,0:T(8,128)(2,1)} fusion(bf16[2048,2048]{1,0:T(8,128)(2,1)} %all-gather.3.cloned.1.call-done.out_weight, bf16[1024,512]{1,0:T(8,128)(2,1)S(1)} %copy-done.19, bf16[1024,512]{1,0:T(8,128)(2,1)S(1)} %copy-done.18, bf16[1024,512]{1,0:T(8,128)(2,1)S(1)} %copy-done.16), kind=kOutput, calls=%fused_computation.33 | convolution fusion | flops 6453985280 | bytes 13631488 | tf_op jit(solution)/shard_map/dot_general | solution.py:382
  740.7 121.0 %input_sum.1 = (bf16[1024,2048]{1,0:T(8,128)(2,1)}, f32[8,2048]{1,0:T(8,128)}) custom-call(bf16[1024,2048]{1,0:T(8,128)(2,1)} %fusion.23.own, bf16[1024,2048]{1,0:T(8,128)(2,1)} %bitcast.source.source_ref, f32[1024,2048]{1,0:T(8,128)} %get-tuple-element.44.back_ref, f32[1,2048]{1,0:T(1,128)} %copy-done.6), custom_call_target="tpu_custom_call" | custom-call | flops 1000000000 | bytes 200000000 | tf_op jit(solution)/shard_map/input_sum/pallas_call | solution.py:764
  861.7 4.6 all-to-all-start.3
  874.3 57.9 %psum.7 = f32[4099]{0:T(1024)S(1)} all-reduce(f32[4099]{0:T(1024)S(1)} %concatenate.36), channel_id=1, replica_groups=mesh['fsdp'=8,'dp'=4] {'fsdp'}, use_global_device_ids=true, to_apply=%region_6.7 | all-reduce | flops 4099 | bytes 32792 | tf_op jit(solution)/shard_map/psum | solution.py:1061
  950.5 4.8 copy.66
  955.3 4.8 copy.67
  (108 shorter events, 50.7 us)
Async XLA Ops:
  7.2 3.6 copy-start.4
  7.2 4.1 copy-start.5
  7.2 101.4 %all-gather.3.cloned.1.call-start = ((), (), s32[]{:S(2)}) async-start(), calls=%async_computation.6 | async-start | bytes 9437184 | tf_op jit(solution)/shard_map/all_gather | solution.py:972
  10.7 256.5 %all-gather.5.cloned.1.call-start = ((), (), s32[]{:S(2)}) async-start(), calls=%async_computation.7 | async-start | bytes 28311552 | tf_op jit(solution)/shard_map/all_gather | solution.py:980
  14.7 5.4 copy-start.13
  14.7 5.4 copy-start.14
  14.7 9.0 copy-start.8
  14.7 9.0 copy-start.9
  14.7 76.4 %all-to-all-start = ((bf16[8,128,2048]{2,1,0:T(8,128)(2,1)}), bf16[8,128,2048]{2,1,0:T(8,128)(2,1)}, u32[]{:S(2)}, u32[]{:S(2)}) async-start(bf16[8,128,2048]{2,1,0:T(8,128)(2,1)} %param.14), calls=%async_computation | async-start | bytes 8388608 | tf_op jit(solution)/shard_map/all_to_all | solution.py:970
  91.1 8.2 copy-start.6
  91.1 176.1 %all-to-all-start.2 = ((bf16[8,128,2048]{2,1,0:T(8,128)(2,1)}), bf16[8,128,2048]{2,1,0:T(8,128)(2,1)}, u32[]{:S(2)}, u32[]{:S(2)}) async-start(bf16[8,128,2048]{2,1,0:T(8,128)(2,1)} %param.15), calls=%async_computation.2 | async-start | bytes 8388608 | tf_op jit(solution)/shard_map/all_to_all | solution.py:970
  95.7 837.8 %reduce-scatter.3.cloned.1.call-start = ((), (), s32[]{:S(2)}) async-start(), calls=%async_computation.8 | async-start | bytes 9437184 | tf_op jit(solution)/shard_map/reduce_scatter | solution.py:1046
  267.2 14.7 %copy-start.10 = (bf16[1024,2048]{1,0:T(8,128)(2,1)S(1)}, bf16[1024,2048]{1,0:T(8,128)(2,1)}, u32[]{:S(2)}) copy-start(bf16[1024,2048]{1,0:T(8,128)(2,1)} %get-tuple-element.33) | copy-start | bytes 12582916
  316.9 12.6 %copy-start.20 = (bf16[1024,2048]{1,0:T(8,128)(2,1)S(1)}, bf16[1024,2048]{1,0:T(8,128)(2,1)}, u32[]{:S(2)}) copy-start(bf16[1024,2048]{1,0:T(8,128)(2,1)} %get-tuple-element.96) | copy-start | bytes 12582916
  463.6 6.4 copy-start.12
  509.4 5.1 copy-start.2
  509.4 5.0 copy-start.17
  514.5 2.5 copy-start.15
  517.0 2.5 copy-start.3
  523.5 415.2 %reduce-scatter.5.cloned.1.call-start = ((), (), s32[]{:S(2)}) async-start(), calls=%async_computation.9 | async-start | bytes 28311552 | tf_op jit(solution)/shard_map/reduce_scatter | solution.py:1023
  523.6 14.6 %copy-start.11 = (bf16[1024,2048]{1,0:T(8,128)(2,1)S(1)}, bf16[1024,2048]{1,0:T(8,128)(2,1)}, u32[]{:S(2)}) copy-start(bf16[1024,2048]{1,0:T(8,128)(2,1)} %get-tuple-element.33) | copy-start | bytes 12582916
  523.6 14.6 %copy-start.21 = (bf16[1024,2048]{1,0:T(8,128)(2,1)S(1)}, bf16[1024,2048]{1,0:T(8,128)(2,1)}, u32[]{:S(2)}) copy-start(bf16[1024,2048]{1,0:T(8,128)(2,1)} %get-tuple-element.96) | copy-start | bytes 12582916
  538.1 11.4 %copy-start.22 = (bf16[1024,2048]{1,0:T(8,128)(2,1)S(1)}, bf16[1024,2048]{1,0:T(8,128)(2,1)}, u32[]{:S(2)}) copy-start(bf16[1024,2048]{1,0:T(8,128)(2,1)} %get-tuple-element.98) | copy-start | bytes 12582916
  710.8 18.8 %copy-start.16 = (bf16[1024,512]{1,0:T(8,128)(2,1)S(1)}, bf16[1024,512]{1,0:T(8,128)(2,1)}, u32[]{:S(2)}) copy-start(bf16[1024,512]{1,0:T(8,128)(2,1)} %get-tuple-element.41) | copy-start | bytes 3145732
  710.9 18.8 %copy-start.18 = (bf16[1024,512]{1,0:T(8,128)(2,1)S(1)}, bf16[1024,512]{1,0:T(8,128)(2,1)}, u32[]{:S(2)}) copy-start(bf16[1024,512]{1,0:T(8,128)(2,1)} %get-tuple-element.42) | copy-start | bytes 3145732
  710.9 18.8 %copy-start.19 = (bf16[1024,512]{1,0:T(8,128)(2,1)S(1)}, bf16[1024,512]{1,0:T(8,128)(2,1)}, u32[]{:S(2)}) copy-start(bf16[1024,512]{1,0:T(8,128)(2,1)} %get-tuple-element.43) | copy-start | bytes 3145732
  710.9 150.8 %all-to-all-start.1 = ((bf16[8,128,2048]{2,1,0:T(8,128)(2,1)}), bf16[8,128,2048]{2,1,0:T(8,128)(2,1)}, u32[]{:S(2)}, u32[]{:S(2)}) async-start(bf16[8,128,2048]{2,1,0:T(8,128)(2,1)} %bitcast.62), calls=%async_computation.1 | async-start | bytes 8388608 | tf_op jit(solution)/shard_map/all_to_all | solution.py:970
  861.7 4.6 copy-start.7
  861.7 71.7 %all-to-all-start.3 = ((bf16[8,128,2048]{2,1,0:T(8,128)(2,1)}), bf16[8,128,2048]{2,1,0:T(8,128)(2,1)}, u32[]{:S(2)}, u32[]{:S(2)}) async-start(bf16[8,128,2048]{2,1,0:T(8,128)(2,1)} %bitcast.61), calls=%async_computation.3 | async-start | bytes 8388608 | tf_op jit(solution)/shard_map/all_to_all | solution.py:970
  933.4 4.3 copy-start.1
  942.6 5.9 copy-start
Sparse Core Ops, SparseCore 0:
  10.8 97.7 all-gather.2
  111.0 153.5 all-gather.4
  523.6 82.4 reduce-scatter.2
  609.6 189.6 reduce-scatter.4

commit v2 on v1

--- a/solution.py
+++ b/solution.py
@@ -367,7 +367,8 @@
 F32 = jnp.float32
 PAIR = 2 * HD
 TILE = 256
-STRIP = 64
+STRIP = 32
+SLAB = 512
 HOP = 2
 
 NT = (((1,), (1,)), ((), ()))
@@ -620,34 +621,61 @@
     )(image, queries, keys, values, grads, mixed, lse, cosine, sine, bias)
 
 
-def line_sum(n, own, flows, make, finish):
-    from_low, from_high, to_high, to_low, sems = flows
+VM = pl.BlockSpec(memory_space=pltpu.VMEM)
+ANY = pl.BlockSpec(memory_space=pl.ANY)
+
+
+def row_mean(values):
+    return jnp.mean(values, axis=1, keepdims=True)
+
+
+def col_sum(values):
+    return jnp.sum(values, axis=0, keepdims=True)
+
+
+def greet(n, peers=0):
+    rank = lax.axis_index("dp")
+    has_low, has_high = rank > 0, rank < n - 1
+    barrier = pltpu.get_barrier_semaphore()
+
+    @pl.when(has_low)
+    def _():
+        pl.semaphore_signal(
+            barrier, inc=1, device_id={"dp": lax.rem(rank + n - 1, n)}, device_id_type=MESH
+        )
+
+    @pl.when(has_high)
+    def _():
+        pl.semaphore_signal(
+            barrier, inc=1, device_id={"dp": lax.rem(rank + 1, n)}, device_id_type=MESH
+        )
+
+    mine = lax.axis_index("fsdp")
+    for ahead in range(1, peers):
+        pl.semaphore_signal(
+            barrier, inc=1, device_id={"fsdp": lax.rem(mine + ahead, peers)}, device_id_type=MESH
+        )
+    both = has_low.astype(jnp.int32) + has_high.astype(jnp.int32)
+    pl.semaphore_wait(barrier, both + max(peers - 1, 0))
+
+
+def line_sum(n, own, flows, work, finish, shift=0):
+    prefix, suffix, sems = flows
     send_high, send_low, got_low, got_high = (sems.at[k] for k in range(4))
     rank = lax.axis_index("dp")
     strips = own.shape[0] // STRIP
     has_low, has_high = rank > 0, rank < n - 1
     higher, lower = lax.rem(rank + 1, n), lax.rem(rank + n - 1, n)
 
-    barrier = pltpu.get_barrier_semaphore()
-
-    @pl.when(has_low)
-    def _():
-        pl.semaphore_signal(barrier, inc=1, device_id={"dp": lower}, device_id_type=MESH)
-
-    @pl.when(has_high)
-    def _():
-        pl.semaphore_signal(barrier, inc=1, device_id={"dp": higher}, device_id_type=MESH)
-
-    pl.semaphore_wait(barrier, has_low.astype(jnp.int32) + has_high.astype(jnp.int32))
-
     def rows_of(strip):
-        return pl.ds(pl.multiple_of(strip * STRIP, STRIP), STRIP)
+        at = strip if isinstance(shift, int) else lax.rem(strip + shift, strips)
+        return pl.ds(pl.multiple_of(at * STRIP, STRIP), STRIP)
 
     def up(strip):
         rows = rows_of(strip)
         return pltpu.make_async_remote_copy(
-            src_ref=to_high.at[rows],
-            dst_ref=from_low.at[rows],
+            src_ref=prefix.at[rows],
+            dst_ref=prefix.at[rows],
             send_sem=send_high.at[strip],
             recv_sem=got_low.at[strip],
             device_id={"dp": higher},
@@ -657,59 +685,58 @@
     def down(strip):
         rows = rows_of(strip)
         return pltpu.make_async_remote_copy(
-            src_ref=to_low.at[rows],
-            dst_ref=from_high.at[rows],
+            src_ref=suffix.at[rows],
+            dst_ref=suffix.at[rows],
             send_sem=send_low.at[strip],
             recv_sem=got_high.at[strip],
             device_id={"dp": lower},
             device_id_type=MESH,
         )
 
-    @pl.when(jnp.logical_not(has_low))
-    def _():
-        from_low[...] = jnp.zeros_like(from_low)
-
-    @pl.when(jnp.logical_not(has_high))
-    def _():
-        from_high[...] = jnp.zeros_like(from_high)
-
     late = jnp.maximum(rank, n - 1 - rank)
 
     def step(s, carry):
-        @pl.when(s < strips)
-        def _():
-            make(s, rows_of(s))
-
+        work(s)
         a = s - rank * HOP
 
         @pl.when((a >= 0) & (a < strips))
         def _():
+            rows = rows_of(a)
+
             @pl.when(has_low)
             def _():
                 up(a).wait_recv()
+                prefix[rows, :] = (
+                    own[rows, :].astype(F32) + prefix[rows, :].astype(F32)
+                ).astype(BF16)
+
+            @pl.when(jnp.logical_not(has_low))
+            def _():
+                prefix[rows, :] = own[rows, :]
 
             @pl.when(has_high)
             def _():
-                rows = rows_of(a)
-                to_high[rows, :] = (
-                    own[rows, :].astype(F32) + from_low[rows, :].astype(F32)
-                ).astype(BF16)
                 up(a).start()
 
         b = s - (n - 1 - rank) * HOP
 
         @pl.when((b >= 0) & (b < strips))
         def _():
+            rows = rows_of(b)
+
             @pl.when(has_high)
             def _():
                 down(b).wait_recv()
+                suffix[rows, :] = (
+                    own[rows, :].astype(F32) + suffix[rows, :].astype(F32)
+                ).astype(BF16)
+
+            @pl.when(jnp.logical_not(has_high))
+            def _():
+                suffix[rows, :] = own[rows, :]
 
             @pl.when(has_low)
             def _():
-                rows = rows_of(b)
-                to_low[rows, :] = (
-                    own[rows, :].astype(F32) + from_high[rows, :].astype(F32)
-                ).astype(BF16)
                 down(b).start()
 
         c = s - late * HOP
@@ -720,9 +747,9 @@
             finish(
                 c,
                 rows,
-                own[rows, :].astype(F32)
-                + from_low[rows, :].astype(F32)
-                + from_high[rows, :].astype(F32),
+                prefix[rows, :].astype(F32)
+                + suffix[rows, :].astype(F32)
+                - own[rows, :].astype(F32),
             )
 
         return carry
@@ -745,203 +772,675 @@
 
 def flow_scratch(length, width):
     whole = pltpu.VMEM((length, width), BF16)
-    return [whole] * 4 + [pltpu.SemaphoreType.DMA((4, length // STRIP))]
-
-
-VM = pl.BlockSpec(memory_space=pltpu.VMEM)
-ANY = pl.BlockSpec(memory_space=pl.ANY)
-
-
-def row_mean(values):
-    return jnp.mean(values, axis=1, keepdims=True)
-
-
-def col_sum(values):
-    return jnp.sum(values, axis=0, keepdims=True)
-
-
-def line_call(kernel, n, name, collective_id, args, out_shape, scratch, specs, flops=10**9):
+    return [whole] * 2 + [pltpu.SemaphoreType.DMA((4, length // STRIP))]
+
+
+def line_call(kernel, n, name, collective_id, args, specs, outs, out_specs, scratch, flops):
     return pl.pallas_call(
         functools.partial(kernel, n),
         in_specs=specs,
-        out_specs=[VM] * len(out_shape),
-        out_shape=out_shape,
+        out_specs=out_specs,
+        out_shape=outs,
         scratch_shapes=scratch,
         compiler_params=pltpu.CompilerParams(
             collective_id=collective_id, has_side_effects=True, vmem_limit_bytes=VMEM_MOST
         ),
         cost_estimate=pl.CostEstimate(
-            flops=flops, bytes_accessed=200_000_000, transcendentals=0
+            flops=flops, bytes_accessed=300_000_000, transcendentals=0
         ),
         name=name,
     )(*args)
+
+
+def wide_rows(group):
+    return pl.ds(pl.multiple_of(group * TILE, TILE), TILE)
+
+
+def product_nt(own, rows, pairs):
+    width = own.shape[1]
+
+    def piece(p, carry):
+        cols = pl.ds(pl.multiple_of(p * SLAB, SLAB), SLAB)
+        total = None
+        for left, right in pairs:
+            term = mm_nt(left(rows), right(cols))
+            total = term if total is None else total + term
+        own[rows, cols] = total.astype(BF16)
+        return carry
+
+    lax.fori_loop(0, width // SLAB, piece, 0)
+
+
+def on_groups(s, length, make):
+    per = TILE // STRIP
+
+    @pl.when((lax.rem(s, per) == 0) & (s < length // STRIP))
+    def _():
+        make(lax.div(s, per))
 
 
 def middle_kernel(
     n,
     mixed_ref,
     out_weight,
-    source,
+    source_hbm,
     gain,
     valid,
     middle_ref,
     normed_ref,
     stats_ref,
+    weight,
+    source,
     own,
-    weight,
-    weight_sem,
+    load_sems,
     *flows,
 ):
     band = weight.shape[1]
-    load = pltpu.make_async_copy(
-        out_weight.at[:, pl.ds(out_weight.shape[1] - band, band)], weight, weight_sem
-    )
-    load.start()
+    length = own.shape[0]
+    loads = [
+        pltpu.make_async_copy(
+            out_weight.at[:, pl.ds(out_weight.shape[1] - band, band)], weight, load_sems.at[0]
+        ),
+        pltpu.make_async_copy(source_hbm, source, load_sems.at[1]),
+    ]
+    for load in loads:
+        load.start()
+    greet(n)
     stats_ref[...] = jnp.zeros_like(stats_ref)
-    load.wait()
-
-    def make(strip, rows):
-        own[rows, :] = mm_nt(mixed_ref[rows, :], weight[...]).astype(BF16)
+    for load in loads:
+        load.wait()
+
+    def make(group):
+        product_nt(
+            own,
+            wide_rows(group),
+            [(lambda rows: mixed_ref[rows, :], lambda cols: weight[cols, :])],
+        )
 
     def finish(strip, rows, total):
         middle = source[rows, :].astype(F32) + total
-        middle_ref[rows, :] = middle
+        middle_ref[rows, :] = middle.astype(BF16)
         square = middle * middle
         scale = lax.rsqrt(row_mean(square) + EPS)
         normed_ref[rows, :] = (middle * scale * gain[...]).astype(BF16)
         stats_ref[0:1, :] += col_sum(square * valid[rows, :])
         stats_ref[1:2, :] += col_sum(total * total * valid[rows, :])
 
-    line_sum(n, own, flows, make, finish)
+    line_sum(n, own, flows, lambda s: on_groups(s, length, make), finish)
 
 
 def middle_sum(n, mixed, gathered, source, gain, valid):
     length, width = source.shape
     band = mixed.shape[1]
+    rows = pltpu.VMEM((length, width), BF16)
     return line_call(
         middle_kernel,
         n,
         "middle_sum",
         1,
         (mixed, gathered, source, gain, valid),
+        [VM, ANY, ANY, VM, VM],
         [
-            jax.ShapeDtypeStruct((length, width), F32),
+            jax.ShapeDtypeStruct((length, width), BF16),
             jax.ShapeDtypeStruct((length, width), BF16),
             jax.ShapeDtypeStruct((8, width), F32),
         ],
+        [VM] * 3,
         [
-            pltpu.VMEM((length, width), BF16),
             pltpu.VMEM((width, band), BF16),
-            pltpu.SemaphoreType.DMA,
+            rows,
+            rows,
+            pltpu.SemaphoreType.DMA((2,)),
         ]
         + flow_scratch(length, width),
-        [VM, ANY, VM, VM, VM],
-    )
-
-
-def middle_back_kernel(n, own, cotangent, middle_ref, gain, back_ref, low_ref, gain_ref, *flows):
+        50_000_000_000,
+    )
+def mlp_kernel(
+    n,
+    normed_hbm,
+    upstream_hbm,
+    middle_hbm,
+    gain,
+    weight_hbm,
+    act_hbm,
+    gate_back_hbm,
+    up_back_hbm,
+    low_ref,
+    gain_ref,
+    weight,
+    normed,
+    upstream,
+    middle_in,
+    own,
+    acc,
+    stage,
+    load_sems,
+    weight_sems,
+    stage_sems,
+    *flows,
+):
+    width, feed = weight.shape[0], weight.shape[1] // 3
+    length = own.shape[0]
+    blocks = feed // SLAB
+    chunks = length // TILE
+    loads = [
+        pltpu.make_async_copy(normed_hbm, normed, load_sems.at[0]),
+        pltpu.make_async_copy(upstream_hbm, upstream, load_sems.at[1]),
+        pltpu.make_async_copy(middle_hbm, middle_in, load_sems.at[2]),
+    ]
+
+    def columns(kind, block):
+        return pl.ds(pl.multiple_of(kind * feed + block * SLAB, SLAB), SLAB)
+
+    def weight_load(kind, block):
+        return pltpu.make_async_copy(
+            weight_hbm.at[:, columns(kind, block)],
+            weight.at[:, columns(kind, block)],
+            weight_sems.at[kind, block],
+        )
+
+    loads[0].start()
+    for kind in range(3):
+        weight_load(kind, 0).start()
+    loads[1].start()
+    for block in range(1, blocks):
+        for kind in range(3):
+            weight_load(kind, block).start()
+    loads[2].start()
+    greet(n)
     gain_ref[...] = jnp.zeros_like(gain_ref)
-
-    def make(strip, rows):
-        pass
+    loads[0].wait()
+    loads[1].wait()
+    backs = (act_hbm, gate_back_hbm, up_back_hbm)
+
+    def store(kind, unit):
+        slot = lax.rem(unit, 2)
+        rows = pl.ds(pl.multiple_of(lax.div(unit, blocks) * TILE, TILE), TILE)
+        cols = pl.ds(pl.multiple_of(lax.rem(unit, blocks) * SLAB, SLAB), SLAB)
+        return pltpu.make_async_copy(
+            stage.at[slot, kind], backs[kind].at[rows, cols], stage_sems.at[slot, kind]
+        )
+
+    def unit_work(unit):
+        block = lax.rem(unit, blocks)
+        rows = pl.ds(pl.multiple_of(lax.div(unit, blocks) * TILE, TILE), TILE)
+        slot = lax.rem(unit, 2)
+
+        @pl.when(unit < blocks)
+        def _():
+            for kind in range(3):
+                weight_load(kind, block).wait()
+
+        @pl.when(unit >= 2)
+        def _():
+            for kind in range(3):
+                store(kind, unit - 2).wait()
+
+        here = normed[rows, :]
+        gate_w = weight[:, columns(0, block)]
+        up_w = weight[:, columns(1, block)]
+        gate = mm(here, gate_w)
+        up = mm(here, up_w)
+        act_grad = mm(upstream[rows, :], weight[:, columns(2, block)])
+        sig = jax.nn.sigmoid(gate)
+        gate_sig = gate * sig
+        stage[slot, 0] = (gate_sig * up).astype(BF16)
+        gate_back = (act_grad * up * (sig + gate_sig * (1.0 - sig))).astype(BF16)
+        up_back = (act_grad * gate_sig).astype(BF16)
+        stage[slot, 1] = gate_back
+        stage[slot, 2] = up_back
+        for kind in range(3):
+            store(kind, unit).start()
+        part = mm_nt(gate_back, gate_w) + mm_nt(up_back, up_w)
+
+        @pl.when(block == 0)
+        def _():
+            acc[...] = part
+
+        @pl.when(block > 0)
+        def _():
+            acc[...] += part
+
+        @pl.when(block == blocks - 1)
+        def _():
+            own[rows, :] = acc[...].astype(BF16)
+
+    units = chunks * blocks
+
+    def first(unit, carry):
+        unit_work(unit)
+        return carry
+
+    lax.fori_loop(0, blocks, first, 0)
+    loads[2].wait()
+    per = (length // STRIP) // chunks
+
+    def work(s):
+        for k in range(max(1, blocks // per)):
+            stride = max(1, per // blocks)
+            unit = blocks + (s * max(1, blocks // per) + k if per <= blocks else lax.div(s, stride))
+
+            @pl.when((unit < units) & (lax.rem(s, stride) == 0))
+            def _(unit=unit):
+                unit_work(unit)
 
     def finish(strip, rows, total):
-        middle = middle_ref[rows, :]
+        middle = middle_in[rows, :].astype(F32)
         scale = lax.rsqrt(row_mean(middle * middle) + EPS)
         scaled = total * gain[...]
         inner = row_mean(scaled * middle)
-        back = cotangent[rows, :].astype(F32) + scale * (scaled - middle * (scale * scale * inner))
-        back_ref[rows, :] = back
+        back = upstream[rows, :].astype(F32) + scale * (scaled - middle * (scale * scale * inner))
         low_ref[rows, :] = back.astype(BF16)
         gain_ref[0:1, :] += col_sum(total * middle * scale)
 
-    line_sum(n, own, flows, make, finish)
-
-
-def middle_back_sum(n, part, cotangent, middle, gain):
-    length, width = part.shape
+    line_sum(n, own, flows, work, finish)
+    for kind in range(3):
+        store(kind, units - 2).wait()
+        store(kind, units - 1).wait()
+
+
+def mlp_sum(n, normed, upstream, middle, gain, weights):
+    length, width = normed.shape
+    feed = weights.shape[1] // 3
+    rows = pltpu.VMEM((length, width), BF16)
+    low = jax.ShapeDtypeStruct((length, feed), BF16)
     return line_call(
-        middle_back_kernel,
+        mlp_kernel,
         n,
-        "middle_back_sum",
+        "mlp_sum",
         2,
-        (part, cotangent, middle, gain),
-        [
-            jax.ShapeDtypeStruct((length, width), F32),
+        (normed, upstream, middle, gain, weights),
+        [ANY, ANY, ANY, VM, ANY],
+        [low] * 3
+        + [
             jax.ShapeDtypeStruct((length, width), BF16),
             jax.ShapeDtypeStruct((8, width), F32),
         ],
-        flow_scratch(length, width),
-        [VM] * 4,
-    )
-
-
-def output_kernel(n, own, middle_ref, valid, out_ref, stats_ref, *flows):
+        [ANY] * 3 + [VM] * 2,
+        [
+            pltpu.VMEM((width, 3 * feed), BF16),
+            rows,
+            rows,
+            rows,
+            rows,
+            pltpu.VMEM((TILE, width), F32),
+            pltpu.VMEM((2, 3, TILE, SLAB), BF16),
+            pltpu.SemaphoreType.DMA((3,)),
+            pltpu.SemaphoreType.DMA((3, feed // SLAB)),
+            pltpu.SemaphoreType.DMA((2, 3)),
+        ]
+        + flow_scratch(length, width),
+        60_000_000_000,
+    )
+TURN = 128
+GRAD = 256
+
+
+def output_kernel(
+    n,
+    act_hbm,
+    weight_hbm,
+    middle_hbm,
+    normed_hbm,
+    upstream_hbm,
+    gate_back_hbm,
+    up_back_hbm,
+    valid,
+    out_ref,
+    stats_ref,
+    grads_hbm,
+    act,
+    down,
+    middle,
+    normed_t,
+    upstream_t,
+    gate_back,
+    up_back,
+    own,
+    slices,
+    stage,
+    load_sems,
+    slice_sems,
+    stage_sems,
+    *flows,
+):
+    length, width = own.shape
+    feed = act.shape[1]
+    loads = [
+        pltpu.make_async_copy(act_hbm, act, load_sems.at[0]),
+        pltpu.make_async_copy(weight_hbm.at[:, pl.ds(2 * feed, feed)], down, load_sems.at[1]),
+        pltpu.make_async_copy(middle_hbm, middle, load_sems.at[2]),
+        pltpu.make_async_copy(gate_back_hbm, gate_back, load_sems.at[3]),
+        pltpu.make_async_copy(up_back_hbm, up_back, load_sems.at[4]),
+    ]
+    turns = length // TURN
+
+    def slice_load(kind, turn):
+        rows = pl.ds(pl.multiple_of(turn * TURN, TURN), TURN)
+        slot = lax.rem(turn, 2)
+        return pltpu.make_async_copy(
+            (normed_hbm, upstream_hbm)[kind].at[rows],
+            slices.at[slot, kind],
+            slice_sems.at[slot, kind],
+        )
+
+    loads[0].start()
+    loads[1].start()
+    for turn in range(2):
+        for kind in range(2):
+            slice_load(kind, turn).start()
+    for load in loads[2:]:
+        load.start()
+    greet(n)
     stats_ref[...] = jnp.zeros_like(stats_ref)
-
-    def make(strip, rows):
-        pass
+    loads[0].wait()
+    loads[1].wait()
+
+    def make(group):
+        product_nt(
+            own, wide_rows(group), [(lambda rows: act[rows, :], lambda cols: down[cols, :])]
+        )
+
+    blocks = feed // GRAD
+    units = 3 * blocks
+
+    def store(unit):
+        cols = pl.ds(pl.multiple_of(unit * GRAD, GRAD), GRAD)
+        slot = lax.rem(unit, 2)
+        return pltpu.make_async_copy(stage.at[slot], grads_hbm.at[:, cols], stage_sems.at[slot])
+
+    def grad_unit(unit):
+        slot = lax.rem(unit, 2)
+
+        @pl.when(unit >= 2)
+        def _():
+            store(unit - 2).wait()
+
+        cols = pl.ds(pl.multiple_of(lax.rem(unit, blocks) * GRAD, GRAD), GRAD)
+        for kind, (left, right) in enumerate(
+            ((normed_t, gate_back), (normed_t, up_back), (upstream_t, act))
+        ):
+
+            @pl.when(lax.div(unit, blocks) == kind)
+            def _(left=left, right=right):
+                def piece(p, carry):
+                    rows = pl.ds(pl.multiple_of(p * SLAB, SLAB), SLAB)
+                    stage[slot, rows, :] = mm(left[rows, :], right[:, cols]).astype(BF16)
+                    return carry
+
+                lax.fori_loop(0, width // SLAB, piece, 0)
+
+        store(unit).start()
+
+    def work(s):
+        on_groups(s, length, make)
+
+        @pl.when(s < turns)
+        def _():
+            slot = lax.rem(s, 2)
+            cols = pl.ds(pl.multiple_of(s * TURN, TURN), TURN)
+            for kind, turned in enumerate((normed_t, upstream_t)):
+                slice_load(kind, s).wait()
+                turned[:, cols] = slices[slot, kind].T
+
+                @pl.when(s + 2 < turns)
+                def _(kind=kind):
+                    slice_load(kind, s + 2).start()
+
+        @pl.when(s == turns)
+        def _():
+            loads[3].wait()
+            loads[4].wait()
+
+        @pl.when((s >= turns) & (s < turns + units))
+        def _():
+            grad_unit(s - turns)
+
+        @pl.when(s == 0)
+        def _():
+            loads[2].wait()
 
     def finish(strip, rows, total):
-        out_ref[rows, :] = (middle_ref[rows, :] + total).astype(BF16)
+        out_ref[rows, :] = (middle[rows, :].astype(F32) + total).astype(BF16)
         stats_ref[0:1, :] += col_sum(total * total * valid[rows, :])
 
-    line_sum(n, own, flows, make, finish)
-
-
-def output_sum(n, part, middle, valid):
-    length, width = part.shape
+    line_sum(n, own, flows, work, finish)
+    store(units - 2).wait()
+    store(units - 1).wait()
+
+
+def output_sum(n, act, weights, middle, normed, upstream, gate_back, up_back, valid):
+    length, width = middle.shape
+    feed = act.shape[1]
+    rows = pltpu.VMEM((length, width), BF16)
+    wide = pltpu.VMEM((length, feed), BF16)
+    turned = pltpu.VMEM((width, length), BF16)
     return line_call(
         output_kernel,
         n,
         "output_sum",
         3,
-        (part, middle, valid),
+        (act, weights, middle, normed, upstream, gate_back, up_back, valid),
+        [ANY] * 7 + [VM],
         [
             jax.ShapeDtypeStruct((length, width), BF16),
             jax.ShapeDtypeStruct((8, width), F32),
+            jax.ShapeDtypeStruct((width, 3 * feed), BF16),
         ],
-        flow_scratch(length, width),
-        [VM] * 3,
-    )
-
-
-def input_kernel(n, own, source_ref, back_ref, gain, grad_ref, gain_ref, *flows):
-    gain_ref[...] = jnp.zeros_like(gain_ref)
-
-    def make(strip, rows):
-        pass
+        [VM, VM, ANY],
+        [
+            wide,
+            pltpu.VMEM((width, feed), BF16),
+            rows,
+            turned,
+            turned,
+            wide,
+            wide,
+            rows,
+            pltpu.VMEM((2, 2, TURN, width), BF16),
+            pltpu.VMEM((2, width, GRAD), BF16),
+            pltpu.SemaphoreType.DMA((5,)),
+            pltpu.SemaphoreType.DMA((2, 2)),
+            pltpu.SemaphoreType.DMA((2,)),
+        ]
+        + flow_scratch(length, width),
+        60_000_000_000,
+    )
+
+
+def input_kernel(
+    n,
+    peers,
+    dq_ref,
+    dk_ref,
+    dv_ref,
+    weight_hbm,
+    source_hbm,
+    back_hbm,
+    gain,
+    rows_ref,
+    out_hbm,
+    small_ref,
+    weight,
+    source,
+    back,
+    own,
+    result,
+    small_own,
+    small_got,
+    load_sems,
+    send_sems,
+    recv_sems,
+    home_sem,
+    small_send,
+    small_recv,
+    *flows,
+):
+    length, width = own.shape
+    band = dq_ref.shape[1]
+    mine = lax.axis_index("fsdp")
+    local = length // peers
+    share = width // peers
+    strips = length // STRIP
+    per = local // STRIP
+    loads = [
+        pltpu.make_async_copy(weight_hbm.at[:, pl.ds(0, 3 * band)], weight, load_sems.at[0]),
+        pltpu.make_async_copy(source_hbm, source, load_sems.at[1]),
+        pltpu.make_async_copy(back_hbm, back, load_sems.at[2]),
+    ]
+    for load in loads:
+        load.start()
+    greet(n, peers)
+    small_own[...] = rows_ref[...]
+    small_own[0:1, :] = jnp.zeros((1, width), F32)
+    loads[0].wait()
+    halves = [
+        (lambda rows, ref=ref: ref[rows, :], lambda cols, k=k: weight[cols, k * band : (k + 1) * band])
+        for k, ref in enumerate((dq_ref, dk_ref, dv_ref))
+    ]
+    shift = mine * per
+
+    def make(group):
+        product_nt(own, wide_rows(group), halves)
+
+    def work(s):
+        full = TILE // STRIP
+        base = lax.rem(s + shift, strips)
+
+        @pl.when((s == 0) | ((lax.rem(base, full) == 0) & (s <= strips - full)))
+        def _():
+            make(lax.div(base, full))
+
+        @pl.when(s == 0)
+        def _():
+            loads[1].wait()
+            loads[2].wait()
+
+    def place(strip):
+        at = lax.rem(strip + shift, strips)
+        owner = lax.div(at, per)
+        inside = pl.ds(pl.multiple_of(lax.rem(at, per) * STRIP, STRIP), STRIP)
+        rows = pl.ds(pl.multiple_of(at * STRIP, STRIP), STRIP)
+        return owner, rows, inside
+
+    def away(strip):
+        owner, rows, inside = place(strip)
+        return pltpu.make_async_remote_copy(
+            src_ref=result.at[rows],
+            dst_ref=out_hbm.at[mine, inside],
+            send_sem=send_sems.at[strip],
+            recv_sem=recv_sems.at[mine],
+            device_id={"fsdp": owner},
+            device_id_type=MESH,
+        )
+
+    def home(strip):
+        owner, rows, inside = place(strip)
+        return pltpu.make_async_copy(
+            result.at[rows], out_hbm.at[mine, inside], home_sem.at[lax.rem(strip, per)]
+        )
 
     def finish(strip, rows, total):
-        source = source_ref[rows, :].astype(F32)
-        scale = lax.rsqrt(row_mean(source * source) + EPS)
+        here = source[rows, :].astype(F32)
+        scale = lax.rsqrt(row_mean(here * here) + EPS)
         scaled = total * gain[...]
-        inner = row_mean(scaled * source)
-        grad_ref[rows, :] = (
-            back_ref[rows, :] + scale * (scaled - source * (scale * scale * inner))
+        inner = row_mean(scaled * here)
+        result[rows, :] = (
+            back[rows, :].astype(F32) + scale * (scaled - here * (scale * scale * inner))
         ).astype(BF16)
-        gain_ref[0:1, :] += col_sum(total * source * scale)
-
-    line_sum(n, own, flows, make, finish)
-
-
-def input_sum(n, part, source, back, gain):
-    length, width = part.shape
+        small_own[0:1, :] += col_sum(total * here * scale)
+
+        @pl.when(strip < per)
+        def _():
+            home(strip).start()
+
+        @pl.when(strip >= per)
+        def _():
+            away(strip).start()
+
+    line_sum(n, own, flows, work, finish, shift)
+
+    def small(ahead):
+        peer = lax.rem(mine + ahead, peers)
+        cols = pl.ds(pl.multiple_of(peer * share, share), share)
+        return pltpu.make_async_remote_copy(
+            src_ref=small_own.at[:, cols],
+            dst_ref=small_got.at[mine],
+            send_sem=small_send.at[ahead],
+            recv_sem=small_recv.at[mine],
+            device_id={"fsdp": peer},
+            device_id_type=MESH,
+        )
+
+    for ahead in range(1, peers):
+        small(ahead).start()
+    for strip in range(per):
+        home(strip).wait()
+
+    def drain(strip, carry):
+        away(strip).wait_send()
+        return carry
+
+    lax.fori_loop(per, strips, drain, 0)
+    total = small_own[:, pl.ds(pl.multiple_of(mine * share, share), share)]
+    for ahead in range(1, peers):
+        peer = lax.rem(mine + ahead, peers)
+        pltpu.make_async_remote_copy(
+            src_ref=small_own.at[:, pl.ds(0, share)],
+            dst_ref=small_got.at[peer],
+            send_sem=small_send.at[ahead],
+            recv_sem=small_recv.at[peer],
+            device_id={"fsdp": peer},
+            device_id_type=MESH,
+        ).wait_recv()
+        total = total + small_got[peer]
+        small(ahead).wait_send()
+        pltpu.make_async_remote_copy(
+            src_ref=result.at[pl.ds(0, local)],
+            dst_ref=out_hbm.at[peer],
+            send_sem=send_sems.at[0],
+            recv_sem=recv_sems.at[peer],
+            device_id={"fsdp": peer},
+            device_id_type=MESH,
+        ).wait_recv()
+    small_ref[...] = total
+
+
+def input_sum(n, peers, dq, dk, dv, weights, source, back, gain, small_rows):
+    length, width = source.shape
+    band = dq.shape[1]
+    rows = pltpu.VMEM((length, width), BF16)
+    share = width // peers
     return line_call(
-        input_kernel,
+        lambda count, *refs: input_kernel(count, peers, *refs),
         n,
         "input_sum",
         4,
-        (part, source, back, gain),
+        (dq, dk, dv, weights, source, back, gain, small_rows),
+        [VM, VM, VM, ANY, ANY, ANY, VM, VM],
         [
-            jax.ShapeDtypeStruct((length, width), BF16),
-            jax.ShapeDtypeStruct((8, width), F32),
+            jax.ShapeDtypeStruct((peers, length // peers, width), BF16),
+            jax.ShapeDtypeStruct((8, share), F32),
         ],
-        flow_scratch(length, width),
-        [VM] * 4,
-    )
-
-
+        [ANY, VM],
+        [
+            pltpu.VMEM((width, 3 * band), BF16),
+            rows,
+            rows,
+            rows,
+            rows,
+            pltpu.VMEM((8, width), F32),
+            pltpu.VMEM((peers, 8, share), F32),
+            pltpu.SemaphoreType.DMA((3,)),
+            pltpu.SemaphoreType.DMA((length // STRIP,)),
+            pltpu.SemaphoreType.DMA((peers,)),
+            pltpu.SemaphoreType.DMA((length // peers // STRIP,)),
+            pltpu.SemaphoreType.DMA((peers,)),
+            pltpu.SemaphoreType.DMA((peers,)),
+        ]
+        + flow_scratch(length, width),
+        50_000_000_000,
+    )
 def per_device(
     mesh_sizes,
     inputs,
@@ -969,14 +1468,16 @@
     def swap(values):
         return lax.all_to_all(values, "fsdp", split_axis=0, concat_axis=0, tiled=True)
 
+    gains = lax.all_gather(jnp.stack([attn_gain, mlp_gain]), "fsdp", axis=1, tiled=True)
+    gains, inputs = lax.optimization_barrier((gains, inputs))
+    gains = gains.astype(F32)
+    attn_g, mlp_g = gains[0:1], gains[1:2]
     attn_w = lax.all_gather(
         jnp.concatenate([query_weight, key_weight, value_weight, output_weight.T], axis=1),
         "fsdp",
         axis=0,
         tiled=True,
     )
-    gains = lax.all_gather(jnp.stack([attn_gain, mlp_gain]), "fsdp", axis=1, tiled=True).astype(F32)
-    attn_g, mlp_g = gains[0:1], gains[1:2]
     mlp_w = lax.all_gather(
         jnp.concatenate([gate_weight, up_weight, down_weight.T], axis=1),
         "fsdp",
@@ -984,6 +1485,7 @@
         tiled=True,
     )
     source = swap(inputs).reshape(length, width)
+    source, cotangent = lax.optimization_barrier((source, cotangent))
     upstream = swap(cotangent).reshape(length, width)
 
     places = jnp.arange(length, dtype=jnp.int32)
@@ -1006,66 +1508,43 @@
     qkv = mm(normed_one, attn_w[:, : 3 * band])
     queries, keys, values, mixed, lse = attend(qkv, cosine, sine, bias, image)
     middle, normed_two, stats = middle_sum(line, mixed, attn_w, source, mlp_g, valid)
-
-    gate = mm(normed_two, mlp_w[:, :feed])
-    up = mm(normed_two, mlp_w[:, feed : 2 * feed])
-    sig = jax.nn.sigmoid(gate)
-    activated = (gate * sig * up).astype(BF16)
-    act_grad = mm(upstream, mlp_w[:, 2 * feed :])
-    gate_back = (act_grad * up * (sig + gate * sig * (1.0 - sig))).astype(BF16)
-    up_back = (act_grad * gate * sig).astype(BF16)
-    back_part = (
-        mm_nt(gate_back, mlp_w[:, :feed]) + mm_nt(up_back, mlp_w[:, feed : 2 * feed])
-    ).astype(BF16)
-    middle_back, middle_low, mlp_gain_sum = middle_back_sum(
-        line, back_part, upstream, middle, mlp_g
-    )
-    mlp_grads = lax.psum_scatter(
-        jnp.concatenate(
-            [
-                mm_tn(normed_two, gate_back).astype(BF16),
-                mm_tn(normed_two, up_back).astype(BF16),
-                mm_tn(upstream, activated).astype(BF16),
-            ],
-            axis=1,
-        ),
-        "fsdp",
-        scatter_dimension=0,
-        tiled=True,
-    ).astype(F32)
+    act, gate_back, up_back, middle_low, mlp_gain_sum = mlp_sum(
+        line, normed_two, upstream, middle, mlp_g, mlp_w
+    )
+    result, mlp_stats, mlp_grads = output_sum(
+        line, act, mlp_w, middle, normed_two, upstream, gate_back, up_back, valid
+    )
+    output = swap(result.reshape(seqs, local, width))
+    mlp_grads = lax.psum_scatter(mlp_grads, "fsdp", scatter_dimension=0, tiled=True).astype(F32)
+
     mixed_back = mm(middle_low, attn_w[:, 3 * band :]).astype(BF16)
     dq, dk, dv = attend_back(
         queries, keys, values, mixed_back, mixed, lse, cosine, sine, bias, image
     )
-    mlp_part = mm_nt(activated, mlp_w[:, 2 * feed :]).astype(BF16)
-    result, mlp_stats = output_sum(line, mlp_part, middle, valid)
-    output = swap(result.reshape(seqs, local, width))
-    front_part = mm_nt(jnp.concatenate([dq, dk, dv], axis=1), attn_w[:, : 3 * band]).astype(BF16)
-    source_grad, attn_gain_sum = input_sum(line, front_part, source, middle_back, attn_g)
-    input_grad = swap(source_grad.reshape(seqs, local, width))
-    attn_grads = lax.psum_scatter(
-        jnp.concatenate(
-            [
-                mm_tn(normed_one, dq).astype(BF16),
-                mm_tn(normed_one, dk).astype(BF16),
-                mm_tn(normed_one, dv).astype(BF16),
-                mm_tn(middle_low, mixed).astype(BF16),
-            ],
-            axis=1,
-        ),
-        "fsdp",
-        scatter_dimension=0,
-        tiled=True,
-    ).astype(F32)
+    attn_terms = jnp.concatenate(
+        [
+            mm_tn(normed_one, dq).astype(BF16),
+            mm_tn(normed_one, dk).astype(BF16),
+            mm_tn(normed_one, dv).astype(BF16),
+            mm_tn(middle_low, mixed).astype(BF16),
+        ],
+        axis=1,
+    )
     sums = jnp.stack([jnp.sum(stats[0]), jnp.sum(stats[1]), jnp.sum(mlp_stats[0])])
-    small = lax.psum(
-        jnp.concatenate([attn_gain_sum[0], mlp_gain_sum[0], sums]), "fsdp"
-    )
-    share = width // spread
-    attn_gain_part = lax.dynamic_slice_in_dim(small, mine * share, share)
-    mlp_gain_part = lax.dynamic_slice_in_dim(small, width + mine * share, share)
+    small_rows = jnp.concatenate(
+        [
+            jnp.zeros((1, width), F32),
+            mlp_gain_sum[0:1],
+            jnp.broadcast_to(sums[:, None], (3, width)),
+            jnp.zeros((3, width), F32),
+        ]
+    )
+    input_grad, small = input_sum(
+        line, spread, dq, dk, dv, attn_w, source, middle_low, attn_g, small_rows
+    )
+    attn_grads = lax.psum_scatter(attn_terms, "fsdp", scatter_dimension=0, tiled=True).astype(F32)
     count = jnp.sum(valid_mask).astype(F32) * width
-    roots = jnp.sqrt(small[2 * width :] / count)
+    roots = jnp.sqrt(small[2:5, 0] / count)
     return (
         output,
         input_grad,
@@ -1073,11 +1552,11 @@
         attn_grads[:, band : 2 * band],
         attn_grads[:, 2 * band : 3 * band],
         attn_grads[:, 3 * band :].T,
-        attn_gain_part,
+        small[0],
         mlp_grads[:, :feed],
         mlp_grads[:, feed : 2 * feed],
         mlp_grads[:, 2 * feed :].T,
-        mlp_gain_part,
+        small[1],
         roots[0],
         roots[1],
         roots[2],

time: 969 us -> 826 us (0.85)
  matrix products: 173 us -> 39 us
  blocking collectives: 120 us -> 10.4 us
  waiting for transfers between devices: 4.13 us -> 113 us
  Pallas kernels: 539 us -> 571 us
  other arithmetic: 46.3 us -> 28.1 us
  starting transfers between devices: 33.9 us -> 16.8 us
    all_to_all x4 -> x3, waiting for transfers between devices: 0.01 us -> 65.5 us  [swap(): lax.all_to_all(values, 'fsdp', split_axis=0, concat_axis=0, tiled=True)]
    psum x1 -> x0, blocking collectives: 57.9 us -> none  [per_device(): lax.psum(jnp.concatenate([attn_gain_sum[0], mlp_gain_sum[0], sums]), 'fsdp')]
    all_gather x1, blocking collectives: 62.2 us -> 10.4 us  [per_device(): lax.all_gather(jnp.stack([attn_gain, mlp_gain]), 'fsdp', axis=1, tiled=True)]
    dot_general x4 -> x0, matrix products: 50.2 us -> none  [mm_nt(): return lax.dot_general(a, b, NT, preferred_element_type=F32)]
    dot_general x5 -> x2, matrix products: 66.2 us -> 17.3 us  [mm(): return jnp.dot(a, b, preferred_element_type=F32)]
    reduce_scatter x2, waiting for transfers between devices: 0.01 us -> 41.2 us  [the longest x1 41.2 us: per_device(): lax.psum_scatter(mlp_grads, 'fsdp', scatter_dimension=0, tiled=True)]
    pallas_call x4, Pallas kernels: 476 us -> 515 us  [line_call(): pl.pallas_call(functools.partial(kernel, n), in_specs=specs, out_specs=ou...]
    dot_general x7 -> x4, matrix products: 56.1 us -> 21.7 us  [mm_tn(): return lax.dot_general(a, b, TN, preferred_element_type=F32)]
  transfers between devices with their start and end apart: 8 -> 7, of which waited for: 1 -> 3; matrix products, arithmetic and copies ran while one was open for 13% -> 5% of each run, Pallas kernels for 40% -> 49%
where the time goes in v2:
time: 826 us; the launch traced here: 821 us
  Pallas kernels  571 us (69%)
  waiting for transfers between devices  113 us (14%)
  matrix products  39 us (5%)
  other arithmetic  28.1 us (3%)
  local copies, waits for them, and re-layouts  27.4 us (3%)
  starting transfers between devices  16.8 us (2%)
  between operations  15 us (2%)
  blocking collectives  10.4 us (1%)
    pallas_call x4, Pallas kernels, line_call(): pl.pallas_call(functools.partial(kernel, n), in_specs=specs, out_specs=ou...  515 us
    all_to_all x3, waiting for transfers between devices, swap(): lax.all_to_all(values, 'fsdp', split_axis=0, concat_axis=0, tiled=True)  65.5 us
    reduce_scatter x1, waiting for transfers between devices, per_device(): lax.psum_scatter(mlp_grads, 'fsdp', scatter_dimension=0, tiled=True)  41.2 us
    pallas_call x1, Pallas kernels, attend_back(): pl.pallas_call(attend_back_kernel, grid_spec=pltpu.PrefetchScalarGridSpec...  31.7 us
    pallas_call x1, Pallas kernels, attend(): pl.pallas_call(attend_kernel, grid_spec=pltpu.PrefetchScalarGridSpec(num_...  24.8 us
    dot_general x4, matrix products, mm_tn(): return lax.dot_general(a, b, TN, preferred_element_type=F32)  21.7 us
    dot_general x2, matrix products, mm(): return jnp.dot(a, b, preferred_element_type=F32)  17.3 us
  transfers between devices with their start and end apart: 7, of which 3 were waited for; matrix products, arithmetic and copies ran while one was open for 5% of the time, Pallas kernels for 49%

profile of v2, /device:TPU:0, one launch (start us, length us, event | category | flops | bytes accessed | tf_op | source)
XLA Modules:
  0.0 821.2 jit_solution(15114113604046523171)
XLA Ops:
  8.5 2.2 pad_maximum_fusion.2
  11.5 2.9 pad_maximum_fusion.1
  14.4 10.4 %all_gather.9 = bf16[2,2048]{1,0:T(2,128)(2,1)S(1)} all-gather(bf16[2,256]{1,0:T(2,128)(2,1)S(1)} %pad_maximum_fusion.5), channel_id=1, replica_groups=mesh['fsdp'=8,'dp'=4] {'fsdp'}, dimensions={1}, use_global_device_ids=true | all-gather | bytes 9216 | tf_op jit(solution)/shard_map/all_gather | solution.py:1471
  24.8 4.7 all-to-all-start
  33.5 1.9 multiply_sine_fusion
  35.6 1.6 pad_maximum_fusion.3
  38.3 65.5 %all-to-all-done = bf16[8,128,2048]{2,1,0:T(8,128)(2,1)} async-done(((bf16[8,128,2048]{2,1,0:T(8,128)(2,1)}), bf16[8,128,2048]{2,1,0:T(8,128)(2,1)}, u32[]{:S(2)}, u32[]{:S(2)}) %all-to-all-start) | async-done | bytes 4194336 | tf_op jit(solution)/shard_map/all_to_all | solution.py:1469
  103.8 4.6 all-to-all-start.1
  108.6 3.1 fusion
  111.7 12.4 %fusion.3.q_in.k_in.v_in = f32[1024,1536]{1,0:T(8,128)} fusion(bf16[2048,2048]{1,0:T(8,128)(2,1)} %all-gather.3.cloned.1.call-done.out_weight.refs_3_, bf16[1024,2048]{1,0:T(8,128)(2,1)} %bitcast.source_hbm.refs_4_, f32[2048]{0:T(1024)S(1)} %bitcast.32, f32[1024]{0:T(1024)S(1)} %add_rsqrt_fusion), kind=kOutput, calls=%fused_computation.6 | convolution fusion | flops 6450839552 | bytes 16789504 | tf_op jit(solution)/shard_map/dot_general | solution.py:379
  124.1 24.8 %attend.1 = (bf16[1024,512]{1,0:T(8,128)(2,1)}, bf16[1024,512]{1,0:T(8,128)(2,1)}, bf16[1024,512]{1,0:T(8,128)(2,1)}, bf16[1024,512]{1,0:T(8,128)(2,1)}, f32[4,8,1024]{2,1,0:T(8,128)}) custom-call(s32[4]{0:T(128)} %broadcast_add_fusion.image_ref, f32[1024,1536]{1,0:T(8,128)} %fusion.3.q_in.k_in.v_in, f32[1024,1536]{1,0:T(8,128)} %fusion.3.q_in.k_in.v_in, ...), custom_call_target="tpu_custom_call" | custom-call | flops 12000000000 | bytes 12000000 | tf_op jit(solution)/shard_map/attend/pallas_call | solution.py:488
  148.9 113.0 %middle_sum.1 = (bf16[1024,2048]{1,0:T(8,128)(2,1)}, bf16[1024,2048]{1,0:T(8,128)(2,1)}, f32[8,2048]{1,0:T(8,128)}) custom-call(bf16[1024,512]{1,0:T(8,128)(2,1)} %get-tuple-element.42.mixed_ref, bf16[2048,2048]{1,0:T(8,128)(2,1)} %all-gather.3.cloned.1.call-done.out_weight.refs_3_, bf16[1024,2048]{1,0:T(8,128)(2,1)} %bitcast.source_hbm.refs_4_, ...), custom_call_target="tpu_custom_call" | custom-call | flops 49999998976 | bytes 300000000 | tf_op jit(solution)/shard_map/middle_sum/pallas_call | solution.py:779
  261.9 6.3 all-gather.5.cloned.1.call-done.weight_hbm
  268.2 134.5 %mlp_sum.1 = (bf16[1024,2048]{1,0:T(8,128)(2,1)}, bf16[1024,2048]{1,0:T(8,128)(2,1)}, bf16[1024,2048]{1,0:T(8,128)(2,1)}, bf16[1024,2048]{1,0:T(8,128)(2,1)}, f32[8,2048]{1,0:T(8,128)}) custom-call(bf16[1024,2048]{1,0:T(8,128)(2,1)} %get-tuple-element.43.normed_hbm, bf16[1024,2048]{1,0:T(8,128)(2,1)} %bitcast.5.upstream_hbm, ...), custom_call_target="tpu_custom_call" | custom-call | flops 60000002048 | bytes 300000000 | tf_op jit(solution)/shard_map/mlp_sum/pallas_call | solution.py:779
  402.7 6.3 convolution_convert_fusion
  409.0 4.9 fusion.7.g_ref
  413.9 31.7 %attend_back.1 = (bf16[1024,512]{1,0:T(8,128)(2,1)}, bf16[1024,512]{1,0:T(8,128)(2,1)}, bf16[1024,512]{1,0:T(8,128)(2,1)}) custom-call(s32[4]{0:T(128)} %broadcast_add_fusion.image_ref, bf16[1024,512]{1,0:T(8,128)(2,1)} %get-tuple-element.50.q_ref, bf16[1024,512]{1,0:T(8,128)(2,1)} %get-tuple-element.51.k_ref, bf16[1024,512]{1,0:T(8,128)(2,1)} %get-tuple-element.52.v_ref, ...), custom_call_target="tpu_custom_call" | custom-call | flops 30000001024 | bytes 12000000 | tf_op jit(solution)/shard_map/attend_back/pallas_call | solution.py:596
  445.7 5.3 convolution_convert_fusion.1
  451.0 5.0 convolution_convert_fusion.2
  456.0 5.1 convolution_convert_fusion.3
  461.1 4.1 pad_maximum_fusion
  465.2 116.1 %output_sum.1 = (bf16[1024,2048]{1,0:T(8,128)(2,1)}, f32[8,2048]{1,0:T(8,128)}, bf16[2048,6144]{1,0:T(8,128)(2,1)}) custom-call(bf16[1024,2048]{1,0:T(8,128)(2,1)} %get-tuple-element.46.act_hbm, bf16[2048,6144]{1,0:T(8,128)(2,1)} %all-gather.5.cloned.1.call-done.weight_hbm, bf16[1024,2048]{1,0:T(8,128)(2,1)} %get-tuple-element.45.middle_hbm, ...), custom_call_target="tpu_custom_call" | custom-call | flops 60000002048 | bytes 300000000 | tf_op jit(solution)/shard_map/output_sum/pallas_call | solution.py:779
  585.8 7.2 all-to-all-start.2
  594.5 2.0 pad_maximum_fusion.6
  597.2 151.4 %input_sum.1 = (bf16[8,128,2048]{2,1,0:T(8,128)(2,1)}, f32[8,256]{1,0:T(8,128)}) custom-call(bf16[1024,512]{1,0:T(8,128)(2,1)} %get-tuple-element.55.refs_0_, bf16[1024,512]{1,0:T(8,128)(2,1)} %get-tuple-element.56.refs_1_, bf16[1024,512]{1,0:T(8,128)(2,1)} %get-tuple-element.57.refs_2_, bf16[2048,2048]{1,0:T(8,128)(2,1)} %all-gather.3.cloned.1.call-done.out_weight.refs_3_, ...), custom_call_target="tpu_custom_call" | custom-call | flops 49999998976 | bytes 300000000 | tf_op jit(solution)/shard_map/input_sum/pallas_call | solution.py:779
  756.6 41.2 %reduce-scatter.5.cloned.1.call-done = bf16[256,6144]{1,0:T(8,128)(2,1)} async-done(((bf16[2048,6144]{1,0:T(8,128)(2,1)}), bf16[256,6144]{1,0:T(8,128)(2,1)}) %reduce-scatter.5.cloned.1.call-update) | async-done | bytes 3145744 | tf_op jit(solution)/shard_map/reduce_scatter | solution.py:1518
  797.8 2.6 convert_element_type.75
  800.4 1.5 slice_bitcast_fusion
  802.0 3.0 copy.53
  805.0 2.5 fusion.17
  807.5 4.9 copy.56
  812.5 2.0 copy.57
  (84 shorter events, 21.6 us)
Async XLA Ops:
  7.2 3.6 copy-start.4
  7.2 4.2 copy-start.5
  7.2 104.5 %all-gather.3.cloned.1.call-start = ((), (), s32[]{:S(2)}) async-start(), calls=%async_computation.5 | async-start | bytes 9437184 | tf_op jit(solution)/shard_map/all_gather | solution.py:1475
  10.7 257.5 %all-gather.5.cloned.1.call-start = ((), (), s32[]{:S(2)}) async-start(), calls=%async_computation.6 | async-start | bytes 28311552 | tf_op jit(solution)/shard_map/all_gather | solution.py:1481
  11.4 2.9 copy-start.13
  11.4 2.9 copy-start.14
  24.8 8.3 %copy-start.11 = (s32[8,2]{0,1:T(2,128)S(1)}, s32[8,2]{0,1:T(2,128)}, u32[]{:S(2)}) copy-start(s32[8,2]{0,1:T(2,128)} %param.16) | copy-start | bytes 196
  24.8 8.3 %copy-start.12 = (s32[8,2]{0,1:T(2,128)S(1)}, s32[8,2]{0,1:T(2,128)}, u32[]{:S(2)}) copy-start(s32[8,2]{0,1:T(2,128)} %param.17) | copy-start | bytes 196
  24.8 78.9 %all-to-all-start = ((bf16[8,128,2048]{2,1,0:T(8,128)(2,1)}), bf16[8,128,2048]{2,1,0:T(8,128)(2,1)}, u32[]{:S(2)}, u32[]{:S(2)}) async-start(bf16[8,128,2048]{2,1,0:T(8,128)(2,1)} %param.14), calls=%async_computation | async-start | bytes 8388608 | tf_op jit(solution)/shard_map/all_to_all | solution.py:1469
  38.3 73.5 %copy-start.7 = (f32[1,2048]{1,0:T(1,128)}, f32[1,2048]{1,0:T(1,128)S(1)}, u32[]{:S(2)}) copy-start(f32[1,2048]{1,0:T(1,128)S(1)} %get-tuple-element.118.refs_6_) | copy-start | bytes 24580
  103.8 158.2 %all-to-all-start.1 = ((bf16[8,128,2048]{2,1,0:T(8,128)(2,1)}), bf16[8,128,2048]{2,1,0:T(8,128)(2,1)}, u32[]{:S(2)}, u32[]{:S(2)}) async-start(bf16[8,128,2048]{2,1,0:T(8,128)(2,1)} %param.15), calls=%async_computation.1 | async-start | bytes 8388608 | tf_op jit(solution)/shard_map/all_to_all | solution.py:1469
  108.3 642.9 %reduce-scatter.3.cloned.1.call-start = ((), (), s32[]{:S(2)}) async-start(), calls=%async_computation.7 | async-start | bytes 9437184 | tf_op jit(solution)/shard_map/reduce_scatter | solution.py:1545
  111.7 12.4 %copy-start.9 = (f32[1024]{0:T(1024)}, f32[1024]{0:T(1024)S(1)}, u32[]{:S(2)}) copy-start(f32[1024]{0:T(1024)S(1)} %add_rsqrt_fusion) | copy-start | bytes 12292
  402.7 6.4 copy-start.15
  413.9 31.7 %copy-start.8 = (f32[1,2048]{1,0:T(1,128)S(1)}, f32[1,2048]{1,0:T(1,128)}, u32[]{:S(2)}) copy-start(f32[1,2048]{1,0:T(1,128)} %copy-done.7) | copy-start | bytes 24580
  413.9 31.7 %copy-start.10 = (f32[1024]{0:T(1024)S(1)}, f32[1024]{0:T(1024)}, u32[]{:S(2)}) copy-start(f32[1024]{0:T(1024)} %copy-done.9) | copy-start | bytes 12292
  445.7 5.3 copy-start.17
  451.0 5.0 copy-start.16
  456.0 5.1 copy-start.3
  465.2 332.6 %reduce-scatter.5.cloned.1.call-start = ((), (), s32[]{:S(2)}) async-start(), calls=%async_computation.8 | async-start | bytes 28311552 | tf_op jit(solution)/shard_map/reduce_scatter | solution.py:1518
  581.3 0.8 copy-start.6
  585.8 165.4 %all-to-all-start.2 = ((bf16[8,128,2048]{2,1,0:T(8,128)(2,1)}), bf16[8,128,2048]{2,1,0:T(8,128)(2,1)}, u32[]{:S(2)}, u32[]{:S(2)}) async-start(bf16[8,128,2048]{2,1,0:T(8,128)(2,1)} %bitcast.29), calls=%async_computation.2 | async-start | bytes 8388608 | tf_op jit(solution)/shard_map/all_to_all | solution.py:1469
  751.2 4.4 copy-start.1
  800.4 4.6 copy-start
  807.5 4.9 copy-start.2
Sparse Core Ops, SparseCore 0:
  10.8 93.9 all-gather.2
  107.3 160.8 all-gather.4
  465.3 73.6 reduce-scatter.2
  581.5 216.2 reduce-scatter.4

commit v3 on v2

--- a/solution.py
+++ b/solution.py
@@ -895,6 +895,10 @@
         + flow_scratch(length, width),
         50_000_000_000,
     )
+TURN = 128
+GRAD = 256
+
+
 def mlp_kernel(
     n,
     normed_hbm,
@@ -905,6 +909,7 @@
     act_hbm,
     gate_back_hbm,
     up_back_hbm,
+    grads_hbm,
     low_ref,
     gain_ref,
     weight,
@@ -917,6 +922,8 @@
     load_sems,
     weight_sems,
     stage_sems,
+    right_sems,
+    grad_sems,
     *flows,
 ):
     width, feed = weight.shape[0], weight.shape[1] // 3
@@ -1014,15 +1021,99 @@
     lax.fori_loop(0, blocks, first, 0)
     loads[2].wait()
     per = (length // STRIP) // chunks
+    stride = per // blocks
+    last = (units - blocks - 1) * stride
+
+    turned = weight.at[:, pl.ds(0, length)]
+    each = feed // GRAD
+    grads = 2 * each
+    turn_steps = 4
+    turns = length // TURN // turn_steps
+    begin = last + 1 + turn_steps
+    at_once = -(-grads // (length // STRIP + (n - 1) * HOP - begin))
+
+    def right(unit):
+        return weight.at[
+            pl.ds(0, length),
+            pl.ds(pl.multiple_of(length + lax.rem(unit, 2) * GRAD, GRAD), GRAD),
+        ]
+
+    def made(unit):
+        return weight.at[
+            :, pl.ds(pl.multiple_of(length + (2 + lax.rem(unit, 2)) * GRAD, GRAD), GRAD)
+        ]
+
+    def right_load(unit, kind):
+        cols = pl.ds(pl.multiple_of(lax.rem(unit, each) * GRAD, GRAD), GRAD)
+        return pltpu.make_async_copy(
+            backs[1 + kind].at[:, cols], right(unit), right_sems.at[lax.rem(unit, 2)]
+        )
+
+    def fetch(unit):
+        for kind in range(2):
+
+            @pl.when(lax.div(unit, each) == kind)
+            def _(kind=kind):
+                right_load(unit, kind).start()
+
+    def grad_store(unit):
+        cols = pl.ds(pl.multiple_of(unit * GRAD, GRAD), GRAD)
+        return pltpu.make_async_copy(
+            made(unit), grads_hbm.at[:, cols], grad_sems.at[lax.rem(unit, 2)]
+        )
+
+    def grad_work(unit):
+        right_load(unit, 0).wait()
+
+        @pl.when(unit >= 2)
+        def _():
+            grad_store(unit - 2).wait()
+
+        here, there = right(unit), made(unit)
+
+        def piece(p, carry):
+            rows = pl.ds(pl.multiple_of(p * SLAB, SLAB), SLAB)
+            there[rows, :] = mm(turned[rows, :], here[...]).astype(BF16)
+            return carry
+
+        lax.fori_loop(0, width // SLAB, piece, 0)
+        grad_store(unit).start()
+
+        @pl.when(unit + 2 < grads)
+        def _():
+            fetch(unit + 2)
 
     def work(s):
-        for k in range(max(1, blocks // per)):
-            stride = max(1, per // blocks)
-            unit = blocks + (s * max(1, blocks // per) + k if per <= blocks else lax.div(s, stride))
-
-            @pl.when((unit < units) & (lax.rem(s, stride) == 0))
-            def _(unit=unit):
-                unit_work(unit)
+        @pl.when((s <= last) & (lax.rem(s, stride) == 0))
+        def _():
+            unit_work(blocks + lax.div(s, stride))
+
+        @pl.when(s == last + 1)
+        def _():
+            for kind in range(3):
+                store(kind, units - 2).wait()
+                store(kind, units - 1).wait()
+            fetch(0)
+            fetch(1)
+
+        @pl.when((s > last) & (s < begin))
+        def _():
+            for k in range(turns):
+                at = pl.multiple_of(((s - last - 1) * turns + k) * TURN, TURN)
+                turned[:, pl.ds(at, TURN)] = normed[pl.ds(at, TURN), :].T
+
+        @pl.when(s >= begin)
+        def _():
+            def some(k, carry):
+                unit = (s - begin) * at_once + k
+
+                @pl.when(unit < grads)
+                def _():
+                    grad_work(unit)
+
+                return carry
+
+            lax.fori_loop(0, at_once, some, 0)
 
     def finish(strip, rows, total):
         middle = middle_in[rows, :].astype(F32)
@@ -1034,9 +1125,8 @@
         gain_ref[0:1, :] += col_sum(total * middle * scale)
 
     line_sum(n, own, flows, work, finish)
-    for kind in range(3):
-        store(kind, units - 2).wait()
-        store(kind, units - 1).wait()
+    grad_store(grads - 2).wait()
+    grad_store(grads - 1).wait()
 
 
 def mlp_sum(n, normed, upstream, middle, gain, weights):
@@ -1053,10 +1143,11 @@
         [ANY, ANY, ANY, VM, ANY],
         [low] * 3
         + [
+            jax.ShapeDtypeStruct((width, 2 * feed), BF16),
             jax.ShapeDtypeStruct((length, width), BF16),
             jax.ShapeDtypeStruct((8, width), F32),
         ],
-        [ANY] * 3 + [VM] * 2,
+        [ANY] * 4 + [VM] * 2,
         [
             pltpu.VMEM((width, 3 * feed), BF16),
             rows,
@@ -1068,40 +1159,125 @@
             pltpu.SemaphoreType.DMA((3,)),
             pltpu.SemaphoreType.DMA((3, feed // SLAB)),
             pltpu.SemaphoreType.DMA((2, 3)),
+            pltpu.SemaphoreType.DMA((2,)),
+            pltpu.SemaphoreType.DMA((2,)),
         ]
         + flow_scratch(length, width),
         60_000_000_000,
     )
-TURN = 128
-GRAD = 256
+def scatter(length, peers, result, out_hbm, sems):
+    send_sems, recv_sems, home_sems = sems
+    mine = lax.axis_index("fsdp")
+    strips, local = length // STRIP, length // peers
+    per = local // STRIP
+    shift = mine * per
+
+    def place(strip):
+        at = lax.rem(strip + shift, strips)
+        inside = pl.ds(pl.multiple_of(lax.rem(at, per) * STRIP, STRIP), STRIP)
+        rows = pl.ds(pl.multiple_of(at * STRIP, STRIP), STRIP)
+        return lax.div(at, per), rows, inside
+
+    def away(strip):
+        owner, rows, inside = place(strip)
+        return pltpu.make_async_remote_copy(
+            src_ref=result.at[rows],
+            dst_ref=out_hbm.at[mine, inside],
+            send_sem=send_sems.at[strip],
+            recv_sem=recv_sems.at[mine],
+            device_id={"fsdp": owner},
+            device_id_type=MESH,
+        )
+
+    def home(strip):
+        _, rows, inside = place(strip)
+        return pltpu.make_async_copy(
+            result.at[rows], out_hbm.at[mine, inside], home_sems.at[lax.rem(strip, per)]
+        )
+
+    def send(strip):
+        @pl.when(strip < per)
+        def _():
+            home(strip).start()
+
+        @pl.when(strip >= per)
+        def _():
+            away(strip).start()
+
+    def drain():
+        for strip in range(per):
+            home(strip).wait()
+
+        def sent(strip, carry):
+            away(strip).wait_send()
+            return carry
+
+        lax.fori_loop(per, strips, sent, 0)
+        for ahead in range(1, peers):
+            peer = lax.rem(mine + ahead, peers)
+            pltpu.make_async_remote_copy(
+                src_ref=result.at[pl.ds(0, local)],
+                dst_ref=out_hbm.at[peer],
+                send_sem=send_sems.at[0],
+                recv_sem=recv_sems.at[peer],
+                device_id={"fsdp": peer},
+                device_id_type=MESH,
+            ).wait_recv()
+
+    return send, drain, shift
+
+
+def scatter_scratch(length, peers):
+    return [
+        pltpu.SemaphoreType.DMA((length // STRIP,)),
+        pltpu.SemaphoreType.DMA((peers,)),
+        pltpu.SemaphoreType.DMA((length // peers // STRIP,)),
+    ]
+
+
+def on_shifted_groups(s, shift, strips, make):
+    full = TILE // STRIP
+    base = lax.rem(s + shift, strips)
+
+    @pl.when((s == 0) | ((lax.rem(base, full) == 0) & (s <= strips - full)))
+    def _():
+        make(lax.div(base, full))
 
 
 def output_kernel(
     n,
+    peers,
     act_hbm,
     weight_hbm,
     middle_hbm,
+    upstream_hbm,
     normed_hbm,
-    upstream_hbm,
-    gate_back_hbm,
-    up_back_hbm,
+    low_hbm,
+    dq_hbm,
+    dk_hbm,
+    dv_hbm,
+    mixed_hbm,
     valid,
-    out_ref,
+    out_hbm,
     stats_ref,
     grads_hbm,
+    result,
     act,
     down,
     middle,
+    upstream_t,
     normed_t,
-    upstream_t,
-    gate_back,
-    up_back,
+    low_t,
+    rights,
     own,
     slices,
     stage,
     load_sems,
     slice_sems,
     stage_sems,
+    send_sems,
+    recv_sems,
+    home_sems,
     *flows,
 ):
     length, width = own.shape
@@ -1110,16 +1286,22 @@
         pltpu.make_async_copy(act_hbm, act, load_sems.at[0]),
         pltpu.make_async_copy(weight_hbm.at[:, pl.ds(2 * feed, feed)], down, load_sems.at[1]),
         pltpu.make_async_copy(middle_hbm, middle, load_sems.at[2]),
-        pltpu.make_async_copy(gate_back_hbm, gate_back, load_sems.at[3]),
-        pltpu.make_async_copy(up_back_hbm, up_back, load_sems.at[4]),
     ]
+    band = dq_hbm.shape[1]
+    for k, ref in enumerate((dq_hbm, dk_hbm, dv_hbm, mixed_hbm)):
+        loads.append(
+            pltpu.make_async_copy(
+                ref, rights.at[:, k * band : (k + 1) * band], load_sems.at[3 + k]
+            )
+        )
+    turned = (upstream_t, normed_t, low_t)
     turns = length // TURN
 
     def slice_load(kind, turn):
         rows = pl.ds(pl.multiple_of(turn * TURN, TURN), TURN)
         slot = lax.rem(turn, 2)
         return pltpu.make_async_copy(
-            (normed_hbm, upstream_hbm)[kind].at[rows],
+            (upstream_hbm, normed_hbm, low_hbm)[kind].at[rows],
             slices.at[slot, kind],
             slice_sems.at[slot, kind],
         )
@@ -1127,11 +1309,11 @@
     loads[0].start()
     loads[1].start()
     for turn in range(2):
-        for kind in range(2):
+        for kind in range(3):
             slice_load(kind, turn).start()
     for load in loads[2:]:
         load.start()
-    greet(n)
+    greet(n, peers)
     stats_ref[...] = jnp.zeros_like(stats_ref)
     loads[0].wait()
     loads[1].wait()
@@ -1141,8 +1323,8 @@
             own, wide_rows(group), [(lambda rows: act[rows, :], lambda cols: down[cols, :])]
         )
 
-    blocks = feed // GRAD
-    units = 3 * blocks
+    edges = (0, feed // GRAD, (feed + 3 * band) // GRAD, (feed + 4 * band) // GRAD)
+    units = edges[3]
 
     def store(unit):
         cols = pl.ds(pl.multiple_of(unit * GRAD, GRAD), GRAD)
@@ -1156,13 +1338,15 @@
         def _():
             store(unit - 2).wait()
 
-        cols = pl.ds(pl.multiple_of(lax.rem(unit, blocks) * GRAD, GRAD), GRAD)
         for kind, (left, right) in enumerate(
-            ((normed_t, gate_back), (normed_t, up_back), (upstream_t, act))
+            ((upstream_t, act), (normed_t, rights), (low_t, rights))
         ):
-
-            @pl.when(lax.div(unit, blocks) == kind)
-            def _(left=left, right=right):
+            first = 0 if kind == 0 else edges[1]
+
+            @pl.when((unit >= edges[kind]) & (unit < edges[kind + 1]))
+            def _(left=left, right=right, first=first):
+                cols = pl.ds(pl.multiple_of((unit - first) * GRAD, GRAD), GRAD)
+
                 def piece(p, carry):
                     rows = pl.ds(pl.multiple_of(p * SLAB, SLAB), SLAB)
                     stage[slot, rows, :] = mm(left[rows, :], right[:, cols]).astype(BF16)
@@ -1172,16 +1356,20 @@
 
         store(unit).start()
 
+    send, drain, shift = scatter(
+        length, peers, result, out_hbm, (send_sems, recv_sems, home_sems)
+    )
+
     def work(s):
-        on_groups(s, length, make)
+        on_shifted_groups(s, shift, length // STRIP, make)
 
         @pl.when(s < turns)
         def _():
             slot = lax.rem(s, 2)
             cols = pl.ds(pl.multiple_of(s * TURN, TURN), TURN)
-            for kind, turned in enumerate((normed_t, upstream_t)):
+            for kind in range(3):
                 slice_load(kind, s).wait()
-                turned[:, cols] = slices[slot, kind].T
+                turned[kind][:, cols] = slices[slot, kind].T
 
                 @pl.when(s + 2 < turns)
                 def _(kind=kind):
@@ -1189,8 +1377,8 @@
 
         @pl.when(s == turns)
         def _():
-            loads[3].wait()
-            loads[4].wait()
+            for load in loads[3:]:
+                load.wait()
 
         @pl.when((s >= turns) & (s < turns + units))
         def _():
@@ -1201,48 +1389,54 @@
             loads[2].wait()
 
     def finish(strip, rows, total):
-        out_ref[rows, :] = (middle[rows, :].astype(F32) + total).astype(BF16)
+        result[rows, :] = (middle[rows, :].astype(F32) + total).astype(BF16)
+        send(strip)
         stats_ref[0:1, :] += col_sum(total * total * valid[rows, :])
 
-    line_sum(n, own, flows, work, finish)
+    line_sum(n, own, flows, work, finish, shift)
+    drain()
     store(units - 2).wait()
     store(units - 1).wait()
 
 
-def output_sum(n, act, weights, middle, normed, upstream, gate_back, up_back, valid):
+def output_sum(
+    n, peers, act, weights, middle, upstream, normed, low, dq, dk, dv, mixed, valid
+):
     length, width = middle.shape
     feed = act.shape[1]
     rows = pltpu.VMEM((length, width), BF16)
     wide = pltpu.VMEM((length, feed), BF16)
     turned = pltpu.VMEM((width, length), BF16)
     return line_call(
-        output_kernel,
+        lambda count, *refs: output_kernel(count, peers, *refs),
         n,
         "output_sum",
         3,
-        (act, weights, middle, normed, upstream, gate_back, up_back, valid),
-        [ANY] * 7 + [VM],
+        (act, weights, middle, upstream, normed, low, dq, dk, dv, mixed, valid),
+        [ANY] * 10 + [VM],
         [
-            jax.ShapeDtypeStruct((length, width), BF16),
+            jax.ShapeDtypeStruct((peers, length // peers, width), BF16),
             jax.ShapeDtypeStruct((8, width), F32),
-            jax.ShapeDtypeStruct((width, 3 * feed), BF16),
+            jax.ShapeDtypeStruct((width, feed + 4 * dq.shape[1]), BF16),
         ],
-        [VM, VM, ANY],
+        [ANY, VM, ANY],
         [
+            rows,
             wide,
             pltpu.VMEM((width, feed), BF16),
             rows,
             turned,
             turned,
-            wide,
-            wide,
+            turned,
+            pltpu.VMEM((length, 4 * dq.shape[1]), BF16),
             rows,
-            pltpu.VMEM((2, 2, TURN, width), BF16),
+            pltpu.VMEM((2, 3, TURN, width), BF16),
             pltpu.VMEM((2, width, GRAD), BF16),
-            pltpu.SemaphoreType.DMA((5,)),
-            pltpu.SemaphoreType.DMA((2, 2)),
+            pltpu.SemaphoreType.DMA((7,)),
+            pltpu.SemaphoreType.DMA((2, 3)),
             pltpu.SemaphoreType.DMA((2,)),
         ]
+        + scatter_scratch(length, peers)
         + flow_scratch(length, width),
         60_000_000_000,
     )
@@ -1269,20 +1463,19 @@
     small_own,
     small_got,
     load_sems,
+    small_send,
+    small_recv,
     send_sems,
     recv_sems,
-    home_sem,
-    small_send,
-    small_recv,
+    home_sems,
     *flows,
 ):
     length, width = own.shape
     band = dq_ref.shape[1]
     mine = lax.axis_index("fsdp")
-    local = length // peers
     share = width // peers
     strips = length // STRIP
-    per = local // STRIP
+    scatter_sems = (send_sems, recv_sems, home_sems)
     loads = [
         pltpu.make_async_copy(weight_hbm.at[:, pl.ds(0, 3 * band)], weight, load_sems.at[0]),
         pltpu.make_async_copy(source_hbm, source, load_sems.at[1]),
@@ -1298,47 +1491,18 @@
         (lambda rows, ref=ref: ref[rows, :], lambda cols, k=k: weight[cols, k * band : (k + 1) * band])
         for k, ref in enumerate((dq_ref, dk_ref, dv_ref))
     ]
-    shift = mine * per
+    send, drain, shift = scatter(length, peers, result, out_hbm, scatter_sems)
 
     def make(group):
         product_nt(own, wide_rows(group), halves)
 
     def work(s):
-        full = TILE // STRIP
-        base = lax.rem(s + shift, strips)
-
-        @pl.when((s == 0) | ((lax.rem(base, full) == 0) & (s <= strips - full)))
-        def _():
-            make(lax.div(base, full))
+        on_shifted_groups(s, shift, strips, make)
 
         @pl.when(s == 0)
         def _():
             loads[1].wait()
             loads[2].wait()
-
-    def place(strip):
-        at = lax.rem(strip + shift, strips)
-        owner = lax.div(at, per)
-        inside = pl.ds(pl.multiple_of(lax.rem(at, per) * STRIP, STRIP), STRIP)
-        rows = pl.ds(pl.multiple_of(at * STRIP, STRIP), STRIP)
-        return owner, rows, inside
-
-    def away(strip):
-        owner, rows, inside = place(strip)
-        return pltpu.make_async_remote_copy(
-            src_ref=result.at[rows],
-            dst_ref=out_hbm.at[mine, inside],
-            send_sem=send_sems.at[strip],
-            recv_sem=recv_sems.at[mine],
-            device_id={"fsdp": owner},
-            device_id_type=MESH,
-        )
-
-    def home(strip):
-        owner, rows, inside = place(strip)
-        return pltpu.make_async_copy(
-            result.at[rows], out_hbm.at[mine, inside], home_sem.at[lax.rem(strip, per)]
-        )
 
     def finish(strip, rows, total):
         here = source[rows, :].astype(F32)
@@ -1350,13 +1514,7 @@
         ).astype(BF16)
         small_own[0:1, :] += col_sum(total * here * scale)
 
-        @pl.when(strip < per)
-        def _():
-            home(strip).start()
-
-        @pl.when(strip >= per)
-        def _():
-            away(strip).start()
+        send(strip)
 
     line_sum(n, own, flows, work, finish, shift)
 
@@ -1374,14 +1532,6 @@
 
     for ahead in range(1, peers):
         small(ahead).start()
-    for strip in range(per):
-        home(strip).wait()
-
-    def drain(strip, carry):
-        away(strip).wait_send()
-        return carry
-
-    lax.fori_loop(per, strips, drain, 0)
     total = small_own[:, pl.ds(pl.multiple_of(mine * share, share), share)]
     for ahead in range(1, peers):
         peer = lax.rem(mine + ahead, peers)
@@ -1395,14 +1545,7 @@
         ).wait_recv()
         total = total + small_got[peer]
         small(ahead).wait_send()
-        pltpu.make_async_remote_copy(
-            src_ref=result.at[pl.ds(0, local)],
-            dst_ref=out_hbm.at[peer],
-            send_sem=send_sems.at[0],
-            recv_sem=recv_sems.at[peer],
-            device_id={"fsdp": peer},
-            device_id_type=MESH,
-        ).wait_recv()
+    drain()
     small_ref[...] = total
 
 
@@ -1432,12 +1575,10 @@
             pltpu.VMEM((8, width), F32),
             pltpu.VMEM((peers, 8, share), F32),
             pltpu.SemaphoreType.DMA((3,)),
-            pltpu.SemaphoreType.DMA((length // STRIP,)),
-            pltpu.SemaphoreType.DMA((peers,)),
-            pltpu.SemaphoreType.DMA((length // peers // STRIP,)),
             pltpu.SemaphoreType.DMA((peers,)),
             pltpu.SemaphoreType.DMA((peers,)),
         ]
+        + scatter_scratch(length, peers)
         + flow_scratch(length, width),
         50_000_000_000,
     )
@@ -1468,6 +1609,9 @@
     def swap(values):
         return lax.all_to_all(values, "fsdp", split_axis=0, concat_axis=0, tiled=True)
 
+    def shares(terms):
+        return lax.psum_scatter(terms, "fsdp", scatter_dimension=0, tiled=True)
+
     gains = lax.all_gather(jnp.stack([attn_gain, mlp_gain]), "fsdp", axis=1, tiled=True)
     gains, inputs = lax.optimization_barrier((gains, inputs))
     gains = gains.astype(F32)
@@ -1508,28 +1652,31 @@
     qkv = mm(normed_one, attn_w[:, : 3 * band])
     queries, keys, values, mixed, lse = attend(qkv, cosine, sine, bias, image)
     middle, normed_two, stats = middle_sum(line, mixed, attn_w, source, mlp_g, valid)
-    act, gate_back, up_back, middle_low, mlp_gain_sum = mlp_sum(
+    act, _, _, front_terms, middle_low, mlp_gain_sum = mlp_sum(
         line, normed_two, upstream, middle, mlp_g, mlp_w
     )
-    result, mlp_stats, mlp_grads = output_sum(
-        line, act, mlp_w, middle, normed_two, upstream, gate_back, up_back, valid
-    )
-    output = swap(result.reshape(seqs, local, width))
-    mlp_grads = lax.psum_scatter(mlp_grads, "fsdp", scatter_dimension=0, tiled=True).astype(F32)
-
+    front_grads = shares(front_terms)
     mixed_back = mm(middle_low, attn_w[:, 3 * band :]).astype(BF16)
     dq, dk, dv = attend_back(
         queries, keys, values, mixed_back, mixed, lse, cosine, sine, bias, image
     )
-    attn_terms = jnp.concatenate(
-        [
-            mm_tn(normed_one, dq).astype(BF16),
-            mm_tn(normed_one, dk).astype(BF16),
-            mm_tn(normed_one, dv).astype(BF16),
-            mm_tn(middle_low, mixed).astype(BF16),
-        ],
-        axis=1,
-    )
+    output, mlp_stats, late_terms = output_sum(
+        line,
+        spread,
+        act,
+        mlp_w,
+        middle,
+        upstream,
+        normed_one,
+        middle_low,
+        dq,
+        dk,
+        dv,
+        mixed,
+        valid,
+    )
+    late_terms, front_grads = lax.optimization_barrier((late_terms, front_grads))
+    late_grads = shares(late_terms)
     sums = jnp.stack([jnp.sum(stats[0]), jnp.sum(stats[1]), jnp.sum(mlp_stats[0])])
     small_rows = jnp.concatenate(
         [
@@ -1542,7 +1689,8 @@
     input_grad, small = input_sum(
         line, spread, dq, dk, dv, attn_w, source, middle_low, attn_g, small_rows
     )
-    attn_grads = lax.psum_scatter(attn_terms, "fsdp", scatter_dimension=0, tiled=True).astype(F32)
+    late_grads = late_grads.astype(F32)
+    attn_grads = late_grads[:, feed:]
     count = jnp.sum(valid_mask).astype(F32) * width
     roots = jnp.sqrt(small[2:5, 0] / count)
     return (
@@ -1553,9 +1701,9 @@
         attn_grads[:, 2 * band : 3 * band],
         attn_grads[:, 3 * band :].T,
         small[0],
-        mlp_grads[:, :feed],
-        mlp_grads[:, feed : 2 * feed],
-        mlp_grads[:, 2 * feed :].T,
+        front_grads[:, :feed].astype(F32),
+        front_grads[:, feed:].astype(F32),
+        late_grads[:, :feed].T,
         small[1],
         roots[0],
         roots[1],

time: 826 us -> 768 us (0.930)
  waiting for transfers between devices: 113 us -> 89.6 us
  matrix products: 39 us -> 19.2 us
    dot_general x4 -> x0, matrix products: 21.7 us -> none  [mm_tn(): return lax.dot_general(a, b, TN, preferred_element_type=F32)]
    reduce_scatter x2, waiting for transfers between devices: 41.2 us -> 23.5 us  [shares(): return lax.psum_scatter(terms, 'fsdp', scatter_dimension=0, tiled=True)]
    convert_element_type x2 -> x3, other arithmetic: 2.78 us -> 11.8 us  [the longest x1 5.61 us: per_device(): normed_one = (residual * scale_one * attn_g).astype(BF16)]
    all_to_all x3 -> x2, waiting for transfers between devices: 65.5 us -> 65.5 us  [swap(): lax.all_to_all(values, 'fsdp', split_axis=0, concat_axis=0, tiled=True)]
  transfers between devices with their start and end apart: 7 -> 6, of which waited for: 3 -> 3; matrix products, arithmetic and copies ran while one was open for 5% -> 7% of each run, Pallas kernels for 49% -> 55%
where the time goes in v3:
time: 768 us; the launch traced here: 764 us
  Pallas kernels  567 us (74%)
  waiting for transfers between devices  89.6 us (12%)
  other arithmetic  33 us (4%)
  local copies, waits for them, and re-layouts  20.4 us (3%)
  matrix products  19.2 us (2%)
  between operations  15 us (2%)
  blocking collectives  10.4 us (1%)
  starting transfers between devices  10.2 us (1%)
    pallas_call x4, Pallas kernels, line_call(): pl.pallas_call(functools.partial(kernel, n), in_specs=specs, out_specs=ou...  510 us
    all_to_all x2, waiting for transfers between devices, swap(): lax.all_to_all(values, 'fsdp', split_axis=0, concat_axis=0, tiled=True)  65.5 us
    pallas_call x1, Pallas kernels, attend_back(): pl.pallas_call(attend_back_kernel, grid_spec=pltpu.PrefetchScalarGridSpec...  31.7 us
    pallas_call x1, Pallas kernels, attend(): pl.pallas_call(attend_kernel, grid_spec=pltpu.PrefetchScalarGridSpec(num_...  24.8 us
    reduce_scatter x2, waiting for transfers between devices, shares(): return lax.psum_scatter(terms, 'fsdp', scatter_dimension=0, tiled=True)  23.5 us
    dot_general x2, matrix products, mm(): return jnp.dot(a, b, preferred_element_type=F32)  19.2 us
  transfers between devices with their start and end apart: 6, of which 3 were waited for; matrix products, arithmetic and copies ran while one was open for 7% of the time, Pallas kernels for 55%

profile of v3, /device:TPU:0, one launch (start us, length us, event | category | flops | bytes accessed | tf_op | source)
XLA Modules:
  0.0 764.3 jit_solution(8698665816632455816)
XLA Ops:
  7.2 1.2 copy.40
  8.5 2.2 pad_maximum_fusion.1
  11.5 2.9 pad_maximum_fusion
  14.4 10.4 %all_gather.9 = bf16[2,2048]{1,0:T(2,128)(2,1)S(1)} all-gather(bf16[2,256]{1,0:T(2,128)(2,1)S(1)} %pad_maximum_fusion.4), channel_id=1, replica_groups=mesh['fsdp'=8,'dp'=4] {'fsdp'}, dimensions={1}, use_global_device_ids=true | all-gather | bytes 9216 | tf_op jit(solution)/shard_map/all_gather | solution.py:1615
  24.8 4.7 all-to-all-start
  30.3 1.0 copy.41.bias_ref
  32.1 1.0 copy.42.valid.refs_10_
  33.5 1.9 multiply_sine_fusion
  35.6 1.6 pad_maximum_fusion.2
  38.3 65.5 %all-to-all-done = bf16[8,128,2048]{2,1,0:T(8,128)(2,1)} async-done(((bf16[8,128,2048]{2,1,0:T(8,128)(2,1)}), bf16[8,128,2048]{2,1,0:T(8,128)(2,1)}, u32[]{:S(2)}, u32[]{:S(2)}) %all-to-all-start) | async-done | bytes 4194336 | tf_op jit(solution)/shard_map/all_to_all | solution.py:1610
  103.8 4.6 all-to-all-start.1
  108.9 3.1 fusion
  112.0 5.6 fusion.2.refs_4_
  117.6 13.0 %fusion.3.q_in.k_in.v_in = f32[1024,1536]{1,0:T(8,128)} fusion(bf16[1024,2048]{1,0:T(8,128)(2,1)} %fusion.2.refs_4_, bf16[2048,2048]{1,0:T(8,128)(2,1)} %all-gather.3.cloned.1.call-done.out_weight.refs_3_), kind=kOutput, calls=%fused_computation.5 | convolution fusion | flops 6442450944 | bytes 16777216 | tf_op jit(solution)/shard_map/dot_general | solution.py:379
  130.6 24.8 %attend.1 = (bf16[1024,512]{1,0:T(8,128)(2,1)}, bf16[1024,512]{1,0:T(8,128)(2,1)}, bf16[1024,512]{1,0:T(8,128)(2,1)}, bf16[1024,512]{1,0:T(8,128)(2,1)}, f32[4,8,1024]{2,1,0:T(8,128)}) custom-call(s32[4]{0:T(128)} %broadcast_add_fusion.image_ref, f32[1024,1536]{1,0:T(8,128)} %fusion.3.q_in.k_in.v_in, f32[1024,1536]{1,0:T(8,128)} %fusion.3.q_in.k_in.v_in, ...), custom_call_target="tpu_custom_call" | custom-call | flops 12000000000 | bytes 12000000 | tf_op jit(solution)/shard_map/attend/pallas_call | solution.py:488
  155.4 112.2 %middle_sum.1 = (bf16[1024,2048]{1,0:T(8,128)(2,1)}, bf16[1024,2048]{1,0:T(8,128)(2,1)}, f32[8,2048]{1,0:T(8,128)}) custom-call(bf16[1024,512]{1,0:T(8,128)(2,1)} %get-tuple-element.43.mixed_ref.refs_9_, bf16[2048,2048]{1,0:T(8,128)(2,1)} %all-gather.3.cloned.1.call-done.out_weight.refs_3_, bf16[1024,2048]{1,0:T(8,128)(2,1)} %bitcast.source_hbm.refs_4_, ...), custom_call_target="tpu_custom_call" | custom-call | flops 49999998976 | bytes 300000000 | tf_op jit(solution)/shard_map/middle_sum/pallas_call | solution.py:779
  268.2 144.0 %mlp_sum.1 = (bf16[1024,2048]{1,0:T(8,128)(2,1)}, bf16[1024,2048]{1,0:T(8,128)(2,1)}, bf16[1024,2048]{1,0:T(8,128)(2,1)}, bf16[2048,4096]{1,0:T(8,128)(2,1)}, bf...) custom-call(bf16[1024,2048]{1,0:T(8,128)(2,1)} %get-tuple-element.44.normed_hbm, ...), custom_call_target="tpu_custom_call" | custom-call | flops 60000002048 | bytes 300000000 | tf_op jit(solution)/shard_map/mlp_sum/pallas_call | solution.py:779
  412.5 6.2 fusion.7.g_ref
  418.6 31.7 %attend_back.1 = (bf16[1024,512]{1,0:T(8,128)(2,1)}, bf16[1024,512]{1,0:T(8,128)(2,1)}, bf16[1024,512]{1,0:T(8,128)(2,1)}) custom-call(s32[4]{0:T(128)} %broadcast_add_fusion.image_ref, bf16[1024,512]{1,0:T(8,128)(2,1)} %get-tuple-element.49.q_ref, bf16[1024,512]{1,0:T(8,128)(2,1)} %get-tuple-element.50.k_ref, bf16[1024,512]{1,0:T(8,128)(2,1)} %get-tuple-element.51.v_ref, ...), custom_call_target="tpu_custom_call" | custom-call | flops 30000001024 | bytes 12000000 | tf_op jit(solution)/shard_map/attend_back/pallas_call | solution.py:596
  450.3 119.5 %output_sum.1 = (bf16[8,128,2048]{2,1,0:T(8,128)(2,1)}, f32[8,2048]{1,0:T(8,128)}, bf16[2048,4096]{1,0:T(8,128)(2,1)}) custom-call(bf16[1024,2048]{1,0:T(8,128)(2,1)} %get-tuple-element.47.refs_0_, bf16[2048,6144]{1,0:T(8,128)(2,1)} %all-gather.5.cloned.1.call-done.weight_hbm.refs_1_, bf16[1024,2048]{1,0:T(8,128)(2,1)} %get-tuple-element.46.middle_hbm.refs_2_, ...), custom_call_target="tpu_custom_call" | custom-call | flops 60000002048 | bytes 300000000 | tf_op jit(solution)/shard_map/output_sum/pallas_call | solution.py:779
  572.0 1.5 slice_reduce_fusion.2
  574.4 1.5 slice_reduce_fusion
  575.9 2.0 pad_maximum_fusion.5
  578.6 134.4 %input_sum.1 = (bf16[8,128,2048]{2,1,0:T(8,128)(2,1)}, f32[8,256]{1,0:T(8,128)}) custom-call(bf16[1024,512]{1,0:T(8,128)(2,1)} %get-tuple-element.53.refs_6_.refs_0_, bf16[1024,512]{1,0:T(8,128)(2,1)} %get-tuple-element.54.refs_7_.refs_1_, bf16[1024,512]{1,0:T(8,128)(2,1)} %get-tuple-element.55.refs_8_.refs_2_, ...), custom_call_target="tpu_custom_call" | custom-call | flops 49999998976 | bytes 300000000 | tf_op jit(solution)/shard_map/input_sum/pallas_call | solution.py:779
  714.2 1.3 fusion.14
  715.6 4.1 slice_convert_fusion
  719.7 23.5 %reduce-scatter.5.cloned.1.call-done = bf16[256,4096]{1,0:T(8,128)(2,1)} async-done(((bf16[2048,4096]{1,0:T(8,128)(2,1)}), bf16[256,4096]{1,0:T(8,128)(2,1)}) %reduce-scatter.5.cloned.1.call-update) | async-done | bytes 2097168 | tf_op jit(solution)/shard_map/reduce_scatter | solution.py:1613
  743.2 2.1 convert_element_type.61
  745.4 1.8 copy.47
  748.2 2.3 fusion.13
  750.5 4.9 copy.50
  755.5 2.0 copy.51
  (57 shorter events, 10.9 us)
Async XLA Ops:
  7.2 3.6 copy-start.1
  7.2 4.2 copy-start.2
  7.2 110.4 %all-gather.3.cloned.1.call-start = ((), (), s32[]{:S(2)}) async-start(), calls=%async_computation.4 | async-start | bytes 9437184 | tf_op jit(solution)/shard_map/all_gather | solution.py:1619
  10.7 257.5 %all-gather.5.cloned.1.call-start = ((), (), s32[]{:S(2)}) async-start(), calls=%async_computation.5 | async-start | bytes 28311552 | tf_op jit(solution)/shard_map/all_gather | solution.py:1625
  11.4 2.9 copy-start.7
  11.4 2.9 copy-start.8
  24.8 8.3 %copy-start.5 = (s32[8,2]{0,1:T(2,128)S(1)}, s32[8,2]{0,1:T(2,128)}, u32[]{:S(2)}) copy-start(s32[8,2]{0,1:T(2,128)} %param.16) | copy-start | bytes 196
  24.8 8.3 %copy-start.6 = (s32[8,2]{0,1:T(2,128)S(1)}, s32[8,2]{0,1:T(2,128)}, u32[]{:S(2)}) copy-start(s32[8,2]{0,1:T(2,128)} %param.17) | copy-start | bytes 196
  24.8 78.9 %all-to-all-start = ((bf16[8,128,2048]{2,1,0:T(8,128)(2,1)}), bf16[8,128,2048]{2,1,0:T(8,128)(2,1)}, u32[]{:S(2)}, u32[]{:S(2)}) async-start(bf16[8,128,2048]{2,1,0:T(8,128)(2,1)} %param.14), calls=%async_computation | async-start | bytes 8388608 | tf_op jit(solution)/shard_map/all_to_all | solution.py:1610
  38.3 73.7 %copy-start.4 = (f32[1,2048]{1,0:T(1,128)}, f32[1,2048]{1,0:T(1,128)S(1)}, u32[]{:S(2)}) copy-start(f32[1,2048]{1,0:T(1,128)S(1)} %get-tuple-element.120.refs_6_) | copy-start | bytes 24580
  103.8 163.8 %all-to-all-start.1 = ((bf16[8,128,2048]{2,1,0:T(8,128)(2,1)}), bf16[8,128,2048]{2,1,0:T(8,128)(2,1)}, u32[]{:S(2)}, u32[]{:S(2)}) async-start(bf16[8,128,2048]{2,1,0:T(8,128)(2,1)} %param.15), calls=%async_computation.1 | async-start | bytes 8388608 | tf_op jit(solution)/shard_map/all_to_all | solution.py:1610
  108.3 461.5 %reduce-scatter.3.cloned.1.call-start = ((), (), s32[]{:S(2)}) async-start(), calls=%async_computation.6 | async-start | bytes 18874368 | tf_op jit(solution)/shard_map/reduce_scatter | solution.py:1613
  412.2 331.0 %reduce-scatter.5.cloned.1.call-start = ((), (), s32[]{:S(2)}) async-start(), calls=%async_computation.7 | async-start | bytes 18874368 | tf_op jit(solution)/shard_map/reduce_scatter | solution.py:1613
  569.9 0.8 copy-start.3
  750.5 4.9 copy-start
Sparse Core Ops, SparseCore 0:
  10.8 93.9 all-gather.2
  107.3 160.8 all-gather.4
  412.3 149.9 reduce-scatter.2
  570.0 173.0 reduce-scatter.4

commit v4 on v3

--- a/solution.py
+++ b/solution.py
@@ -1251,12 +1251,13 @@
     weight_hbm,
     middle_hbm,
     upstream_hbm,
-    normed_hbm,
+    source_hbm,
     low_hbm,
     dq_hbm,
     dk_hbm,
     dv_hbm,
     mixed_hbm,
+    gain,
     valid,
     out_hbm,
     stats_ref,
@@ -1301,7 +1302,7 @@
         rows = pl.ds(pl.multiple_of(turn * TURN, TURN), TURN)
         slot = lax.rem(turn, 2)
         return pltpu.make_async_copy(
-            (upstream_hbm, normed_hbm, low_hbm)[kind].at[rows],
+            (upstream_hbm, source_hbm, low_hbm)[kind].at[rows],
             slices.at[slot, kind],
             slice_sems.at[slot, kind],
         )
@@ -1369,7 +1370,12 @@
             cols = pl.ds(pl.multiple_of(s * TURN, TURN), TURN)
             for kind in range(3):
                 slice_load(kind, s).wait()
-                turned[kind][:, cols] = slices[slot, kind].T
+                here = slices[slot, kind]
+                if kind == 1:
+                    here = here.astype(F32)
+                    scale = lax.rsqrt(row_mean(here * here) + EPS)
+                    here = (here * scale * gain[...]).astype(BF16)
+                turned[kind][:, cols] = here.T
 
                 @pl.when(s + 2 < turns)
                 def _(kind=kind):
@@ -1400,7 +1406,7 @@
 
 
 def output_sum(
-    n, peers, act, weights, middle, upstream, normed, low, dq, dk, dv, mixed, valid
+    n, peers, act, weights, middle, upstream, source, low, dq, dk, dv, mixed, gain, valid
 ):
     length, width = middle.shape
     feed = act.shape[1]
@@ -1412,8 +1418,8 @@
         n,
         "output_sum",
         3,
-        (act, weights, middle, upstream, normed, low, dq, dk, dv, mixed, valid),
-        [ANY] * 10 + [VM],
+        (act, weights, middle, upstream, source, low, dq, dk, dv, mixed, gain, valid),
+        [ANY] * 10 + [VM] * 2,
         [
             jax.ShapeDtypeStruct((peers, length // peers, width), BF16),
             jax.ShapeDtypeStruct((8, width), F32),
@@ -1582,6 +1588,22 @@
         + flow_scratch(length, width),
         50_000_000_000,
     )
+def settle_kernel(in_ref, out_ref):
+    out_ref[...] = in_ref[...]
+
+
+def settle(values):
+    block = pl.BlockSpec((1,) + values.shape[1:], lambda i: (i, 0, 0))
+    return pl.pallas_call(
+        settle_kernel,
+        grid=(values.shape[0],),
+        in_specs=[block],
+        out_specs=block,
+        out_shape=jax.ShapeDtypeStruct(values.shape, values.dtype),
+        name="settle",
+    )(values)
+
+
 def per_device(
     mesh_sizes,
     inputs,
@@ -1667,16 +1689,18 @@
         mlp_w,
         middle,
         upstream,
-        normed_one,
+        source,
         middle_low,
         dq,
         dk,
         dv,
         mixed,
+        attn_g,
         valid,
     )
     late_terms, front_grads = lax.optimization_barrier((late_terms, front_grads))
     late_grads = shares(late_terms)
+    output = settle(output)
     sums = jnp.stack([jnp.sum(stats[0]), jnp.sum(stats[1]), jnp.sum(mlp_stats[0])])
     small_rows = jnp.concatenate(
         [
@@ -1689,6 +1713,8 @@
     input_grad, small = input_sum(
         line, spread, dq, dk, dv, attn_w, source, middle_low, attn_g, small_rows
     )
+    input_grad = settle(input_grad)
+    late_grads, output, input_grad = lax.optimization_barrier((late_grads, output, input_grad))
     late_grads = late_grads.astype(F32)
     attn_grads = late_grads[:, feed:]
     count = jnp.sum(valid_mask).astype(F32) * width

time: 768 us -> 758 us (0.987)
  Pallas kernels: 567 us -> 582 us
  other arithmetic: 33 us -> 23.6 us
  waiting for transfers between devices: 89.6 us -> 80.7 us
    pallas_call x0 -> x2, Pallas kernels: none -> 13.5 us  [settle(): pl.pallas_call(settle_kernel, grid=(values.shape[0],), in_specs=[block],...]
    reduce_scatter x2, waiting for transfers between devices: 23.5 us -> 12.6 us  [shares(): return lax.psum_scatter(terms, 'fsdp', scatter_dimension=0, tiled=True)]
  transfers between devices with their start and end apart: 6 -> 6, of which waited for: 3 -> 3; matrix products, arithmetic and copies ran while one was open for 7% -> 6% of each run, Pallas kernels for 55% -> 58%
where the time goes in v4:
time: 758 us; the launch traced here: 753 us
  Pallas kernels  582 us (77%)
  waiting for transfers between devices  80.7 us (11%)
  other arithmetic  23.6 us (3%)
  matrix products  18.7 us (2%)
  between operations  15 us (2%)
  local copies, waits for them, and re-layouts  12.8 us (2%)
  blocking collectives  10.4 us (1%)
  starting transfers between devices  10.2 us (1%)
    pallas_call x4, Pallas kernels, line_call(): pl.pallas_call(functools.partial(kernel, n), in_specs=specs, out_specs=ou...  505 us
    all_to_all x2, waiting for transfers between devices, swap(): lax.all_to_all(values, 'fsdp', split_axis=0, concat_axis=0, tiled=True)  65.5 us
    pallas_call x1, Pallas kernels, attend_back(): pl.pallas_call(attend_back_kernel, grid_spec=pltpu.PrefetchScalarGridSpec...  35.3 us
    pallas_call x1, Pallas kernels, attend(): pl.pallas_call(attend_kernel, grid_spec=pltpu.PrefetchScalarGridSpec(num_...  28.2 us
    dot_general x2, matrix products, mm(): return jnp.dot(a, b, preferred_element_type=F32)  18.7 us
  transfers between devices with their start and end apart: 6, of which 3 were waited for; matrix products, arithmetic and copies ran while one was open for 6% of the time, Pallas kernels for 58%

profile of v4, /device:TPU:0, one launch (start us, length us, event | category | flops | bytes accessed | tf_op | source)
XLA Modules:
  0.0 753.2 jit_solution(2111698046527183455)
XLA Ops:
  7.2 1.2 copy.40
  8.5 2.2 pad_maximum_fusion.1
  11.5 2.9 pad_maximum_fusion
  14.4 10.4 %all_gather.9 = bf16[2,2048]{1,0:T(2,128)(2,1)S(1)} all-gather(bf16[2,256]{1,0:T(2,128)(2,1)S(1)} %pad_maximum_fusion.4), channel_id=1, replica_groups=mesh['fsdp'=8,'dp'=4] {'fsdp'}, dimensions={1}, use_global_device_ids=true | all-gather | bytes 9216 | tf_op jit(solution)/shard_map/all_gather | solution.py:1637
  24.8 4.7 all-to-all-start
  30.3 1.0 copy.41.bias_ref
  32.1 1.0 copy.42.valid.refs_11_
  33.5 1.9 multiply_sine_fusion
  35.6 1.6 pad_maximum_fusion.2
  38.3 65.5 %all-to-all-done = bf16[8,128,2048]{2,1,0:T(8,128)(2,1)} async-done(((bf16[8,128,2048]{2,1,0:T(8,128)(2,1)}), bf16[8,128,2048]{2,1,0:T(8,128)(2,1)}, u32[]{:S(2)}, u32[]{:S(2)}) %all-to-all-start) | async-done | bytes 4194336 | tf_op jit(solution)/shard_map/all_to_all | solution.py:1632
  103.8 4.6 all-to-all-start.1
  108.9 3.1 fusion
  112.0 12.6 %fusion.3.q_in.k_in.v_in = f32[1024,1536]{1,0:T(8,128)} fusion(bf16[2048,2048]{1,0:T(8,128)(2,1)} %all-gather.3.cloned.1.call-done.out_weight.refs_3_, bf16[1024,2048]{1,0:T(8,128)(2,1)} %bitcast.source_hbm.refs_4_, f32[2048]{0:T(1024)S(1)} %bitcast.25, f32[1024]{0:T(1024)S(1)} %add_rsqrt_fusion), kind=kOutput, calls=%fused_computation.5 | convolution fusion | flops 6450839552 | bytes 16789504 | tf_op jit(solution)/shard_map/dot_general | solution.py:379
  124.6 28.2 %attend.1 = (bf16[1024,512]{1,0:T(8,128)(2,1)}, bf16[1024,512]{1,0:T(8,128)(2,1)}, bf16[1024,512]{1,0:T(8,128)(2,1)}, bf16[1024,512]{1,0:T(8,128)(2,1)}, f32[4,8,1024]{2,1,0:T(8,128)}) custom-call(s32[4]{0:T(128)} %broadcast_add_fusion.image_ref, f32[1024,1536]{1,0:T(8,128)} %fusion.3.q_in.k_in.v_in, f32[1024,1536]{1,0:T(8,128)} %fusion.3.q_in.k_in.v_in, ...), custom_call_target="tpu_custom_call" | custom-call | flops 12000000000 | bytes 12000000 | tf_op jit(solution)/shard_map/attend/pallas_call | solution.py:488
  152.8 112.8 %middle_sum.1 = (bf16[1024,2048]{1,0:T(8,128)(2,1)}, bf16[1024,2048]{1,0:T(8,128)(2,1)}, f32[8,2048]{1,0:T(8,128)}) custom-call(bf16[1024,512]{1,0:T(8,128)(2,1)} %get-tuple-element.46.mixed_ref.refs_9_, bf16[2048,2048]{1,0:T(8,128)(2,1)} %all-gather.3.cloned.1.call-done.out_weight.refs_3_, bf16[1024,2048]{1,0:T(8,128)(2,1)} %bitcast.source_hbm.refs_4_, ...), custom_call_target="tpu_custom_call" | custom-call | flops 49999998976 | bytes 300000000 | tf_op jit(solution)/shard_map/middle_sum/pallas_call | solution.py:779
  265.7 2.5 all-gather.5.cloned.1.call-done.weight_hbm.refs_1_
  268.2 143.5 %mlp_sum.1 = (bf16[1024,2048]{1,0:T(8,128)(2,1)}, bf16[1024,2048]{1,0:T(8,128)(2,1)}, bf16[1024,2048]{1,0:T(8,128)(2,1)}, bf16[2048,4096]{1,0:T(8,128)(2,1)}, bf...) custom-call(bf16[1024,2048]{1,0:T(8,128)(2,1)} %get-tuple-element.47.normed_hbm, ...), custom_call_target="tpu_custom_call" | custom-call | flops 60000002048 | bytes 300000000 | tf_op jit(solution)/shard_map/mlp_sum/pallas_call | solution.py:779
  412.0 6.2 fusion.10.g_ref
  418.2 35.3 %attend_back.1 = (bf16[1024,512]{1,0:T(8,128)(2,1)}, bf16[1024,512]{1,0:T(8,128)(2,1)}, bf16[1024,512]{1,0:T(8,128)(2,1)}) custom-call(s32[4]{0:T(128)} %broadcast_add_fusion.image_ref, bf16[1024,512]{1,0:T(8,128)(2,1)} %get-tuple-element.52.q_ref, bf16[1024,512]{1,0:T(8,128)(2,1)} %get-tuple-element.53.k_ref, bf16[1024,512]{1,0:T(8,128)(2,1)} %get-tuple-element.54.v_ref, ...), custom_call_target="tpu_custom_call" | custom-call | flops 30000001024 | bytes 12000000 | tf_op jit(solution)/shard_map/attend_back/pallas_call | solution.py:596
  453.4 118.1 %output_sum.1 = (bf16[8,128,2048]{2,1,0:T(8,128)(2,1)}, f32[8,2048]{1,0:T(8,128)}, bf16[2048,4096]{1,0:T(8,128)(2,1)}) custom-call(bf16[1024,2048]{1,0:T(8,128)(2,1)} %get-tuple-element.50.refs_0_, bf16[2048,6144]{1,0:T(8,128)(2,1)} %all-gather.5.cloned.1.call-done.weight_hbm.refs_1_, bf16[1024,2048]{1,0:T(8,128)(2,1)} %get-tuple-element.49.middle_hbm.refs_2_, ...), custom_call_target="tpu_custom_call" | custom-call | flops 60000002048 | bytes 300000000 | tf_op jit(solution)/shard_map/output_sum/pallas_call | solution.py:779
  573.7 1.5 slice_reduce_fusion.2
  575.3 0.8 slice.75
  576.1 1.5 slice_reduce_fusion
  577.6 2.0 pad_maximum_fusion.5
  580.3 130.4 %input_sum.1 = (bf16[8,128,2048]{2,1,0:T(8,128)(2,1)}, f32[8,256]{1,0:T(8,128)}) custom-call(bf16[1024,512]{1,0:T(8,128)(2,1)} %get-tuple-element.56.refs_6_.refs_0_, bf16[1024,512]{1,0:T(8,128)(2,1)} %get-tuple-element.57.refs_7_.refs_1_, bf16[1024,512]{1,0:T(8,128)(2,1)} %get-tuple-element.58.refs_8_.refs_2_, ...), custom_call_target="tpu_custom_call" | custom-call | flops 49999998976 | bytes 300000000 | tf_op jit(solution)/shard_map/input_sum/pallas_call | solution.py:779
  710.7 6.7 settle.3
  717.4 6.8 settle.2
  725.4 2.5 slice_convert_fusion
  727.9 12.6 %reduce-scatter.5.cloned.1.call-done = bf16[256,4096]{1,0:T(8,128)(2,1)} async-done(((bf16[2048,4096]{1,0:T(8,128)(2,1)}), bf16[256,4096]{1,0:T(8,128)(2,1)}) %reduce-scatter.5.cloned.1.call-update) | async-done | bytes 2097168 | tf_op jit(solution)/shard_map/reduce_scatter | solution.py:1635
  740.5 2.5 fusion.16
  743.6 1.8 copy.47
  745.5 1.0 copy.46
  (60 shorter events, 8.8 us)
Async XLA Ops:
  7.2 3.6 copy-start.2
  7.2 4.2 copy-start.3
  7.2 104.8 %all-gather.3.cloned.1.call-start = ((), (), s32[]{:S(2)}) async-start(), calls=%async_computation.4 | async-start | bytes 9437184 | tf_op jit(solution)/shard_map/all_gather | solution.py:1641
  10.7 257.5 %all-gather.5.cloned.1.call-start = ((), (), s32[]{:S(2)}) async-start(), calls=%async_computation.5 | async-start | bytes 28311552 | tf_op jit(solution)/shard_map/all_gather | solution.py:1647
  11.4 2.9 copy-start.9
  11.4 2.9 copy-start.10
  24.8 8.3 %copy-start.7 = (s32[8,2]{0,1:T(2,128)S(1)}, s32[8,2]{0,1:T(2,128)}, u32[]{:S(2)}) copy-start(s32[8,2]{0,1:T(2,128)} %param.16) | copy-start | bytes 196
  24.8 8.3 %copy-start.8 = (s32[8,2]{0,1:T(2,128)S(1)}, s32[8,2]{0,1:T(2,128)}, u32[]{:S(2)}) copy-start(s32[8,2]{0,1:T(2,128)} %param.17) | copy-start | bytes 196
  24.8 78.9 %all-to-all-start = ((bf16[8,128,2048]{2,1,0:T(8,128)(2,1)}), bf16[8,128,2048]{2,1,0:T(8,128)(2,1)}, u32[]{:S(2)}, u32[]{:S(2)}) async-start(bf16[8,128,2048]{2,1,0:T(8,128)(2,1)} %param.14), calls=%async_computation | async-start | bytes 8388608 | tf_op jit(solution)/shard_map/all_to_all | solution.py:1632
  38.3 73.8 %copy-start.5 = (f32[1,2048]{1,0:T(1,128)}, f32[1,2048]{1,0:T(1,128)S(1)}, u32[]{:S(2)}) copy-start(f32[1,2048]{1,0:T(1,128)S(1)} %get-tuple-element.126.refs_10_.refs_6_) | copy-start | bytes 24580
  103.8 161.9 %all-to-all-start.1 = ((bf16[8,128,2048]{2,1,0:T(8,128)(2,1)}), bf16[8,128,2048]{2,1,0:T(8,128)(2,1)}, u32[]{:S(2)}, u32[]{:S(2)}) async-start(bf16[8,128,2048]{2,1,0:T(8,128)(2,1)} %param.15), calls=%async_computation.1 | async-start | bytes 8388608 | tf_op jit(solution)/shard_map/all_to_all | solution.py:1632
  108.3 463.2 %reduce-scatter.3.cloned.1.call-start = ((), (), s32[]{:S(2)}) async-start(), calls=%async_computation.6 | async-start | bytes 18874368 | tf_op jit(solution)/shard_map/reduce_scatter | solution.py:1635
  411.8 328.7 %reduce-scatter.5.cloned.1.call-start = ((), (), s32[]{:S(2)}) async-start(), calls=%async_computation.7 | async-start | bytes 18874368 | tf_op jit(solution)/shard_map/reduce_scatter | solution.py:1635
  571.6 0.8 copy-start.4
  717.4 6.8 copy-start.6
  717.4 7.9 %copy-start.1 = (bf16[256,4096]{1,0:T(8,128)(2,1)S(1)}, bf16[256,4096]{1,0:T(8,128)(2,1)}, u32[]{:S(2)}) copy-start(bf16[256,4096]{1,0:T(8,128)(2,1)} %reduce-scatter.3.cloned.1.call-done) | copy-start | bytes 6291460
  740.5 2.5 copy-start
Sparse Core Ops, SparseCore 0:
  10.8 93.9 all-gather.2
  107.3 160.8 all-gather.4
  411.9 148.2 reduce-scatter.2
  571.7 168.6 reduce-scatter.4
